TPU v7x, 256 devices: a whole 4x4x8 slice. The times are simulated.
256 devices in a mesh: seg: 16 (over z, core), sec: 16 (over y, x).
Axes of the slice: x: 4, y: 4, z: 8, core: 2. Of those that a mesh axis runs over, the one named last changes fastest.
Arguments:
- psi: float32 [16, 32, 256, 256], P('seg', 'sec'), may hold values from -6 to 6
- left_env: bfloat16 [16, 6, 32, 256, 256], P('seg', None, 'sec'), may hold values from -1 to 2, as said below
- right_env: bfloat16 [16, 6, 32, 256, 256], P('seg', None, 'sec'), may hold values from -1 to 2, as said below
- hop_outer: bfloat16 [16, 2, 32, 256, 256], P('seg', None, 'sec'), may hold values from -0.75 to 0.75
- hop_inner: bfloat16 [16, 2, 32, 256, 256], P('seg', None, 'sec'), may hold values from -0.75 to 0.75
- dims: int32 [16, 32], P('seg'), may hold values from 1 to 256, 6144 in all within a row
Outputs:
- solution: float32 [16, 32, 256, 256], P('seg', 'sec')
- energy: float32 [16], P('seg')
- env_next: bfloat16 [16, 6, 32, 256, 256], P('seg', None, 'sec')
Inputs may be any that keep to these rules, and one draw needn't show every extreme that they name: `left_env`: each block is mostly its diagonal, positive, with small off-diagonal entries. `right_env`: drawn in the same way as left_env. In each segment the dims sum to 6144, and one sector has 256.
All inputs are finite; a program needn't handle non-finite values.
Results may differ from a plain program's by a relative error of at most 0.0085.
Values may be sent and summed in bfloat16 or wider, within the bound.
No kernel may reach another device: no remote copies, remote signals or barrier semaphores. Data moves between devices by JAX's collectives and lax.ppermute only.
A program may use at most 64 MiB of HBM per device.

v0:
```python
import jax
import jax.numpy as jnp
from jax import lax
from jax.sharding import PartitionSpec as P

ITERS = 4


TAU = 0.05


def with_halo(shard, sides, width):
    for axis, dim in sides:
        size, length = (lax.axis_size(axis), shard.shape[dim])
        up = [(i, (i + 1) % size) for i in range(size - 1)]
        down = [(j, i) for i, j in up]
        last = lax.slice_in_dim(shard, length - width, length, axis=dim)
        first = lax.slice_in_dim(shard, 0, width, axis=dim)
        before = lax.ppermute(last, axis, up)
        after = lax.ppermute(first, axis, down)
        shard = jnp.concatenate([before, shard, after], axis=dim)
    return shard


def passed_along(shard, axis, by):
    length = lax.axis_size(axis)
    pairs = [(i, i + by) for i in range(length) if 0 <= i + by < length]
    return lax.ppermute(shard, axis, pairs)


def apply_operator(iterate, env_left, env_right, hop_out, hop_in, block_mask):
    rounded = iterate.astype(jnp.bfloat16)
    padded = with_halo(rounded, (("sec", 0),), 1)
    halfway = jnp.einsum(
        "sij,wskj->wsik", rounded, env_right, preferred_element_type=jnp.float32
    ).astype(jnp.bfloat16)
    image = jnp.einsum("wsik,wskj->sij", env_left, halfway, preferred_element_type=jnp.float32)
    lower = jnp.einsum(
        "sij,skj->sik", padded[:-2], hop_in[0], preferred_element_type=jnp.float32
    ).astype(jnp.bfloat16)
    upper = jnp.einsum(
        "sij,skj->sik", padded[2:], hop_in[1], preferred_element_type=jnp.float32
    ).astype(jnp.bfloat16)
    image = image + jnp.einsum(
        "sik,skj->sij", hop_out[0], lower, preferred_element_type=jnp.float32
    )
    image = image + jnp.einsum(
        "sik,skj->sij", hop_out[1], upper, preferred_element_type=jnp.float32
    )
    return image * block_mask


def relax(iterate, env_left, env_right, hop_out, hop_in, block_mask, live_count):
    energy = jnp.float32(0.0)
    for sweep_iter in range(ITERS):
        image = apply_operator(iterate, env_left, env_right, hop_out, hop_in, block_mask)
        self_dot, cross_dot = lax.psum(
            (jnp.sum(iterate * iterate), jnp.sum(iterate * image)), "sec"
        )
        energy = cross_dot / self_dot
        step = iterate - TAU * (image - energy * iterate)
        step_norm = lax.psum(jnp.sum(step * step), "sec")
        iterate = step * jnp.sqrt(live_count / step_norm)
    return (iterate, energy)


def body(psi, left_env, right_env, hop_outer, hop_inner, dims):
    sectors_here = psi.shape[1]
    capacity = psi.shape[2]
    first_sector = lax.axis_index("sec") * sectors_here
    own_dims = lax.dynamic_slice_in_dim(dims[0], first_sector, sectors_here)
    sizes_f = dims[0].astype(jnp.float32)
    live_count = jnp.sum(sizes_f * sizes_f)
    indices = jnp.arange(capacity, dtype=jnp.int32)
    active = (indices[None, :] < own_dims[:, None]).astype(jnp.float32)
    block_mask = active[:, :, None] * active[:, None, :]
    env_left = left_env[0]
    env_right = right_env[0]
    hop_out = hop_outer[0]
    hop_in = hop_inner[0]
    iterate, energy = relax(
        psi[0] * block_mask, env_left, env_right, hop_out, hop_in, block_mask, live_count
    )
    factor = iterate.astype(jnp.bfloat16)
    grown = jnp.einsum(
        "wsik,skj->wsij", env_left, factor, preferred_element_type=jnp.float32
    ).astype(jnp.bfloat16)
    renewed = jnp.einsum("ski,wskj->wsij", factor, grown, preferred_element_type=jnp.float32)
    renewed = (renewed / own_dims.astype(jnp.float32)[None, :, None, None]).astype(jnp.bfloat16)
    passed = passed_along(renewed, "seg", 1)
    boundary = jnp.where(lax.axis_index("seg") == 0, env_left, passed)
    iterate, energy = relax(iterate, boundary, env_right, hop_out, hop_in, block_mask, live_count)
    return (iterate[None], jnp.reshape(energy, (1,)), renewed[None])


def solution(mesh):
    return jax.shard_map(
        body,
        mesh=mesh,
        in_specs=(
            P("seg", "sec", None, None),
            P("seg", None, "sec", None, None),
            P("seg", None, "sec", None, None),
            P("seg", None, "sec", None, None),
            P("seg", None, "sec", None, None),
            P("seg", None),
        ),
        out_specs=(P("seg", "sec", None, None), P("seg"), P("seg", None, "sec", None, None)),
        check_vma=False,
    )
```

profile of v0, /device:TPU:128, one launch (start us, length us, event | category | flops | bytes accessed | tf_op | source)
XLA Modules:
  0.0 799.5 jit_solution(6214907563608245950)
XLA Ops:
  3.7 4.0 collective-permute-start
  23.4 41.8 %all-reduce.7 = (f32[]{:T(128)}, f32[]{:T(128)}) all-reduce(f32[]{:T(128)} %get-tuple-element.7, f32[]{:T(128)} %get-tuple-element.6), channel_id=1, replica_groups=mesh['seg'=16,'sec'=16] {'sec'}, use_global_device_ids=true, to_apply=%region_1.0 | all-reduce | flops 2 | bytes 16 | tf_op jit(solution)/shard_map/psum | solution.py:57
  68.5 36.1 %psum.170 = f32[]{:T(128)} all-reduce(f32[]{:T(128)} %get-tuple-element.52), channel_id=1, replica_groups=mesh['seg'=16,'sec'=16] {'sec'}, use_global_device_ids=true, to_apply=%region_6.0 | all-reduce | flops 1 | bytes 8 | tf_op jit(solution)/shard_map/psum | solution.py:62
  106.8 4.6 collective-permute-start.2
  124.5 36.1 %all-reduce.6 = (f32[]{:T(128)}, f32[]{:T(128)}) all-reduce(f32[]{:T(128)} %get-tuple-element.21, f32[]{:T(128)} %get-tuple-element.20), channel_id=1, replica_groups=mesh['seg'=16,'sec'=16] {'sec'}, use_global_device_ids=true, to_apply=%region_8.0 | all-reduce | flops 2 | bytes 16 | tf_op jit(solution)/shard_map/psum | solution.py:57
  163.8 38.1 %psum.173 = f32[]{:T(128)} all-reduce(f32[]{:T(128)} %get-tuple-element.50), channel_id=1, replica_groups=mesh['seg'=16,'sec'=16] {'sec'}, use_global_device_ids=true, to_apply=%region_12.0 | all-reduce | flops 1 | bytes 8 | tf_op jit(solution)/shard_map/psum | solution.py:62
  213.4 3.5 collective-permute-done.5
  219.8 36.1 %all-reduce.5 = (f32[]{:T(128)}, f32[]{:T(128)}) all-reduce(f32[]{:T(128)} %get-tuple-element.19, f32[]{:T(128)} %get-tuple-element.18), channel_id=1, replica_groups=mesh['seg'=16,'sec'=16] {'sec'}, use_global_device_ids=true, to_apply=%region_14.0 | all-reduce | flops 2 | bytes 16 | tf_op jit(solution)/shard_map/psum | solution.py:57
  259.1 38.1 %psum.176 = f32[]{:T(128)} all-reduce(f32[]{:T(128)} %get-tuple-element.48), channel_id=1, replica_groups=mesh['seg'=16,'sec'=16] {'sec'}, use_global_device_ids=true, to_apply=%region_18.0 | all-reduce | flops 1 | bytes 8 | tf_op jit(solution)/shard_map/psum | solution.py:62
  315.0 36.1 %all-reduce.4 = (f32[]{:T(128)}, f32[]{:T(128)}) all-reduce(f32[]{:T(128)} %get-tuple-element.17, f32[]{:T(128)} %get-tuple-element.16), channel_id=1, replica_groups=mesh['seg'=16,'sec'=16] {'sec'}, use_global_device_ids=true, to_apply=%region_20.0 | all-reduce | flops 2 | bytes 16 | tf_op jit(solution)/shard_map/psum | solution.py:57
  354.9 38.1 %psum.179 = f32[]{:T(128)} all-reduce(f32[]{:T(128)} %get-tuple-element.46), channel_id=1, replica_groups=mesh['seg'=16,'sec'=16] {'sec'}, use_global_device_ids=true, to_apply=%region_24.0 | all-reduce | flops 1 | bytes 8 | tf_op jit(solution)/shard_map/psum | solution.py:62
  395.5 3.5 divide_convert_fusion
  412.3 10.0 %collective-permute-done.8 = bf16[6,2,256,256]{2,3,0,1:T(8,128)(2,1)} collective-permute-done((bf16[6,2,256,256]{2,3,0,1:T(8,128)(2,1)}, bf16[6,2,256,256]{2,3,0,1:T(8,128)(2,1)}, u32[]{:S(2)}, u32[]{:S(2)}) %collective-permute-start.8) | collective-permute-done | bytes 1572896 | tf_op jit(solution)/shard_map/ppermute | solution.py:28
  425.5 4.3 multiply_reduce_fusion.10
  429.8 36.2 %all-reduce.3 = (f32[]{:T(128)}, f32[]{:T(128)}) all-reduce(f32[]{:T(128)} %get-tuple-element.15, f32[]{:T(128)} %get-tuple-element.14), channel_id=1, replica_groups=mesh['seg'=16,'sec'=16] {'sec'}, use_global_device_ids=true, to_apply=%region_26.27 | all-reduce | flops 2 | bytes 16 | tf_op jit(solution)/shard_map/psum | solution.py:57
  469.8 38.0 %psum.182 = f32[]{:T(128)} all-reduce(f32[]{:T(128)} %get-tuple-element.42), channel_id=1, replica_groups=mesh['seg'=16,'sec'=16] {'sec'}, use_global_device_ids=true, to_apply=%region_30.31 | all-reduce | flops 1 | bytes 8 | tf_op jit(solution)/shard_map/psum | solution.py:62
  522.2 4.3 multiply_reduce_fusion.7
  526.5 36.1 %all-reduce.2 = (f32[]{:T(128)}, f32[]{:T(128)}) all-reduce(f32[]{:T(128)} %get-tuple-element.13, f32[]{:T(128)} %get-tuple-element.12), channel_id=1, replica_groups=mesh['seg'=16,'sec'=16] {'sec'}, use_global_device_ids=true, to_apply=%region_32.33 | all-reduce | flops 2 | bytes 16 | tf_op jit(solution)/shard_map/psum | solution.py:57
  566.5 38.1 %psum.185 = f32[]{:T(128)} all-reduce(f32[]{:T(128)} %get-tuple-element.40), channel_id=1, replica_groups=mesh['seg'=16,'sec'=16] {'sec'}, use_global_device_ids=true, to_apply=%region_36.37 | all-reduce | flops 1 | bytes 8 | tf_op jit(solution)/shard_map/psum | solution.py:62
  618.8 4.3 multiply_reduce_fusion.4
  623.1 36.1 %all-reduce.1 = (f32[]{:T(128)}, f32[]{:T(128)}) all-reduce(f32[]{:T(128)} %get-tuple-element.11, f32[]{:T(128)} %get-tuple-element.10), channel_id=1, replica_groups=mesh['seg'=16,'sec'=16] {'sec'}, use_global_device_ids=true, to_apply=%region_38.39 | all-reduce | flops 2 | bytes 16 | tf_op jit(solution)/shard_map/psum | solution.py:57
  662.4 38.1 %psum.188 = f32[]{:T(128)} all-reduce(f32[]{:T(128)} %get-tuple-element.38), channel_id=1, replica_groups=mesh['seg'=16,'sec'=16] {'sec'}, use_global_device_ids=true, to_apply=%region_42.43 | all-reduce | flops 1 | bytes 8 | tf_op jit(solution)/shard_map/psum | solution.py:62
  717.0 36.1 %all-reduce = (f32[]{:T(128)}, f32[]{:T(128)}) all-reduce(f32[]{:T(128)} %get-tuple-element.9, f32[]{:T(128)} %get-tuple-element.8), channel_id=1, replica_groups=mesh['seg'=16,'sec'=16] {'sec'}, use_global_device_ids=true, to_apply=%region_44.45 | all-reduce | flops 2 | bytes 16 | tf_op jit(solution)/shard_map/psum | solution.py:57
  757.8 38.1 %psum.191 = f32[]{:T(128)} all-reduce(f32[]{:T(128)} %multiply_reduce_fusion), channel_id=1, replica_groups=mesh['seg'=16,'sec'=16] {'sec'}, use_global_device_ids=true, to_apply=%region_48.49 | all-reduce | flops 1 | bytes 8 | tf_op jit(solution)/shard_map/psum | solution.py:62
  (105 shorter events, 140.2 us)
Async XLA Ops:
  0.6 11.0 %copy-start = (bf16[1,6,2,256,256]{4,3,2,1,0:T(8,128)(2,1)S(1)}, bf16[1,6,2,256,256]{4,3,2,1,0:T(8,128)(2,1)}, u32[]{:S(2)}) copy-start(bf16[1,6,2,256,256]{4,3,2,1,0:T(8,128)(2,1)} %param.8) | copy-start | bytes 4718596
  2.8 17.6 %copy-start.5 = (f32[1,2,256,256]{2,3,1,0:T(8,128)}, f32[1,2,256,256]{2,3,1,0:T(8,128)S(1)}, u32[]{:S(2)}) copy-start(f32[1,2,256,256]{2,3,1,0:T(8,128)S(1)} %copy.9) | copy-start | bytes 1572868
  3.7 14.5 %collective-permute-start = (bf16[1,256,256]{1,2,0:T(8,128)(2,1)}, bf16[1,256,256]{1,2,0:T(8,128)(2,1)}, u32[]{:S(2)}, u32[]{:S(2)}) collective-permute-start(bf16[1,256,256]{1,2,0:T(8,128)(2,1)} %get-tuple-element.69), channel_id=1, source_target_pairs={{0,1},{1,2},{2,3},{3,4},{4,5},{5,6},{6,7},{7,8},{8,9},{9,10},{10,1... | collective-permute-start | bytes 393224 | tf_op jit(solution)/shard_map/ppermute | solution.py:19
  7.7 12.7 %collective-permute-start.1 = (bf16[1,256,256]{1,2,0:T(8,128)(2,1)}, bf16[1,256,256]{1,2,0:T(8,128)(2,1)S(1)}, u32[]{:S(2)}, u32[]{:S(2)}) collective-permute-start(bf16[1,256,256]{1,2,0:T(8,128)(2,1)} %get-tuple-element.68), channel_id=1, source_target_pairs={{1,0},{2,1},{3,2},{4,3},{5,4},{6,5},{7,6},{8,7},{9,8},{10,9},{11,1... | collective-permute-start | bytes 393224 | tf_op jit(solution)/shard_map/ppermute | solution.py:20
  68.5 53.1 %copy-start.4 = (f32[2,256,256]{1,2,0:T(8,128)}, f32[2,256,256]{1,2,0:T(8,128)S(1)}, u32[]{:S(2)}) copy-start(f32[2,256,256]{1,2,0:T(8,128)S(1)} %get-tuple-element.53) | copy-start | bytes 1572868
  106.8 9.0 %collective-permute-start.2 = (bf16[1,256,256]{1,2,0:T(8,128)(2,1)}, bf16[1,256,256]{1,2,0:T(8,128)(2,1)}, u32[]{:S(2)}, u32[]{:S(2)}) collective-permute-start(bf16[1,256,256]{1,2,0:T(8,128)(2,1)} %get-tuple-element.67), channel_id=1, source_target_pairs={{0,1},{1,2},{2,3},{3,4},{4,5},{5,6},{6,7},{7,8},{8,9},{9,10},{10,1... | collective-permute-start | bytes 393224 | tf_op jit(solution)/shard_map/ppermute | solution.py:19
  114.5 7.1 collective-permute-start.3
  163.8 53.1 %copy-start.3 = (f32[2,256,256]{1,2,0:T(8,128)}, f32[2,256,256]{1,2,0:T(8,128)S(1)}, u32[]{:S(2)}) copy-start(f32[2,256,256]{1,2,0:T(8,128)S(1)} %get-tuple-element.51) | copy-start | bytes 1572868
  204.0 7.0 collective-permute-start.4
  209.8 7.1 collective-permute-start.5
  299.3 7.0 collective-permute-start.6
  305.1 7.1 collective-permute-start.7
  399.1 23.3 %collective-permute-start.8 = (bf16[6,2,256,256]{2,3,0,1:T(8,128)(2,1)}, bf16[6,2,256,256]{2,3,0,1:T(8,128)(2,1)}, u32[]{:S(2)}, u32[]{:S(2)}) collective-permute-start(bf16[6,2,256,256]{2,3,0,1:T(8,128)(2,1)} %bitcast.387), channel_id=1, source_target_pairs={{0,16},{16,32},{32,48},{48,64},{64,80},{80,96},{96,112},{112,128},... | collective-permute-start | bytes 4718600 | tf_op jit(solution)/shard_map/ppermute | solution.py:28
  401.0 5.6 collective-permute-start.9
  403.0 8.2 %collective-permute-start.10 = (bf16[1,256,256]{1,2,0:T(8,128)(2,1)S(1)}, bf16[1,256,256]{1,2,0:T(8,128)(2,1)S(1)}, u32[]{:S(2)}, u32[]{:S(2)}) collective-permute-start(bf16[1,256,256]{1,2,0:T(8,128)(2,1)S(1)} %get-tuple-element.61), channel_id=1, source_target_pairs={{1,0},{2,1},{3,2},{4,3},{5,4},{6,5},{7,6},{8,7},{9,8},{10,9},{11,1... | collective-permute-start | bytes 393224 | tf_op jit(solution)/shard_map/ppermute | solution.py:20
  412.3 13.2 %copy-start.6 = (f32[2,256,256]{1,2,0:T(8,128)S(1)}, f32[2,256,256]{1,2,0:T(8,128)}, u32[]{:S(2)}) copy-start(f32[2,256,256]{1,2,0:T(8,128)} %get-tuple-element.47) | copy-start | bytes 1572868
  510.4 11.8 %copy-start.7 = (f32[2,256,256]{1,2,0:T(8,128)S(1)}, f32[2,256,256]{1,2,0:T(8,128)}, u32[]{:S(2)}) copy-start(f32[2,256,256]{1,2,0:T(8,128)} %get-tuple-element.43) | copy-start | bytes 1572868
  510.4 4.6 collective-permute-start.11
  513.2 7.0 collective-permute-start.12
  607.1 11.7 %copy-start.8 = (f32[2,256,256]{1,2,0:T(8,128)S(1)}, f32[2,256,256]{1,2,0:T(8,128)}, u32[]{:S(2)}) copy-start(f32[2,256,256]{1,2,0:T(8,128)} %get-tuple-element.41) | copy-start | bytes 1572868
  607.1 4.5 collective-permute-start.13
  609.8 7.0 collective-permute-start.14
  702.0 4.4 collective-permute-start.15
  704.6 7.0 collective-permute-start.16
  (3 other events, 9.5 us)
where the time goes:
time: 802 us; the launch traced here: 800 us
  blocking collectives  597 us (74%)
  matrix products  68 us (8%)
  waiting for transfers between devices  36.8 us (5%)
  starting transfers between devices  36 us (4%)
  other arithmetic  24.8 us (3%)
  between operations  23.8 us (3%)
  local copies, waits for them, and re-layouts  13.1 us (2%)
    psum x8, blocking collectives, relax(): step_norm = lax.psum(jnp.sum(step * step), 'sec')  303 us
    psum x8, blocking collectives, relax(): lax.psum((jnp.sum(iterate * iterate), jnp.sum(iterate * image)), 'sec')  294 us
    dot_general x8, matrix products, apply_operator(): jnp.einsum('wsik,wskj->sij', env_left, halfway, preferred_element_type=jn...  29 us
    ppermute x8, starting transfers between devices, with_halo(): before = lax.ppermute(last, axis, up)  23.6 us
    ppermute x8, waiting for transfers between devices, with_halo(): after = lax.ppermute(first, axis, down)  22.9 us
    dot_general x8, matrix products, apply_operator(): jnp.einsum('sik,skj->sij', hop_out[1], upper, preferred_element_type=jnp....  18.9 us
    dot_general x8, matrix products, apply_operator(): jnp.einsum('sik,skj->sij', hop_out[0], lower, preferred_element_type=jnp....  16.5 us
    reduce_sum x8, other arithmetic, relax(): step_norm = lax.psum(jnp.sum(step * step), 'sec')  16.3 us
  transfers between devices with their start and end apart: 17, of which 12 were waited for; matrix products, arithmetic and copies ran while one was open for 5% of the time, Pallas kernels for 0%

commit v1 on v0

v1 whole, which is shorter than its diff:
```python
import jax
import jax.numpy as jnp
from jax import lax
from jax.sharding import PartitionSpec as P

ITERS = 4


TAU = 0.05


def passed_along(shard, axis, by):
    length = lax.axis_size(axis)
    pairs = [(i, i + by) for i in range(length) if 0 <= i + by < length]
    return lax.ppermute(shard, axis, pairs)


def row_sum(values, axis):
    size = lax.axis_size(axis)
    rows = jnp.broadcast_to(values[None, None, :], (size, 1, values.shape[0]))
    return jnp.sum(lax.all_to_all(rows, axis, 0, 0), axis=(0, 1))


def apply_operator(iterate, env_left, env_right, hop_out, hop_in, block_mask):
    rounded = iterate.astype(jnp.bfloat16)
    before = passed_along(rounded[-1:], "sec", 1)
    after = passed_along(rounded[:1], "sec", -1)
    padded = jnp.concatenate([before, rounded, after], axis=0)
    halfway = jnp.einsum(
        "sij,wskj->wsik", rounded, env_right, preferred_element_type=jnp.float32
    ).astype(jnp.bfloat16)
    image = jnp.einsum("wsik,wskj->sij", env_left, halfway, preferred_element_type=jnp.float32)
    lower = jnp.einsum(
        "sij,skj->sik", padded[:-2], hop_in[0], preferred_element_type=jnp.float32
    ).astype(jnp.bfloat16)
    upper = jnp.einsum(
        "sij,skj->sik", padded[2:], hop_in[1], preferred_element_type=jnp.float32
    ).astype(jnp.bfloat16)
    image = image + jnp.einsum(
        "sik,skj->sij", hop_out[0], lower, preferred_element_type=jnp.float32
    )
    image = image + jnp.einsum(
        "sik,skj->sij", hop_out[1], upper, preferred_element_type=jnp.float32
    )
    return image * block_mask


def combination(gram, shift, live_count):
    def inner(left, right):
        total = jnp.float32(0.0)
        for i, a in enumerate(left):
            for j, b in enumerate(right):
                if a is not None and b is not None:
                    total = total + a * b * gram[min(i, j), max(i, j)]
        return total

    coefs = [jnp.float32(1.0)]
    energy = jnp.float32(0.0)
    for sweep_iter in range(ITERS):
        raised = [None] + coefs
        offset = (1.0 - inner(coefs, raised) / inner(coefs, coefs)) / TAU
        energy = shift + offset
        moved = [
            (raised[i] if raised[i] is not None else 0.0)
            + (TAU * offset * coefs[i] if i < len(coefs) else 0.0)
            for i in range(len(raised))
        ]
        scale = jnp.sqrt(live_count / inner(moved, moved))
        coefs = [scale * c for c in moved]
    return coefs, energy


def relax(iterate, env_left, env_right, hop_out, hop_in, block_mask, live_count):
    shift = float(env_left.shape[0])
    basis = [iterate]
    for sweep_iter in range(ITERS):
        image = apply_operator(basis[-1], env_left, env_right, hop_out, hop_in, block_mask)
        basis.append(basis[-1] - TAU * (image - shift * basis[-1]))
    pairs = [(i, j) for i in range(ITERS + 1) for j in range(i, ITERS + 1)]
    dots = jnp.stack([jnp.sum(basis[i] * basis[j]) for i, j in pairs])
    dots = row_sum(jnp.pad(dots, (0, 128 - len(pairs))), "sec")
    gram = {pair: dots[n] for n, pair in enumerate(pairs)}
    coefs, energy = combination(gram, shift, live_count)
    return (sum(c * v for c, v in zip(coefs, basis)), energy)


def grow(env_left, factor, own_dims):
    grown = jnp.einsum(
        "wsik,skj->wsij", env_left, factor, preferred_element_type=jnp.float32
    ).astype(jnp.bfloat16)
    renewed = jnp.einsum("ski,wskj->wsij", factor, grown, preferred_element_type=jnp.float32)
    return (renewed / own_dims.astype(jnp.float32)[None, :, None, None]).astype(jnp.bfloat16)


def body(psi, left_env, right_env, hop_outer, hop_inner, dims):
    sectors_here = psi.shape[1]
    capacity = psi.shape[2]
    first_sector = lax.axis_index("sec") * sectors_here
    env_left = left_env[0]
    env_right = right_env[0]
    hop_out = hop_outer[0]
    hop_in = hop_inner[0]
    earlier_env = passed_along(env_left, "seg", 1)
    earlier_dims = passed_along(dims[0], "seg", 1)
    own_dims = lax.dynamic_slice_in_dim(dims[0], first_sector, sectors_here)
    earlier_dims = lax.dynamic_slice_in_dim(earlier_dims, first_sector, sectors_here)
    sizes_f = dims[0].astype(jnp.float32)
    live_count = jnp.sum(sizes_f * sizes_f)
    indices = jnp.arange(capacity, dtype=jnp.int32)
    active = (indices[None, :] < own_dims[:, None]).astype(jnp.float32)
    block_mask = active[:, :, None] * active[:, None, :]
    iterate, energy = relax(
        psi[0] * block_mask, env_left, env_right, hop_out, hop_in, block_mask, live_count
    )
    factor = iterate.astype(jnp.bfloat16)
    earlier_factor = passed_along(factor, "seg", 1)
    renewed = grow(env_left, factor, own_dims)
    boundary = jnp.where(
        lax.axis_index("seg") == 0,
        env_left,
        grow(earlier_env, earlier_factor, jnp.maximum(earlier_dims, 1)),
    )
    iterate, energy = relax(iterate, boundary, env_right, hop_out, hop_in, block_mask, live_count)
    return (iterate[None], jnp.reshape(energy, (1,)), renewed[None])


def solution(mesh):
    return jax.shard_map(
        body,
        mesh=mesh,
        in_specs=(
            P("seg", "sec", None, None),
            P("seg", None, "sec", None, None),
            P("seg", None, "sec", None, None),
            P("seg", None, "sec", None, None),
            P("seg", None, "sec", None, None),
            P("seg", None),
        ),
        out_specs=(P("seg", "sec", None, None), P("seg"), P("seg", None, "sec", None, None)),
        check_vma=False,
    )
```

time: 802 us -> 330 us (0.41)
  blocking collectives: 597 us -> 0 us
  between operations: 23.8 us -> 112 us
  starting transfers between devices: 36 us -> 75.4 us
  local copies, waits for them, and re-layouts: 13.1 us -> 36.2 us
  other arithmetic: 24.8 us -> 5.69 us
    psum x16 -> x0, blocking collectives: 597 us -> none  [the longest x8 303 us: relax(): step_norm = lax.psum(jnp.sum(step * step), 'sec')]
    ppermute x1 -> x19, starting transfers between devices: 1.91 us -> 53.1 us  [passed_along(): return lax.ppermute(shard, axis, pairs)]
    ppermute x16 -> x0, starting transfers between devices: 34.1 us -> none  [the longest x8 23.6 us: with_halo(): before = lax.ppermute(last, axis, up)]
    ppermute x16 -> x0, waiting for transfers between devices: 26.8 us -> none  [the longest x8 22.9 us: with_halo(): after = lax.ppermute(first, axis, down)]
    all_to_all x0 -> x2, starting transfers between devices: none -> 22.3 us  [row_sum(): return jnp.sum(lax.all_to_all(rows, axis, 0, 0), axis=(0, 1))]
    another operation x0 -> x2, local copies, waits for them, and re-layouts: none -> 18.7 us  [relax(): dots = jnp.stack([jnp.sum(basis[i] * basis[j]) for i, j in pairs])]
    dot_general x1 -> x18, matrix products: 3.55 us -> 22.1 us  [the longest x8 8.09 us: apply_operator(): jnp.einsum('sij,skj->sik', padded[:-2], hop_in[0], preferred_element_type...]
    reduce_sum x8 -> x2, other arithmetic: 16.3 us -> 0.03 us  [row_sum(): return jnp.sum(lax.all_to_all(rows, axis, 0, 0), axis=(0, 1))]
  transfers between devices with their start and end apart: 17 -> 21, of which waited for: 12 -> 10; matrix products, arithmetic and copies ran while one was open for 5% -> 21% of each run, Pallas kernels for 0% -> 0%
where the time goes in v1:
time: 330 us; the launch traced here: 325 us
  between operations  112 us (34%)
  starting transfers between devices  75.4 us (23%)
  matrix products  63.1 us (19%)
  local copies, waits for them, and re-layouts  36.2 us (11%)
  waiting for transfers between devices  32.6 us (10%)
  other arithmetic  5.69 us (2%)
    ppermute x19, starting transfers between devices, passed_along(): return lax.ppermute(shard, axis, pairs)  53.1 us
    dot_general x8, matrix products, apply_operator(): jnp.einsum('wsik,wskj->sij', env_left, halfway, preferred_element_type=jn...  26.8 us
    ppermute x19, waiting for transfers between devices, passed_along(): return lax.ppermute(shard, axis, pairs)  24.2 us
    all_to_all x2, starting transfers between devices, row_sum(): return jnp.sum(lax.all_to_all(rows, axis, 0, 0), axis=(0, 1))  22.3 us
    another operation x2, local copies, waits for them, and re-layouts, relax(): dots = jnp.stack([jnp.sum(basis[i] * basis[j]) for i, j in pairs])  18.7 us
    unnamed x66, local copies, waits for them, and re-layouts  10.8 us
    all_to_all x2, waiting for transfers between devices, row_sum(): return jnp.sum(lax.all_to_all(rows, axis, 0, 0), axis=(0, 1))  8.34 us
    dot_general x8, matrix products, apply_operator(): jnp.einsum('sij,skj->sik', padded[:-2], hop_in[0], preferred_element_type...  8.09 us
  transfers between devices with their start and end apart: 21, of which 10 were waited for; matrix products, arithmetic and copies ran while one was open for 21% of the time, Pallas kernels for 0%

profile of v1, /device:TPU:128, one launch (start us, length us, event | category | flops | bytes accessed | tf_op | source)
XLA Modules:
  0.0 325.0 jit_solution(17075329245595711164)
XLA Ops:
  3.0 4.0 %collective-permute-start = (bf16[1,256,256]{1,2,0:T(8,128)(2,1)S(1)}, bf16[1,256,256]{1,2,0:T(8,128)(2,1)}, u32[]{:S(2)}, u32[]{:S(2)}) collective-permute-start(bf16[1,256,256]{1,2,0:T(8,128)(2,1)S(1)} %get-tuple-element.61), channel_id=1, source_target_pairs={{0,1},{1,2},{2,3},{3,4},{4,5},{5,6},{6,7},{7,8},{8,9},{9,10},{10,1... | collective-permute-start | bytes 393224 | tf_op jit(solution)/shard_map/ppermute | solution.py:15
  13.0 3.3 %fusion.21 = f32[2,256,256]{2,1,0:T(8,128)} fusion(bf16[2,256,256]{1,2,0:T(8,128)(2,1)S(1)} %fusion.199, bf16[1,6,2,256,256]{4,3,2,1,0:T(8,128)(2,1)} %param.7, bf16[1,6,2,256,256]{4,3,2,1,0:T(8,128)(2,1)S(1)} %copy-done), kind=kOutput, calls=%fused_computation.42 | convolution fusion | flops 806092800 | bytes 3932160 | tf_op jit(solution)/shard_map/wsik,wskj->sij/dot_general | solution.py:32
  19.4 5.2 %collective-permute-start.2 = (bf16[1,256,256]{1,2,0:T(8,128)(2,1)}, bf16[1,256,256]{1,2,0:T(8,128)(2,1)}, u32[]{:S(2)}, u32[]{:S(2)}) collective-permute-start(bf16[1,256,256]{1,2,0:T(8,128)(2,1)} %get-tuple-element.59), channel_id=1, source_target_pairs={{0,1},{1,2},{2,3},{3,4},{4,5},{5,6},{6,7},{7,8},{8,9},{9,10},{10,1... | collective-permute-start | bytes 393224 | tf_op jit(solution)/shard_map/ppermute | solution.py:15
  31.0 5.2 %collective-permute-done.3 = bf16[1,256,256]{1,2,0:T(8,128)(2,1)S(1)} collective-permute-done((bf16[1,256,256]{1,2,0:T(8,128)(2,1)S(1)}, bf16[1,256,256]{1,2,0:T(8,128)(2,1)S(1)}, u32[]{:S(2)}, u32[]{:S(2)}) %collective-permute-start.3) | collective-permute-done | bytes 131104 | tf_op jit(solution)/shard_map/ppermute | solution.py:15
  41.1 3.4 %fusion.27 = f32[2,256,256]{2,1,0:T(8,128)} fusion(bf16[2,256,256]{1,2,0:T(8,128)(2,1)S(1)} %get-tuple-element.94, bf16[1,6,2,256,256]{4,3,2,1,0:T(8,128)(2,1)} %param.7, bf16[1,6,2,256,256]{4,3,2,1,0:T(8,128)(2,1)S(1)} %copy-done), kind=kOutput, calls=%fused_computation.44 | convolution fusion | flops 806092800 | bytes 3932160 | tf_op jit(solution)/shard_map/wsik,wskj->sij/dot_general | solution.py:32
  47.5 4.6 %collective-permute-done.5 = bf16[1,256,256]{1,2,0:T(8,128)(2,1)S(1)} collective-permute-done((bf16[1,256,256]{1,2,0:T(8,128)(2,1)S(1)}, bf16[1,256,256]{1,2,0:T(8,128)(2,1)S(1)}, u32[]{:S(2)}, u32[]{:S(2)}) %collective-permute-start.5) | collective-permute-done | bytes 131104 | tf_op jit(solution)/shard_map/ppermute | solution.py:15
  54.1 6.6 %collective-permute-start.6 = (bf16[1,256,256]{1,2,0:T(8,128)(2,1)}, bf16[1,256,256]{1,2,0:T(8,128)(2,1)}, u32[]{:S(2)}, u32[]{:S(2)}) collective-permute-start(bf16[1,256,256]{1,2,0:T(8,128)(2,1)} %get-tuple-element.55), channel_id=1, source_target_pairs={{0,1},{1,2},{2,3},{3,4},{4,5},{5,6},{6,7},{7,8},{8,9},{9,10},{10,1... | collective-permute-start | bytes 393224 | tf_op jit(solution)/shard_map/ppermute | solution.py:15
  60.7 3.4 %fusion.30 = f32[2,256,256]{2,1,0:T(8,128)} fusion(bf16[2,256,256]{1,2,0:T(8,128)(2,1)S(1)} %get-tuple-element.96, bf16[1,6,2,256,256]{4,3,2,1,0:T(8,128)(2,1)} %param.7, bf16[1,6,2,256,256]{4,3,2,1,0:T(8,128)(2,1)S(1)} %copy-done), kind=kOutput, calls=%fused_computation.45 | convolution fusion | flops 806092800 | bytes 3932160 | tf_op jit(solution)/shard_map/wsik,wskj->sij/dot_general | solution.py:32
  67.1 3.9 %collective-permute-done.7 = bf16[1,256,256]{1,2,0:T(8,128)(2,1)S(1)} collective-permute-done((bf16[1,256,256]{1,2,0:T(8,128)(2,1)S(1)}, bf16[1,256,256]{1,2,0:T(8,128)(2,1)S(1)}, u32[]{:S(2)}, u32[]{:S(2)}) %collective-permute-start.7) | collective-permute-done | bytes 131104 | tf_op jit(solution)/shard_map/ppermute | solution.py:15
  73.7 9.2 %stack.111 = f32[15]{0:T(128)S(1)} concatenate(f32[1]{0:T(128)} %bitcast.3, f32[1]{0:T(128)} %bitcast.15, f32[1]{0:T(128)} %bitcast.21, f32[1]{0:T(128)} %bitcast.27, f32[1]{0:T(128)} %bitcast.33, f32[1]{0:T(128)} %bitcast.34, f32[1]{0:T(128)} %bitcast.35, f32[1]{0:T(128)} %bitcast.36, f32[1]{0:T(128)} %bitcast.37, f32[1]{0:T(128)} %bitcast.38, f32[1]{0:T(128)} %bitcast.39, ...), dimensions={0} | concatenate | bytes 120 | tf_op jit(solution)/shard_map/stack | solution.py:80
  83.5 7.9 %all-to-all-start = ((f32[16,1,128]{2,1,0:T(1,128)}), f32[16,1,128]{2,1,0:T(1,128)S(1)}, u32[]{:S(2)}, u32[]{:S(2)}) async-start(f32[16,1,128]{2,1,0:T(1,128)} %broadcast_in_dim.8), calls=%async_computation | async-start | bytes 16384 | tf_op jit(solution)/shard_map/all_to_all | solution.py:21
  92.0 7.0 %all-to-all-done = f32[16,1,128]{2,1,0:T(1,128)S(1)} async-done(((f32[16,1,128]{2,1,0:T(1,128)}), f32[16,1,128]{2,1,0:T(1,128)S(1)}, u32[]{:S(2)}, u32[]{:S(2)}) %all-to-all-start) | async-done | bytes 8224 | tf_op jit(solution)/shard_map/all_to_all | solution.py:21
  161.2 4.2 %collective-permute-done.10 = s32[32]{0:T(128)S(1)} collective-permute-done((s32[32]{0:T(128)S(1)}, s32[32]{0:T(128)S(1)}, u32[]{:S(2)}, u32[]{:S(2)}) %collective-permute-start.10) | collective-permute-done | bytes 160 | tf_op jit(solution)/shard_map/ppermute | solution.py:15
  170.8 3.7 %collective-permute-done.12 = bf16[1,256,256]{1,2,0:T(8,128)(2,1)S(1)} collective-permute-done((bf16[1,256,256]{1,2,0:T(8,128)(2,1)S(1)}, bf16[1,256,256]{1,2,0:T(8,128)(2,1)S(1)}, u32[]{:S(2)}, u32[]{:S(2)}) %collective-permute-start.12) | collective-permute-done | bytes 131104 | tf_op jit(solution)/shard_map/ppermute | solution.py:15
  176.9 4.1 %bitcast_select_fusion = bf16[6,2,256,256]{3,2,0,1:T(8,128)(2,1)} fusion(pred[]{:T(512)S(6)} %eq.3, f32[2]{0:T(128)S(1)} %maximum_convert_fusion, bf16[6,2,256,256]{3,2,0,1:T(8,128)(2,1)} %collective-permute-done.9, bf16[2,256,256]{1,2,0:T(8,128)(2,1)S(1)} %collective-permute-done.8, bf16[1,6,2,256,256]{4,3,2,1,0:T(8,128)(2,1)} %param.7), kind=kOutput, calls=%fused_computation.30 | convolution fusion | flops 808452096 | bytes 4980745 | tf_op jit(solution)/shard_map/ski,wskj->wsij/dot_general | solution.py:91
  188.5 3.4 %fusion.36 = f32[2,256,256]{1,2,0:T(8,128)} fusion(bf16[6,2,256,256]{3,2,0,1:T(8,128)(2,1)} %bitcast_select_fusion, bf16[2,256,256]{1,2,0:T(8,128)(2,1)} %copy-done.12, bf16[1,6,2,256,256]{4,3,2,1,0:T(8,128)(2,1)S(1)} %copy-done), kind=kOutput, calls=%fused_computation.47 | convolution fusion | flops 806092800 | bytes 3932160 | tf_op jit(solution)/shard_map/wsik,wskj->sij/dot_general | solution.py:32
  191.9 4.7 %collective-permute-start.13 = (bf16[1,256,256]{1,2,0:T(8,128)(2,1)S(1)}, bf16[1,256,256]{1,2,0:T(8,128)(2,1)S(1)}, u32[]{:S(2)}, u32[]{:S(2)}) collective-permute-start(bf16[1,256,256]{1,2,0:T(8,128)(2,1)S(1)} %get-tuple-element.50), channel_id=1, source_target_pairs={{0,1},{1,2},{2,3},{3,4},{4,5},{5,6},{6,7},{7,8},{8,9},{9,10},{10,1... | collective-permute-start | bytes 393224 | tf_op jit(solution)/shard_map/ppermute | solution.py:15
  203.2 3.4 %fusion.39 = f32[2,256,256]{1,2,0:T(8,128)} fusion(bf16[6,2,256,256]{3,2,0,1:T(8,128)(2,1)} %bitcast_select_fusion, bf16[2,256,256]{1,2,0:T(8,128)(2,1)} %copy-done.14, bf16[1,6,2,256,256]{4,3,2,1,0:T(8,128)(2,1)S(1)} %copy-done), kind=kOutput, calls=%fused_computation.48 | convolution fusion | flops 806092800 | bytes 3932160 | tf_op jit(solution)/shard_map/wsik,wskj->sij/dot_general | solution.py:32
  206.5 5.1 %collective-permute-start.15 = (bf16[1,256,256]{1,2,0:T(8,128)(2,1)S(1)}, bf16[1,256,256]{1,2,0:T(8,128)(2,1)S(1)}, u32[]{:S(2)}, u32[]{:S(2)}) collective-permute-start(bf16[1,256,256]{1,2,0:T(8,128)(2,1)S(1)} %get-tuple-element.48), channel_id=1, source_target_pairs={{0,1},{1,2},{2,3},{3,4},{4,5},{5,6},{6,7},{7,8},{8,9},{9,10},{10,1... | collective-permute-start | bytes 393224 | tf_op jit(solution)/shard_map/ppermute | solution.py:15
  218.3 3.4 %fusion.42 = f32[2,256,256]{1,2,0:T(8,128)} fusion(bf16[6,2,256,256]{3,2,0,1:T(8,128)(2,1)} %bitcast_select_fusion, bf16[2,256,256]{1,2,0:T(8,128)(2,1)} %copy-done.10, bf16[1,6,2,256,256]{4,3,2,1,0:T(8,128)(2,1)S(1)} %copy-done), kind=kOutput, calls=%fused_computation.49 | convolution fusion | flops 806092800 | bytes 3932160 | tf_op jit(solution)/shard_map/wsik,wskj->sij/dot_general | solution.py:32
  221.7 5.1 %collective-permute-start.17 = (bf16[1,256,256]{1,2,0:T(8,128)(2,1)S(1)}, bf16[1,256,256]{1,2,0:T(8,128)(2,1)S(1)}, u32[]{:S(2)}, u32[]{:S(2)}) collective-permute-start(bf16[1,256,256]{1,2,0:T(8,128)(2,1)S(1)} %get-tuple-element.46), channel_id=1, source_target_pairs={{0,1},{1,2},{2,3},{3,4},{4,5},{5,6},{6,7},{7,8},{8,9},{9,10},{10,1... | collective-permute-start | bytes 393224 | tf_op jit(solution)/shard_map/ppermute | solution.py:15
  231.9 9.5 %stack.127 = f32[15]{0:T(128)S(1)} concatenate(f32[1]{0:T(128)} %bitcast.60, f32[1]{0:T(128)} %bitcast.71, f32[1]{0:T(128)} %bitcast.77, f32[1]{0:T(128)} %bitcast.83, f32[1]{0:T(128)} %bitcast.89, f32[1]{0:T(128)} %bitcast.90, f32[1]{0:T(128)} %bitcast.91, f32[1]{0:T(128)} %bitcast.92, f32[1]{0:T(128)} %bitcast.93, f32[1]{0:T(128)} %bitcast.94, f32[1]{0:T(128)} %bitcast.95, ...), dimensions={0} | concatenate | bytes 120 | tf_op jit(solution)/shard_map/stack | solution.py:80
  242.0 14.4 %all-to-all-start.1 = ((f32[16,1,128]{2,1,0:T(1,128)}), f32[16,1,128]{2,1,0:T(1,128)S(1)}, u32[]{:S(2)}, u32[]{:S(2)}) async-start(f32[16,1,128]{2,1,0:T(1,128)} %broadcast_in_dim.9), calls=%async_computation.1 | async-start | bytes 16384 | tf_op jit(solution)/shard_map/all_to_all | solution.py:21
  256.4 3.6 %fusion.18 = bf16[1,6,2,256,256]{3,4,1,2,0:T(8,128)(2,1)} fusion(f32[2]{0:T(128)S(1)} %get-tuple-element.42, bf16[2,256,256]{1,2,0:T(8,128)(2,1)S(1)} %get-tuple-element.44, bf16[1,6,2,256,256]{4,3,2,1,0:T(8,128)(2,1)} %param.7), kind=kOutput, calls=%fused_computation.41 | convolution fusion | flops 807665664 | bytes 3407880 | tf_op jit(solution)/shard_map/ski,wskj->wsij/dot_general | solution.py:91
  (151 shorter events, 84.8 us)
Async XLA Ops:
  3.0 13.4 %collective-permute-start = (bf16[1,256,256]{1,2,0:T(8,128)(2,1)S(1)}, bf16[1,256,256]{1,2,0:T(8,128)(2,1)}, u32[]{:S(2)}, u32[]{:S(2)}) collective-permute-start(bf16[1,256,256]{1,2,0:T(8,128)(2,1)S(1)} %get-tuple-element.61), channel_id=1, source_target_pairs={{0,1},{1,2},{2,3},{3,4},{4,5},{5,6},{6,7},{7,8},{8,9},{9,10},{10,1... | collective-permute-start | bytes 393224 | tf_op jit(solution)/shard_map/ppermute | solution.py:15
  7.0 11.0 %collective-permute-start.1 = (bf16[1,256,256]{1,2,0:T(8,128)(2,1)S(1)}, bf16[1,256,256]{1,2,0:T(8,128)(2,1)S(1)}, u32[]{:S(2)}, u32[]{:S(2)}) collective-permute-start(bf16[1,256,256]{1,2,0:T(8,128)(2,1)S(1)} %get-tuple-element.60), channel_id=1, source_target_pairs={{1,0},{2,1},{3,2},{4,3},{5,4},{6,5},{7,6},{8,7},{9,8},{10,9},{11,1... | collective-permute-start | bytes 393224 | tf_op jit(solution)/shard_map/ppermute | solution.py:15
  11.0 165.9 %collective-permute-start.9 = (bf16[6,2,256,256]{3,2,0,1:T(8,128)(2,1)}, bf16[6,2,256,256]{3,2,0,1:T(8,128)(2,1)}, u32[]{:S(2)}, u32[]{:S(2)}) collective-permute-start(bf16[6,2,256,256]{3,2,0,1:T(8,128)(2,1)} %bitcast.481), channel_id=1, source_target_pairs={{0,16},{16,32},{32,48},{48,64},{64,80},{80,96},{96,112},{112,128},... | collective-permute-start | bytes 4718600 | tf_op jit(solution)/shard_map/ppermute | solution.py:15
  18.7 52.6 %copy-start.2 = (f32[2,256,256]{1,2,0:T(8,128)}, f32[2,256,256]{1,2,0:T(8,128)S(1)}, u32[]{:S(2)}) copy-start(f32[2,256,256]{1,2,0:T(8,128)S(1)} %get-tuple-element.93) | copy-start | bytes 1572868
  19.4 10.0 %collective-permute-start.2 = (bf16[1,256,256]{1,2,0:T(8,128)(2,1)}, bf16[1,256,256]{1,2,0:T(8,128)(2,1)}, u32[]{:S(2)}, u32[]{:S(2)}) collective-permute-start(bf16[1,256,256]{1,2,0:T(8,128)(2,1)} %get-tuple-element.59), channel_id=1, source_target_pairs={{0,1},{1,2},{2,3},{3,4},{4,5},{5,6},{6,7},{7,8},{8,9},{9,10},{10,1... | collective-permute-start | bytes 393224 | tf_op jit(solution)/shard_map/ppermute | solution.py:15
  28.0 8.3 %collective-permute-start.3 = (bf16[1,256,256]{1,2,0:T(8,128)(2,1)S(1)}, bf16[1,256,256]{1,2,0:T(8,128)(2,1)S(1)}, u32[]{:S(2)}, u32[]{:S(2)}) collective-permute-start(bf16[1,256,256]{1,2,0:T(8,128)(2,1)S(1)} %get-tuple-element.58), channel_id=1, source_target_pairs={{1,0},{2,1},{3,2},{4,3},{5,4},{6,5},{7,6},{8,7},{9,8},{10,9},{11,1... | collective-permute-start | bytes 393224 | tf_op jit(solution)/shard_map/ppermute | solution.py:15
  38.3 7.6 %collective-permute-start.4 = (bf16[1,256,256]{1,2,0:T(8,128)(2,1)}, bf16[1,256,256]{1,2,0:T(8,128)(2,1)}, u32[]{:S(2)}, u32[]{:S(2)}) collective-permute-start(bf16[1,256,256]{1,2,0:T(8,128)(2,1)} %get-tuple-element.57), channel_id=1, source_target_pairs={{0,1},{1,2},{2,3},{3,4},{4,5},{5,6},{6,7},{7,8},{8,9},{9,10},{10,1... | collective-permute-start | bytes 393224 | tf_op jit(solution)/shard_map/ppermute | solution.py:15
  44.4 7.6 %collective-permute-start.5 = (bf16[1,256,256]{1,2,0:T(8,128)(2,1)S(1)}, bf16[1,256,256]{1,2,0:T(8,128)(2,1)S(1)}, u32[]{:S(2)}, u32[]{:S(2)}) collective-permute-start(bf16[1,256,256]{1,2,0:T(8,128)(2,1)S(1)} %get-tuple-element.56), channel_id=1, source_target_pairs={{1,0},{2,1},{3,2},{4,3},{5,4},{6,5},{7,6},{8,7},{9,8},{10,9},{11,1... | collective-permute-start | bytes 393224 | tf_op jit(solution)/shard_map/ppermute | solution.py:15
  54.1 11.4 %collective-permute-start.6 = (bf16[1,256,256]{1,2,0:T(8,128)(2,1)}, bf16[1,256,256]{1,2,0:T(8,128)(2,1)}, u32[]{:S(2)}, u32[]{:S(2)}) collective-permute-start(bf16[1,256,256]{1,2,0:T(8,128)(2,1)} %get-tuple-element.55), channel_id=1, source_target_pairs={{0,1},{1,2},{2,3},{3,4},{4,5},{5,6},{6,7},{7,8},{8,9},{9,10},{10,1... | collective-permute-start | bytes 393224 | tf_op jit(solution)/shard_map/ppermute | solution.py:15
  64.1 7.0 %collective-permute-start.7 = (bf16[1,256,256]{1,2,0:T(8,128)(2,1)S(1)}, bf16[1,256,256]{1,2,0:T(8,128)(2,1)S(1)}, u32[]{:S(2)}, u32[]{:S(2)}) collective-permute-start(bf16[1,256,256]{1,2,0:T(8,128)(2,1)S(1)} %get-tuple-element.54), channel_id=1, source_target_pairs={{1,0},{2,1},{3,2},{4,3},{5,4},{6,5},{7,6},{8,7},{9,8},{10,9},{11,1... | collective-permute-start | bytes 393224 | tf_op jit(solution)/shard_map/ppermute | solution.py:15
  71.4 20.1 %copy-start.22 = (s32[1,32]{1,0:T(1,128)S(1)}, s32[1,32]{1,0:T(1,128)}, u32[]{:S(2)}) copy-start(s32[1,32]{1,0:T(1,128)} %param.11) | copy-start | bytes 388
  83.5 15.5 %all-to-all-start = ((f32[16,1,128]{2,1,0:T(1,128)}), f32[16,1,128]{2,1,0:T(1,128)S(1)}, u32[]{:S(2)}, u32[]{:S(2)}) async-start(f32[16,1,128]{2,1,0:T(1,128)} %broadcast_in_dim.8), calls=%async_computation | async-start | bytes 16384 | tf_op jit(solution)/shard_map/all_to_all | solution.py:21
  156.3 12.5 %collective-permute-start.11 = (bf16[1,256,256]{1,2,0:T(8,128)(2,1)S(1)}, bf16[1,256,256]{1,2,0:T(8,128)(2,1)}, u32[]{:S(2)}, u32[]{:S(2)}) collective-permute-start(bf16[1,256,256]{1,2,0:T(8,128)(2,1)S(1)} %get-tuple-element.52), channel_id=1, source_target_pairs={{0,1},{1,2},{2,3},{3,4},{4,5},{5,6},{6,7},{7,8},{8,9},{9,10},{10,1... | collective-permute-start | bytes 393224 | tf_op jit(solution)/shard_map/ppermute | solution.py:15
  159.2 6.1 %collective-permute-start.10 = (s32[32]{0:T(128)S(1)}, s32[32]{0:T(128)S(1)}, u32[]{:S(2)}, u32[]{:S(2)}) collective-permute-start(s32[32]{0:T(128)S(1)} %bitcast.484), channel_id=1, source_target_pairs={{0,16},{16,32},{32,48},{48,64},{64,80},{80,96},{96,112},{112,128},... | collective-permute-start | bytes 392 | tf_op jit(solution)/shard_map/ppermute | solution.py:15
  165.4 11.4 %collective-permute-start.8 = (bf16[2,256,256]{1,2,0:T(8,128)(2,1)S(1)}, bf16[2,256,256]{1,2,0:T(8,128)(2,1)S(1)}, u32[]{:S(2)}, u32[]{:S(2)}) collective-permute-start(bf16[2,256,256]{1,2,0:T(8,128)(2,1)S(1)} %get-tuple-element.44), channel_id=1, source_target_pairs={{0,16},{16,32},{32,48},{48,64},{64,80},{80,96},{96,112},{112,128},... | collective-permute-start | bytes 786440 | tf_op jit(solution)/shard_map/ppermute | solution.py:15
  167.3 7.2 %collective-permute-start.12 = (bf16[1,256,256]{1,2,0:T(8,128)(2,1)S(1)}, bf16[1,256,256]{1,2,0:T(8,128)(2,1)S(1)}, u32[]{:S(2)}, u32[]{:S(2)}) collective-permute-start(bf16[1,256,256]{1,2,0:T(8,128)(2,1)S(1)} %get-tuple-element.53), channel_id=1, source_target_pairs={{1,0},{2,1},{3,2},{4,3},{5,4},{6,5},{7,6},{8,7},{9,8},{10,9},{11,1... | collective-permute-start | bytes 393224 | tf_op jit(solution)/shard_map/ppermute | solution.py:15
  187.2 9.3 %collective-permute-start.14 = (bf16[1,256,256]{1,2,0:T(8,128)(2,1)}, bf16[1,256,256]{1,2,0:T(8,128)(2,1)}, u32[]{:S(2)}, u32[]{:S(2)}) collective-permute-start(bf16[1,256,256]{1,2,0:T(8,128)(2,1)} %get-tuple-element.51), channel_id=1, source_target_pairs={{1,0},{2,1},{3,2},{4,3},{5,4},{6,5},{7,6},{8,7},{9,8},{10,9},{11,1... | collective-permute-start | bytes 393224 | tf_op jit(solution)/shard_map/ppermute | solution.py:15
  191.9 7.2 %collective-permute-start.13 = (bf16[1,256,256]{1,2,0:T(8,128)(2,1)S(1)}, bf16[1,256,256]{1,2,0:T(8,128)(2,1)S(1)}, u32[]{:S(2)}, u32[]{:S(2)}) collective-permute-start(bf16[1,256,256]{1,2,0:T(8,128)(2,1)S(1)} %get-tuple-element.50), channel_id=1, source_target_pairs={{0,1},{1,2},{2,3},{3,4},{4,5},{5,6},{6,7},{7,8},{8,9},{9,10},{10,1... | collective-permute-start | bytes 393224 | tf_op jit(solution)/shard_map/ppermute | solution.py:15
  201.9 9.8 %collective-permute-start.16 = (bf16[1,256,256]{1,2,0:T(8,128)(2,1)}, bf16[1,256,256]{1,2,0:T(8,128)(2,1)}, u32[]{:S(2)}, u32[]{:S(2)}) collective-permute-start(bf16[1,256,256]{1,2,0:T(8,128)(2,1)} %get-tuple-element.49), channel_id=1, source_target_pairs={{1,0},{2,1},{3,2},{4,3},{5,4},{6,5},{7,6},{8,7},{9,8},{10,9},{11,1... | collective-permute-start | bytes 393224 | tf_op jit(solution)/shard_map/ppermute | solution.py:15
  206.5 7.6 %collective-permute-start.15 = (bf16[1,256,256]{1,2,0:T(8,128)(2,1)S(1)}, bf16[1,256,256]{1,2,0:T(8,128)(2,1)S(1)}, u32[]{:S(2)}, u32[]{:S(2)}) collective-permute-start(bf16[1,256,256]{1,2,0:T(8,128)(2,1)S(1)} %get-tuple-element.48), channel_id=1, source_target_pairs={{0,1},{1,2},{2,3},{3,4},{4,5},{5,6},{6,7},{7,8},{8,9},{9,10},{10,1... | collective-permute-start | bytes 393224 | tf_op jit(solution)/shard_map/ppermute | solution.py:15
  217.0 9.8 %collective-permute-start.18 = (bf16[1,256,256]{1,2,0:T(8,128)(2,1)}, bf16[1,256,256]{1,2,0:T(8,128)(2,1)}, u32[]{:S(2)}, u32[]{:S(2)}) collective-permute-start(bf16[1,256,256]{1,2,0:T(8,128)(2,1)} %get-tuple-element.47), channel_id=1, source_target_pairs={{1,0},{2,1},{3,2},{4,3},{5,4},{6,5},{7,6},{8,7},{9,8},{10,9},{11,1... | collective-permute-start | bytes 393224 | tf_op jit(solution)/shard_map/ppermute | solution.py:15
  221.7 7.6 %collective-permute-start.17 = (bf16[1,256,256]{1,2,0:T(8,128)(2,1)S(1)}, bf16[1,256,256]{1,2,0:T(8,128)(2,1)S(1)}, u32[]{:S(2)}, u32[]{:S(2)}) collective-permute-start(bf16[1,256,256]{1,2,0:T(8,128)(2,1)S(1)} %get-tuple-element.46), channel_id=1, source_target_pairs={{0,1},{1,2},{2,3},{3,4},{4,5},{5,6},{6,7},{7,8},{8,9},{9,10},{10,1... | collective-permute-start | bytes 393224 | tf_op jit(solution)/shard_map/ppermute | solution.py:15
  242.0 22.0 %all-to-all-start.1 = ((f32[16,1,128]{2,1,0:T(1,128)}), f32[16,1,128]{2,1,0:T(1,128)S(1)}, u32[]{:S(2)}, u32[]{:S(2)}) async-start(f32[16,1,128]{2,1,0:T(1,128)} %broadcast_in_dim.9), calls=%async_computation.1 | async-start | bytes 16384 | tf_op jit(solution)/shard_map/all_to_all | solution.py:21
  259.9 59.7 %copy-start.7 = (f32[2,256,256]{1,2,0:T(8,128)S(1)}, f32[2,256,256]{1,2,0:T(8,128)}, u32[]{:S(2)}) copy-start(f32[2,256,256]{1,2,0:T(8,128)} %get-tuple-element.102) | copy-start | bytes 1572868
  (28 other events, 161.7 us)

commit v2 on v0

v2 whole, which is shorter than its diff:
```python
import functools

import jax
import jax.numpy as jnp
from jax import lax
from jax.experimental import pallas as pl
from jax.experimental.pallas import tpu as pltpu
from jax.sharding import PartitionSpec as P

ITERS = 4
TAU = 0.05
F32 = jnp.float32
BF16 = jnp.bfloat16
LANES = 128
VMEM_LIMIT = 24 << 20
ROWS = 8

VMEM = pl.BlockSpec(memory_space=pltpu.VMEM)
SMEM = pl.BlockSpec(memory_space=pltpu.SMEM)


def nn(a, b):
    return lax.dot_general(a, b, (((1,), (0,)), ((), ())), preferred_element_type=F32)


def nt(a, b):
    return lax.dot_general(a, b, (((1,), (1,)), ((), ())), preferred_element_type=F32)


def hop(block, inner, outer):
    return nn(outer, nt(block, inner).astype(BF16))


def active(dim, cap):
    rows = lax.broadcasted_iota(jnp.int32, (cap, cap), 0)
    cols = lax.broadcasted_iota(jnp.int32, (cap, cap), 1)
    return jnp.logical_and(rows < dim, cols < dim)


def masked(block, dim):
    return jnp.where(active(dim, block.shape[-1]), block, 0.0)


def local_part(v, env, right, outer, inner, dims, first, shift):
    held = len(v)
    b = [x.astype(BF16) for x in v]
    out = []
    for s in range(held):
        image = None
        for w in range(right.shape[1]):
            term = nn(env(w, s), nt(b[s], right[0, w, s]).astype(BF16))
            image = term if image is None else image + term
        if s > 0:
            image = image + hop(b[s - 1], inner[0, 0, s], outer[0, 0, s])
        if s + 1 < held:
            image = image + hop(b[s + 1], inner[0, 1, s], outer[0, 1, s])
        out.append(v[s] - TAU * (masked(image, dims[0, first + s]) - shift * v[s]))
    return out


def dot_rows(basis, last):
    rows = lax.broadcasted_iota(jnp.int32, (ROWS, LANES), 0)
    out = jnp.zeros((ROWS, LANES), F32)
    for i, other in enumerate(basis):
        total = sum(jnp.sum(a * b, axis=0, keepdims=True) for a, b in zip(other, last))
        total = sum(total[:, n : n + LANES] for n in range(0, total.shape[1], LANES))
        out = jnp.where(rows == i, total, out)
    return out


def put_edges(odd, low, high, inside, across):
    inside[...] = jnp.where(odd, low, high)
    across[...] = jnp.where(odd, high, low)


def edges_from(odd, inside, across):
    return jnp.where(odd, inside, across), jnp.where(odd, across, inside)


def is_odd(place):
    return place[0] % 2 == 1


def start_kernel(
    place, dims, psi, low_outer, low_inner, high_outer, high_inner, v0, inside, across
):
    held = psi.shape[1]
    first = place[0] * held
    odd = is_odd(place)
    blocks = [masked(psi[0, s], dims[0, first + s]) for s in range(held)]
    for s in range(held):
        v0[s] = blocks[s]
    low = [blocks[0].astype(BF16), low_outer[0, 0, 0], low_inner[0, 0, 0]]
    high = [blocks[-1].astype(BF16), high_outer[0, 0, 0], high_inner[0, 0, 0]]
    for n in range(3):
        inside[n] = jnp.where(odd, low[n], high[n])
        across[n] = jnp.where(odd, high[n], low[n])


def local_kernel(shift, place, dims, v0, left, right, outer, inner, q, inside, across, dots):
    held = v0.shape[0]
    v = [v0[s] for s in range(held)]
    out = local_part(
        v, lambda w, s: left[0, w, s], right, outer, inner, dims, place[0] * held, shift
    )
    for s in range(held):
        q[s] = out[s]
    put_edges(is_odd(place), out[0].astype(BF16), out[-1].astype(BF16), inside, across)
    dots[...] = dot_rows([v], v)


def ghosts(k, place, dims, v_before, inside, across, hops_inside, hops_across):
    odd = is_odd(place)
    if k == 0:
        return edges_from(odd, inside[0], across[0])
    low, high = edges_from(odd, inside[...], across[...])
    held = v_before.shape[0]
    first = place[0] * held
    last = dims.shape[1] - 1
    low_dim = dims[0, jnp.maximum(first - 1, 0)]
    high_dim = dims[0, jnp.minimum(first + held, last)]
    low_outer, high_outer = edges_from(odd, hops_inside[1], hops_across[1])
    low_inner, high_inner = edges_from(odd, hops_inside[2], hops_across[2])
    into_low = hop(v_before[0].astype(BF16), low_inner, low_outer)
    into_high = hop(v_before[held - 1].astype(BF16), high_inner, high_outer)
    low = (low.astype(F32) - TAU * masked(into_low, low_dim)).astype(BF16)
    high = (high.astype(F32) - TAU * masked(into_high, high_dim)).astype(BF16)
    return low, high


def step_kernel(k, keep, shift, names, *refs):
    r = dict(zip(names, refs))
    place, dims, q, outer, inner = (r[n] for n in ("place", "dims", "q", "outer", "inner"))
    held = q.shape[0]
    first = place[0] * held
    if "came_inside" in r:
        low, high = ghosts(
            k,
            place,
            dims,
            r.get("v_before"),
            r["came_inside"],
            r["came_across"],
            r.get("hops_inside"),
            r.get("hops_across"),
        )
    else:
        low, high = r["at_low"][...], r["at_high"][...]
    if keep:
        r["ghost_low"][...] = low
        r["ghost_high"][...] = high
    v = [q[s] for s in range(held)]
    v[0] = v[0] - TAU * masked(hop(low, inner[0, 0, 0], outer[0, 0, 0]), dims[0, first])
    v[-1] = v[-1] - TAU * masked(
        hop(high, inner[0, 1, held - 1], outer[0, 1, held - 1]), dims[0, first + held - 1]
    )
    for s in range(held):
        r["v"][s] = v[s]
    basis = [[r[f"v{i}"][s] for s in range(held)] for i in range(k + 1)]
    if k + 1 < ITERS:
        left = r["left"]
        env = (lambda w, s: left[0, w, s]) if len(left.shape) == 5 else (lambda w, s: left[w, s])
        out = local_part(v, env, r["right"], outer, inner, dims, first, shift)
        for s in range(held):
            r["q_next"][s] = out[s]
        put_edges(
            is_odd(place), out[0].astype(BF16), out[-1].astype(BF16), r["inside"], r["across"]
        )
        r["dots"][...] = dot_rows(basis + [v], v)
    else:
        lanes = lax.broadcasted_iota(jnp.int32, (ROWS, LANES), 1)
        rows = lax.broadcasted_iota(jnp.int32, (ROWS, LANES), 0)
        line = jnp.zeros((1, LANES), F32)
        for j in range(ITERS + 1):
            part = r[f"dots{j}"][...] if j < ITERS else dot_rows(basis + [v], v)
            part = jnp.sum(part, axis=1, keepdims=True)
            line = line + jnp.sum(
                jnp.where(lanes == ROWS * j + rows, part, 0.0), axis=0, keepdims=True
            )
        for n in range(r["line"].shape[0]):
            r["line"][n] = line


def combination(line, live_count, shift):
    lanes = lax.broadcasted_iota(jnp.int32, (1, LANES), 1)
    gram = {}
    for j in range(ITERS + 1):
        for i in range(j + 1):
            gram[i, j] = jnp.sum(
                jnp.where(lanes == ROWS * j + i, line, 0.0), axis=1, keepdims=True
            )
            gram[j, i] = gram[i, j]
    coefs = [jnp.ones((1, 1), F32)]
    energy = None
    for _ in range(ITERS):
        n = len(coefs)
        onto = [sum(coefs[i] * gram[i, j] for i in range(n)) for j in range(n + 1)]
        raised = [sum(coefs[i] * gram[i + 1, j] for i in range(n)) for j in range(1, n + 1)]
        self_dot = sum(coefs[j] * onto[j] for j in range(n))
        cross = sum(coefs[j] * onto[j + 1] for j in range(n))
        square = sum(coefs[j] * raised[j] for j in range(n))
        ratio = cross / self_dot
        gain = 1.0 - ratio
        energy = shift + gain / TAU
        norm = square + gain * (2.0 * cross + gain * self_dot)
        scale = jnp.sqrt(live_count / norm)
        moved = [gain * c for c in coefs] + [jnp.zeros((1, 1), F32)]
        moved = [moved[0]] + [moved[i + 1] + coefs[i] for i in range(n)]
        coefs = [scale * c for c in moved]
    return coefs, energy


def live_count_of(dims):
    total = jnp.int32(0)
    for s in range(dims.shape[1]):
        total = total + dims[0, s] * dims[0, s]
    return jnp.full((1, 1), total.astype(F32))


def join_kernel(shift, names, *refs):
    r = dict(zip(names, refs))
    place, dims = r["place"], r["dims"]
    line = jnp.sum(r["lines"][...], axis=0)
    coefs, _ = combination(line, live_count_of(dims), shift)
    held, cap, _ = r["v0"].shape
    for s in range(held):
        block = sum(c * r[f"v{k}"][s] for k, c in enumerate(coefs))
        r["x"][s] = block
        r["factor"][s, :cap] = block.astype(BF16)
        r["factor"][s, cap:] = jnp.full(
            (r["factor"].shape[1] - cap, cap), dims[0, place[0] * held + s].astype(F32)
        ).astype(BF16)
    low, high = ghosts(
        ITERS,
        place,
        dims,
        r[f"v{ITERS - 1}"],
        r["came_inside"],
        r["came_across"],
        r["hops_inside"],
        r["hops_across"],
    )
    for side, last in (("low", low), ("high", high)):
        blocks = [r[f"ghost_{side}{k}"][...] for k in range(ITERS)] + [last]
        total = sum(c * b.astype(F32) for c, b in zip(coefs, blocks))
        r[f"at_{side}"][...] = total.astype(BF16)


def grow_kernel(left, factor, out):
    held, cap = left.shape[2], left.shape[3]
    for s in range(held):
        block = factor[s, :cap]
        dim = factor[s, cap : cap + 1].astype(F32)
        for w in range(left.shape[1]):
            product = nn(block.T, nn(left[0, w, s], block).astype(BF16))
            out[0, w, s] = (product / dim).astype(BF16)


def second_kernel(
    shift, place, dims, x, left, earlier, factor, right, outer, inner, env, q, inside, across, dots
):
    held, cap, _ = x.shape

    @pl.when(place[1] == 0)
    def _():
        env[...] = left[0]

    @pl.when(place[1] != 0)
    def _():
        for s in range(held):
            block = factor[s, :cap]
            dim = factor[s, cap : cap + 1].astype(F32)
            for w in range(left.shape[1]):
                product = nn(block.T, nn(earlier[0, w, s], block).astype(BF16))
                env[w, s] = (product / dim).astype(BF16)

    v = [x[s] for s in range(held)]
    out = local_part(v, lambda w, s: env[w, s], right, outer, inner, dims, place[0] * held, shift)
    for s in range(held):
        q[s] = out[s]
    put_edges(is_odd(place), out[0].astype(BF16), out[-1].astype(BF16), inside, across)
    dots[...] = dot_rows([v], v)


def finish_kernel(shift, names, *refs):
    r = dict(zip(names, refs))
    line = jnp.sum(r["lines"][...], axis=0)
    coefs, energy = combination(line, live_count_of(r["dims"]), shift)
    for s in range(r["v0"].shape[0]):
        r["x"][0, s] = sum(c * r[f"v{k}"][s] for k, c in enumerate(coefs))
    r["energy"][0] = energy[0, 0]


def struct(shape, dtype):
    return jax.ShapeDtypeStruct(shape, dtype)


def call(kernel, name, outs, *args, flops=0, specs=None, grid=()):
    return pl.pallas_call(
        kernel,
        out_shape=tuple(outs),
        grid=grid,
        in_specs=specs or [SMEM if a.dtype == jnp.int32 else VMEM for a in args],
        out_specs=tuple(SMEM if o.shape == (1,) else VMEM for o in outs),
        name=name,
        compiler_params=pltpu.CompilerParams(vmem_limit_bytes=VMEM_LIMIT),
        cost_estimate=pl.CostEstimate(
            flops=flops,
            transcendentals=0,
            bytes_accessed=sum(a.size * a.dtype.itemsize for a in args),
        ),
    )(*args)


def named(kernel, name, ins, outs, flops=0):
    values = call(
        functools.partial(kernel, tuple(ins) + tuple(outs)),
        name,
        outs.values(),
        *ins.values(),
        flops=flops,
    )
    return dict(zip(outs, values))


def body(psi, left_env, right_env, hop_outer, hop_inner, dims):
    _, terms, held, cap, _ = left_env.shape
    shift = float(terms)
    size = lax.axis_size("sec")
    place = jnp.stack([lax.axis_index("sec"), lax.axis_index("seg")]).astype(jnp.int32)
    block = struct((cap, cap), BF16)
    blocks = struct((held, cap, cap), F32)
    triple = struct((3, cap, cap), BF16)
    dots_of = struct((ROWS, LANES), F32)
    pairs = [(i, i ^ 1) for i in range(size)]
    others = [(i, i + 1 if i % 2 else i - 1) for i in range(1, size - 1)]
    onward = [(i, i + 1) for i in range(lax.axis_size("seg") - 1)]
    one = 2 * cap**3

    def exchange(inside, across):
        return lax.ppermute(inside, "sec", pairs), lax.ppermute(across, "sec", others)

    def relaxed(v0, q, sent, first, dots, env, hops, keep):
        basis = {"v0": v0}
        all_dots = {"dots0": dots}
        kept = {}
        before = first
        for k in range(ITERS):
            came = exchange(*sent)
            ins = {"place": place, "dims": dims, "q": q, "outer": hop_outer, "inner": hop_inner}
            ins.update(basis)
            ins.update(before)
            if k > 0:
                ins.update(v_before=basis[f"v{k - 1}"], hops_inside=hops[0], hops_across=hops[1])
            outs = {"v": blocks}
            if keep:
                outs.update(ghost_low=block, ghost_high=block)
            if k + 1 < ITERS:
                ins.update(left=env, right=right_env)
                outs.update(q_next=blocks, inside=block, across=block, dots=dots_of)
            else:
                ins.update(all_dots)
                outs.update(line=struct((size, 1, LANES), F32))
            got = named(
                functools.partial(step_kernel, k, keep, shift),
                f"step{k}",
                ins,
                outs,
                flops=one * 36,
            )
            basis[f"v{k + 1}"] = got["v"]
            if keep:
                kept[f"ghost_low{k}"], kept[f"ghost_high{k}"] = got["ghost_low"], got["ghost_high"]
            before = {"came_inside": came[0], "came_across": came[1]}
            if k + 1 < ITERS:
                q, sent = got["q_next"], (got["inside"], got["across"])
                all_dots[f"dots{k + 1}"] = got["dots"]
        lines = lax.all_to_all(got["line"], "sec", 0, 0)
        return basis, kept, lines, before

    def block_at(side, sector):
        return pl.BlockSpec((1, 1, 1, cap, cap), lambda n: (0, side, sector, 0, 0))

    v0, inside, across = call(
        start_kernel,
        "start",
        (blocks, triple, triple),
        place,
        dims,
        psi,
        hop_outer,
        hop_inner,
        hop_outer,
        hop_inner,
        specs=[SMEM, SMEM, VMEM] + 2 * [block_at(0, 0)] + 2 * [block_at(1, held - 1)],
        grid=(1,),
    )
    hops = exchange(inside, across)
    earlier = lax.ppermute(left_env, "seg", onward)
    q, inside, across, dots = call(
        functools.partial(local_kernel, shift),
        "local",
        (blocks, block, block, dots_of),
        place,
        dims,
        v0,
        left_env,
        right_env,
        hop_outer,
        hop_inner,
        flops=one * 28,
    )
    first = {"came_inside": hops[0], "came_across": hops[1]}
    basis, kept, lines, last = relaxed(
        v0, q, (inside, across), first, dots, left_env, hops, True
    )
    ins = {"place": place, "dims": dims, "lines": lines}
    ins.update(basis)
    ins.update(kept)
    ins.update(last)
    ins.update(hops_inside=hops[0], hops_across=hops[1])
    outs = {
        "x": blocks,
        "factor": struct((held, cap + 16, cap), BF16),
        "at_low": block,
        "at_high": block,
    }
    got = named(functools.partial(join_kernel, shift), "join", ins, outs, flops=one * 4)
    x, factor = got["x"], got["factor"]
    earlier_factor = lax.ppermute(factor, "seg", onward)
    (renewed,) = call(
        grow_kernel, "grow", (struct(left_env.shape, BF16),), left_env, factor, flops=one * 24
    )
    env, q, inside, across, dots = call(
        functools.partial(second_kernel, shift),
        "second",
        (struct((terms, held, cap, cap), BF16), blocks, block, block, dots_of),
        place,
        dims,
        x,
        left_env,
        earlier,
        earlier_factor,
        right_env,
        hop_outer,
        hop_inner,
        flops=one * 52,
    )
    first = {"at_low": got["at_low"], "at_high": got["at_high"]}
    basis, _, lines, _ = relaxed(x, q, (inside, across), first, dots, env, hops, False)
    ins = {"dims": dims, "lines": lines}
    ins.update(basis)
    outs = {"x": struct(psi.shape, F32), "energy": struct((1,), F32)}
    got = named(functools.partial(finish_kernel, shift), "finish", ins, outs)
    return (got["x"], got["energy"], renewed)


def solution(mesh):
    return jax.shard_map(
        body,
        mesh=mesh,
        in_specs=(
            P("seg", "sec", None, None),
            P("seg", None, "sec", None, None),
            P("seg", None, "sec", None, None),
            P("seg", None, "sec", None, None),
            P("seg", None, "sec", None, None),
            P("seg", None),
        ),
        out_specs=(P("seg", "sec", None, None), P("seg"), P("seg", None, "sec", None, None)),
        check_vma=False,
    )
```

time: 802 us -> 119 us (0.15)
  blocking collectives: 597 us -> 15.8 us
  matrix products: 68 us -> 0 us
  Pallas kernels: 0 us -> 33.3 us
  other arithmetic: 24.8 us -> 0.08 us
  waiting for transfers between devices: 36.8 us -> 13.8 us
  between operations: 23.8 us -> 1.19 us
  starting transfers between devices: 36 us -> 45.8 us
    psum x16 -> x0, blocking collectives: 597 us -> none  [the longest x8 303 us: relax(): step_norm = lax.psum(jnp.sum(step * step), 'sec')]
    dot_general x25 -> x0, matrix products: 68 us -> none  [the longest x8 29 us: apply_operator(): jnp.einsum('wsik,wskj->sij', env_left, halfway, preferred_element_type=jn...]
    pallas_call x0 -> x14, Pallas kernels: none -> 33.3 us  [call(): pl.pallas_call(kernel, out_shape=tuple(outs), grid=grid, in_specs=specs o...]
    ppermute x17 -> x18, waiting for transfers between devices: 36.8 us -> 8.56 us  [the longest x1 6.97 us: body(): earlier_factor = lax.ppermute(factor, 'seg', onward)]
    reduce_sum x9 -> x0, other arithmetic: 17 us -> none  [the longest x8 16.3 us: relax(): step_norm = lax.psum(jnp.sum(step * step), 'sec')]
    all_to_all x0 -> x1, blocking collectives: none -> 15.8 us  [relaxed(): lines = lax.all_to_all(got['line'], 'sec', 0, 0)]
    all_to_all x0 -> x1, starting transfers between devices: none -> 8.8 us  [relaxed(): lines = lax.all_to_all(got['line'], 'sec', 0, 0)]
    ppermute x17 -> x18, starting transfers between devices: 36 us -> 37 us  [the longest x8 27.6 us: exchange(): lax.ppermute(inside, 'sec', pairs)]
  transfers between devices with their start and end apart: 17 -> 19, of which waited for: 12 -> 3; matrix products, arithmetic and copies ran while one was open for 5% -> 0% of each run, Pallas kernels for 0% -> 21%
where the time goes in v2:
time: 119 us; the launch traced here: 118 us
  starting transfers between devices  45.8 us (38%)
  Pallas kernels  33.3 us (28%)
  blocking collectives  15.8 us (13%)
  waiting for transfers between devices  13.8 us (12%)
  local copies, waits for them, and re-layouts  8.11 us (7%)
  between operations  1.19 us (1%)
    pallas_call x14, Pallas kernels, call(): pl.pallas_call(kernel, out_shape=tuple(outs), grid=grid, in_specs=specs o...  33.3 us
    ppermute x8, starting transfers between devices, exchange(): lax.ppermute(inside, 'sec', pairs)  27.6 us
    all_to_all x1, blocking collectives, relaxed(): lines = lax.all_to_all(got['line'], 'sec', 0, 0)  15.8 us
    all_to_all x1, starting transfers between devices, relaxed(): lines = lax.all_to_all(got['line'], 'sec', 0, 0)  8.8 us
    unnamed x40, local copies, waits for them, and re-layouts  8.11 us
    ppermute x1, waiting for transfers between devices, body(): earlier_factor = lax.ppermute(factor, 'seg', onward)  6.97 us
    ppermute x8, starting transfers between devices, exchange(): lax.ppermute(across, 'sec', others)  5.27 us
    all_to_all x1, waiting for transfers between devices, relaxed(): lines = lax.all_to_all(got['line'], 'sec', 0, 0)  5.24 us
  transfers between devices with their start and end apart: 19, of which 3 were waited for; matrix products, arithmetic and copies ran while one was open for 0% of the time, Pallas kernels for 21%

profile of v2, /device:TPU:128, one launch (start us, length us, event | category | flops | bytes accessed | tf_op | source)
XLA Modules:
  0.0 118.1 jit_solution(6729306944340522691)
XLA Ops:
  0.6 2.1 %collective-permute-start.10 = (bf16[1,6,2,256,256]{4,3,2,1,0:T(8,128)(2,1)}, bf16[1,6,2,256,256]{4,3,2,1,0:T(8,128)(2,1)}, u32[]{:S(2)}, u32[]{:S(2)}) collective-permute-start(bf16[1,6,2,256,256]{4,3,2,1,0:T(8,128)(2,1)} %left.5), channel_id=1, source_target_pairs={{0,16},{16,32},{32,48},{48,64},{64,80},{80,96},{96,112},{112,128},... | collective-permute-start | bytes 4718600 | tf_op jit(solution)/shard_map/ppermute | solution.py:399
  11.0 2.0 %local.1 = (f32[2,256,256]{2,1,0:T(8,128)S(1)}, bf16[256,256]{1,0:T(8,128)(2,1)S(1)}, bf16[256,256]{1,0:T(8,128)(2,1)S(1)}, f32[8,128]{1,0:T(8,128)S(1)}) custom-call(s32[2]{0:T(128)S(1)} %pad_add_fusion.place.refs_0_, s32[1,32]{1,0:T(1,128)S(1)} %copy-done.18, f32[2,256,256]{2,1,0:T(8,128)S(1)} %get-tuple-element.61.v0.refs_5_.refs_9_.refs_3_, ...), custom_call_target="tpu_custom_call" | custom-call | flops 939524096 | bytes 4718728 | tf_op jit(solution)/shard_map/local/pallas_call | solution.py:299
  13.0 4.0 %collective-permute-start.2 = (bf16[256,256]{1,0:T(8,128)(2,1)S(1)}, bf16[256,256]{1,0:T(8,128)(2,1)S(1)}, u32[]{:S(2)}, u32[]{:S(2)}) collective-permute-start(bf16[256,256]{1,0:T(8,128)(2,1)S(1)} %get-tuple-element.67), channel_id=1, source_target_pairs={{0,1},{1,0},{2,3},{3,2},{4,5},{5,4},{6,7},{7,6},{8,9},{9,8},{10,11... | collective-permute-start | bytes 393224 | tf_op jit(solution)/shard_map/ppermute | solution.py:341
  19.2 2.4 %step0.2 = (f32[2,256,256]{2,1,0:T(8,128)S(1)}, bf16[256,256]{1,0:T(8,128)(2,1)S(1)}, bf16[256,256]{1,0:T(8,128)(2,1)S(1)}, f32[2,256,256]{2,1,0:T(8,128)S(1)}, ...) custom-call(s32[2]{0:T(128)S(1)} %pad_add_fusion.place.refs_0_, ...), custom_call_target="tpu_custom_call" | custom-call | flops 1207959552 | bytes 6029448 | tf_op jit(solution)/shard_map/step0/pallas_call | solution.py:299
  21.6 4.1 %collective-permute-start.4 = (bf16[256,256]{1,0:T(8,128)(2,1)S(1)}, bf16[256,256]{1,0:T(8,128)(2,1)S(1)}, u32[]{:S(2)}, u32[]{:S(2)}) collective-permute-start(bf16[256,256]{1,0:T(8,128)(2,1)S(1)} %get-tuple-element.71), channel_id=1, source_target_pairs={{0,1},{1,0},{2,3},{3,2},{4,5},{5,4},{6,7},{7,6},{8,9},{9,8},{10,11... | collective-permute-start | bytes 393224 | tf_op jit(solution)/shard_map/ppermute | solution.py:341
  26.4 2.8 %step1.2 = (f32[2,256,256]{2,1,0:T(8,128)S(1)}, bf16[256,256]{1,0:T(8,128)(2,1)S(1)}, bf16[256,256]{1,0:T(8,128)(2,1)S(1)}, f32[2,256,256]{2,1,0:T(8,128)S(1)}, ...) custom-call(s32[2]{0:T(128)S(1)} %pad_add_fusion.place.refs_0_, ...), custom_call_target="tpu_custom_call" | custom-call | flops 1207959552 | bytes 7340168 | tf_op jit(solution)/shard_map/step1/pallas_call | solution.py:299
  29.1 6.4 %collective-permute-start.6 = (bf16[256,256]{1,0:T(8,128)(2,1)S(1)}, bf16[256,256]{1,0:T(8,128)(2,1)S(1)}, u32[]{:S(2)}, u32[]{:S(2)}) collective-permute-start(bf16[256,256]{1,0:T(8,128)(2,1)S(1)} %get-tuple-element.75), channel_id=1, source_target_pairs={{0,1},{1,0},{2,3},{3,2},{4,5},{5,4},{6,7},{7,6},{8,9},{9,8},{10,11... | collective-permute-start | bytes 393224 | tf_op jit(solution)/shard_map/ppermute | solution.py:341
  36.3 2.8 %step2.2 = (f32[2,256,256]{2,1,0:T(8,128)S(1)}, bf16[256,256]{1,0:T(8,128)(2,1)S(1)}, bf16[256,256]{1,0:T(8,128)(2,1)S(1)}, f32[2,256,256]{2,1,0:T(8,128)S(1)}, ...) custom-call(s32[2]{0:T(128)S(1)} %pad_add_fusion.place.refs_0_, ...), custom_call_target="tpu_custom_call" | custom-call | flops 1207959552 | bytes 7864456 | tf_op jit(solution)/shard_map/step2/pallas_call | solution.py:299
  39.1 3.5 %collective-permute-start.8 = (bf16[256,256]{1,0:T(8,128)(2,1)S(1)}, bf16[256,256]{1,0:T(8,128)(2,1)S(1)}, u32[]{:S(2)}, u32[]{:S(2)}) collective-permute-start(bf16[256,256]{1,0:T(8,128)(2,1)S(1)} %get-tuple-element.91), channel_id=1, source_target_pairs={{0,1},{1,0},{2,3},{3,2},{4,5},{5,4},{6,7},{7,6},{8,9},{9,8},{10,11... | collective-permute-start | bytes 393224 | tf_op jit(solution)/shard_map/ppermute | solution.py:341
  43.2 1.8 %step3.2 = (f32[2,256,256]{2,1,0:T(8,128)S(1)}, bf16[256,256]{1,0:T(8,128)(2,1)S(1)}, bf16[256,256]{1,0:T(8,128)(2,1)S(1)}, f32[16,1,128]{2,1,0:T(1,128)S(1)}) custom-call(s32[2]{0:T(128)S(1)} %pad_add_fusion.place.refs_0_, s32[1,32]{1,0:T(1,128)S(1)} %copy-done.18, f32[2,256,256]{2,1,0:T(8,128)S(1)} %get-tuple-element.73.refs_2_, ...), custom_call_target="tpu_custom_call" | custom-call | flops 1207959552 | bytes 5259400 | tf_op jit(solution)/shard_map/step3/pallas_call | solution.py:299
  45.0 15.8 %all_to_all.10.refs_2_ = f32[16,1,128]{2,1,0:T(1,128)S(1)} all-to-all(f32[16,1,128]{2,1,0:T(1,128)S(1)} %get-tuple-element.81), channel_id=1, replica_groups=mesh['seg'=16,'sec'=16] {'sec'}, dimensions={0} | all-to-all | bytes 16384 | tf_op jit(solution)/shard_map/all_to_all | solution.py:378
  62.5 2.1 %collective-permute-start.11 = (bf16[2,272,256]{2,1,0:T(8,128)(2,1)S(1)}, bf16[2,272,256]{2,1,0:T(8,128)(2,1)S(1)}, u32[]{:S(2)}, u32[]{:S(2)}) collective-permute-start(bf16[2,272,256]{2,1,0:T(8,128)(2,1)S(1)} %get-tuple-element.94.factor), channel_id=1, source_target_pairs={{0,16},{16,32},{32,48},{48,64},{64,80},{80,96},{96,112},{112,128},... | collective-permute-start | bytes 835592 | tf_op jit(solution)/shard_map/ppermute | solution.py:430
  64.6 7.0 %collective-permute-done.11.factor = bf16[2,272,256]{2,1,0:T(8,128)(2,1)S(1)} collective-permute-done((bf16[2,272,256]{2,1,0:T(8,128)(2,1)S(1)}, bf16[2,272,256]{2,1,0:T(8,128)(2,1)S(1)}, u32[]{:S(2)}, u32[]{:S(2)}) %collective-permute-start.11) | collective-permute-done | bytes 278560 | tf_op jit(solution)/shard_map/ppermute | solution.py:430
  71.6 4.0 %second.1 = (bf16[6,2,256,256]{3,2,1,0:T(8,128)(2,1)S(1)}, f32[2,256,256]{2,1,0:T(8,128)S(1)}, bf16[256,256]{1,0:T(8,128)(2,1)S(1)}, bf16[256,256]{1,0:T(8,128)(2,1)S(1)}, f32[8,128]{1,0:T(8,128)S(1)}) custom-call(s32[2]{0:T(128)S(1)} %pad_add_fusion.place.refs_0_, s32[1,32]{1,0:T(1,128)S(1)} %copy-done.18, ...), custom_call_target="tpu_custom_call" | custom-call | flops 1744830464 | bytes 6570120 | tf_op jit(solution)/shard_map/second/pallas_call | solution.py:299
  76.9 2.4 %step0.3 = (f32[2,256,256]{2,1,0:T(8,128)S(1)}, f32[2,256,256]{2,1,0:T(8,128)S(1)}, bf16[256,256]{1,0:T(8,128)(2,1)S(1)}, bf16[256,256]{1,0:T(8,128)(2,1)S(1)}, f32[8,128]{1,0:T(8,128)S(1)}) custom-call(s32[2]{0:T(128)S(1)} %pad_add_fusion.place.refs_0_, s32[1,32]{1,0:T(1,128)S(1)} %copy-done.18, f32[2,256,256]{2,1,0:T(8,128)S(1)} %get-tuple-element.95.refs_2_, ...), custom_call_target="tpu_custom_call" | custom-call | flops 1207959552 | bytes 5505160 | tf_op jit(solution)/shard_map/step0/pallas_call | solution.py:299
  79.3 3.4 %collective-permute-start.14 = (bf16[256,256]{1,0:T(8,128)(2,1)S(1)}, bf16[256,256]{1,0:T(8,128)(2,1)S(1)}, u32[]{:S(2)}, u32[]{:S(2)}) collective-permute-start(bf16[256,256]{1,0:T(8,128)(2,1)S(1)} %get-tuple-element.105), channel_id=1, source_target_pairs={{0,1},{1,0},{2,3},{3,2},{4,5},{5,4},{6,7},{7,6},{8,9},{9,8},{10,11... | collective-permute-start | bytes 393224 | tf_op jit(solution)/shard_map/ppermute | solution.py:341
  83.4 2.8 %step1.3 = (f32[2,256,256]{2,1,0:T(8,128)S(1)}, f32[2,256,256]{2,1,0:T(8,128)S(1)}, bf16[256,256]{1,0:T(8,128)(2,1)S(1)}, bf16[256,256]{1,0:T(8,128)(2,1)S(1)}, f32[8,128]{1,0:T(8,128)S(1)}) custom-call(s32[2]{0:T(128)S(1)} %pad_add_fusion.place.refs_0_, s32[1,32]{1,0:T(1,128)S(1)} %copy-done.18, f32[2,256,256]{2,1,0:T(8,128)S(1)} %get-tuple-element.99.refs_2_, ...), custom_call_target="tpu_custom_call" | custom-call | flops 1207959552 | bytes 7340168 | tf_op jit(solution)/shard_map/step1/pallas_call | solution.py:299
  86.2 4.0 %collective-permute-start.16 = (bf16[256,256]{1,0:T(8,128)(2,1)S(1)}, bf16[256,256]{1,0:T(8,128)(2,1)S(1)}, u32[]{:S(2)}, u32[]{:S(2)}) collective-permute-start(bf16[256,256]{1,0:T(8,128)(2,1)S(1)} %get-tuple-element.109), channel_id=1, source_target_pairs={{0,1},{1,0},{2,3},{3,2},{4,5},{5,4},{6,7},{7,6},{8,9},{9,8},{10,11... | collective-permute-start | bytes 393224 | tf_op jit(solution)/shard_map/ppermute | solution.py:341
  90.8 3.5 %step2.3 = (f32[2,256,256]{2,1,0:T(8,128)S(1)}, f32[2,256,256]{2,1,0:T(8,128)S(1)}, bf16[256,256]{1,0:T(8,128)(2,1)}, bf16[256,256]{1,0:T(8,128)(2,1)}, f32[8,128]{1,0:T(8,128)S(1)}) custom-call(s32[2]{0:T(128)S(1)} %pad_add_fusion.place.refs_0_, s32[1,32]{1,0:T(1,128)S(1)} %copy-done.18, f32[2,256,256]{2,1,0:T(8,128)S(1)} %get-tuple-element.103.refs_2_, ...), custom_call_target="tpu_custom_call" | custom-call | flops 1207959552 | bytes 7864456 | tf_op jit(solution)/shard_map/step2/pallas_call | solution.py:299
  94.4 2.4 %step3.3 = (f32[2,256,256]{2,1,0:T(8,128)S(1)}, f32[16,1,128]{2,1,0:T(1,128)}) custom-call(s32[2]{0:T(128)S(1)} %pad_add_fusion.place.refs_0_, s32[1,32]{1,0:T(1,128)S(1)} %copy-done.18, f32[2,256,256]{2,1,0:T(8,128)S(1)} %get-tuple-element.107.refs_2_, bf16[1,2,2,256,256]{4,3,2,1,0:T(8,128)(2,1)S(1)} %copy-done.2, ...), custom_call_target="tpu_custom_call" | custom-call | flops 1207959552 | bytes 5259400 | tf_op jit(solution)/shard_map/step3/pallas_call | solution.py:299
  97.5 8.8 %all-to-all-start.1 = ((f32[16,1,128]{2,1,0:T(1,128)}), f32[16,1,128]{2,1,0:T(1,128)S(1)}, u32[]{:S(2)}, u32[]{:S(2)}) async-start(f32[16,1,128]{2,1,0:T(1,128)} %get-tuple-element.115), calls=%async_computation.1 | async-start | bytes 16384 | tf_op jit(solution)/shard_map/all_to_all | solution.py:378
  106.4 2.3 %grow.1 = bf16[1,6,2,256,256]{4,3,2,1,0:T(8,128)(2,1)} custom-call(bf16[1,6,2,256,256]{4,3,2,1,0:T(8,128)(2,1)S(1)} %copy-done.6, bf16[2,272,256]{2,1,0:T(8,128)(2,1)S(1)} %get-tuple-element.94.factor), custom_call_target="tpu_custom_call" | custom-call | flops 805306368 | bytes 1851392 | tf_op jit(solution)/shard_map/grow/pallas_call | solution.py:299
  108.7 5.2 %all-to-all-done.1.refs_1_ = f32[16,1,128]{2,1,0:T(1,128)S(1)} async-done(((f32[16,1,128]{2,1,0:T(1,128)}), f32[16,1,128]{2,1,0:T(1,128)S(1)}, u32[]{:S(2)}, u32[]{:S(2)}) %all-to-all-start.1) | async-done | bytes 8224 | tf_op jit(solution)/shard_map/all_to_all | solution.py:378
  116.0 1.9 %finish.1 = (f32[1,2,256,256]{3,2,1,0:T(8,128)}, f32[1]{0:T(128)}) custom-call(s32[1,32]{1,0:T(1,128)S(1)} %copy-done.19, f32[16,1,128]{2,1,0:T(1,128)S(1)} %all-to-all-done.1.refs_1_, f32[2,256,256]{2,1,0:T(8,128)S(1)} %copy-done.8, f32[2,256,256]{2,1,0:T(8,128)S(1)} %copy-done.10, f32[2,256,256]{2,1,0:T(8,128)S(1)} %copy-done.12, ...), custom_call_target="tpu_custom_call" | custom-call | bytes 2629760 | tf_op jit(solution)/shard_map/finish/pallas_call | solution.py:299
  (70 shorter events, 19.6 us)
Async XLA Ops:
  0.6 8.9 %copy-start = (bf16[1,6,2,256,256]{4,3,2,1,0:T(8,128)(2,1)S(1)}, bf16[1,6,2,256,256]{4,3,2,1,0:T(8,128)(2,1)}, u32[]{:S(2)}) copy-start(bf16[1,6,2,256,256]{4,3,2,1,0:T(8,128)(2,1)} %refs_14_.3) | copy-start | bytes 4718596
  0.6 70.9 %collective-permute-start.10 = (bf16[1,6,2,256,256]{4,3,2,1,0:T(8,128)(2,1)}, bf16[1,6,2,256,256]{4,3,2,1,0:T(8,128)(2,1)}, u32[]{:S(2)}, u32[]{:S(2)}) collective-permute-start(bf16[1,6,2,256,256]{4,3,2,1,0:T(8,128)(2,1)} %left.5), channel_id=1, source_target_pairs={{0,16},{16,32},{32,48},{48,64},{64,80},{80,96},{96,112},{112,128},... | collective-permute-start | bytes 4718600 | tf_op jit(solution)/shard_map/ppermute | solution.py:399
  7.2 11.9 %collective-permute-start = (bf16[3,256,256]{2,1,0:T(8,128)(2,1)S(1)}, bf16[3,256,256]{2,1,0:T(8,128)(2,1)S(1)}, u32[]{:S(2)}, u32[]{:S(2)}) collective-permute-start(bf16[3,256,256]{2,1,0:T(8,128)(2,1)S(1)} %get-tuple-element.63), channel_id=1, source_target_pairs={{0,1},{1,0},{2,3},{3,2},{4,5},{5,4},{6,7},{7,6},{8,9},{9,8},{10,11... | collective-permute-start | bytes 1179656 | tf_op jit(solution)/shard_map/ppermute | solution.py:341
  8.8 10.3 %collective-permute-start.1 = (bf16[3,256,256]{2,1,0:T(8,128)(2,1)S(1)}, bf16[3,256,256]{2,1,0:T(8,128)(2,1)S(1)}, u32[]{:S(2)}, u32[]{:S(2)}) collective-permute-start(bf16[3,256,256]{2,1,0:T(8,128)(2,1)S(1)} %get-tuple-element.64), channel_id=1, source_target_pairs={{1,2},{2,1},{3,4},{4,3},{5,6},{6,5},{7,8},{8,7},{9,10},{10,9},{11,... | collective-permute-start | bytes 1179656 | tf_op jit(solution)/shard_map/ppermute | solution.py:341
  13.0 13.4 %collective-permute-start.2 = (bf16[256,256]{1,0:T(8,128)(2,1)S(1)}, bf16[256,256]{1,0:T(8,128)(2,1)S(1)}, u32[]{:S(2)}, u32[]{:S(2)}) collective-permute-start(bf16[256,256]{1,0:T(8,128)(2,1)S(1)} %get-tuple-element.67), channel_id=1, source_target_pairs={{0,1},{1,0},{2,3},{3,2},{4,5},{5,4},{6,7},{7,6},{8,9},{9,8},{10,11... | collective-permute-start | bytes 393224 | tf_op jit(solution)/shard_map/ppermute | solution.py:341
  17.0 9.4 %collective-permute-start.3 = (bf16[256,256]{1,0:T(8,128)(2,1)S(1)}, bf16[256,256]{1,0:T(8,128)(2,1)S(1)}, u32[]{:S(2)}, u32[]{:S(2)}) collective-permute-start(bf16[256,256]{1,0:T(8,128)(2,1)S(1)} %get-tuple-element.68), channel_id=1, source_target_pairs={{1,2},{2,1},{3,4},{4,3},{5,6},{6,5},{7,8},{8,7},{9,10},{10,9},{11,... | collective-permute-start | bytes 393224 | tf_op jit(solution)/shard_map/ppermute | solution.py:341
  21.6 14.7 %collective-permute-start.4 = (bf16[256,256]{1,0:T(8,128)(2,1)S(1)}, bf16[256,256]{1,0:T(8,128)(2,1)S(1)}, u32[]{:S(2)}, u32[]{:S(2)}) collective-permute-start(bf16[256,256]{1,0:T(8,128)(2,1)S(1)} %get-tuple-element.71), channel_id=1, source_target_pairs={{0,1},{1,0},{2,3},{3,2},{4,5},{5,4},{6,7},{7,6},{8,9},{9,8},{10,11... | collective-permute-start | bytes 393224 | tf_op jit(solution)/shard_map/ppermute | solution.py:341
  25.7 10.6 %collective-permute-start.5 = (bf16[256,256]{1,0:T(8,128)(2,1)S(1)}, bf16[256,256]{1,0:T(8,128)(2,1)S(1)}, u32[]{:S(2)}, u32[]{:S(2)}) collective-permute-start(bf16[256,256]{1,0:T(8,128)(2,1)S(1)} %get-tuple-element.72), channel_id=1, source_target_pairs={{1,2},{2,1},{3,4},{4,3},{5,6},{6,5},{7,8},{8,7},{9,10},{10,9},{11,... | collective-permute-start | bytes 393224 | tf_op jit(solution)/shard_map/ppermute | solution.py:341
  29.1 14.1 %collective-permute-start.6 = (bf16[256,256]{1,0:T(8,128)(2,1)S(1)}, bf16[256,256]{1,0:T(8,128)(2,1)S(1)}, u32[]{:S(2)}, u32[]{:S(2)}) collective-permute-start(bf16[256,256]{1,0:T(8,128)(2,1)S(1)} %get-tuple-element.75), channel_id=1, source_target_pairs={{0,1},{1,0},{2,3},{3,2},{4,5},{5,4},{6,7},{7,6},{8,9},{9,8},{10,11... | collective-permute-start | bytes 393224 | tf_op jit(solution)/shard_map/ppermute | solution.py:341
  35.6 7.7 %collective-permute-start.7 = (bf16[256,256]{1,0:T(8,128)(2,1)S(1)}, bf16[256,256]{1,0:T(8,128)(2,1)S(1)}, u32[]{:S(2)}, u32[]{:S(2)}) collective-permute-start(bf16[256,256]{1,0:T(8,128)(2,1)S(1)} %get-tuple-element.76), channel_id=1, source_target_pairs={{1,2},{2,1},{3,4},{4,3},{5,6},{6,5},{7,8},{8,7},{9,10},{10,9},{11,... | collective-permute-start | bytes 393224 | tf_op jit(solution)/shard_map/ppermute | solution.py:341
  39.1 21.7 %collective-permute-start.8 = (bf16[256,256]{1,0:T(8,128)(2,1)S(1)}, bf16[256,256]{1,0:T(8,128)(2,1)S(1)}, u32[]{:S(2)}, u32[]{:S(2)}) collective-permute-start(bf16[256,256]{1,0:T(8,128)(2,1)S(1)} %get-tuple-element.91), channel_id=1, source_target_pairs={{0,1},{1,0},{2,3},{3,2},{4,5},{5,4},{6,7},{7,6},{8,9},{9,8},{10,11... | collective-permute-start | bytes 393224 | tf_op jit(solution)/shard_map/ppermute | solution.py:341
  42.6 18.2 %collective-permute-start.9 = (bf16[256,256]{1,0:T(8,128)(2,1)S(1)}, bf16[256,256]{1,0:T(8,128)(2,1)S(1)}, u32[]{:S(2)}, u32[]{:S(2)}) collective-permute-start(bf16[256,256]{1,0:T(8,128)(2,1)S(1)} %get-tuple-element.92), channel_id=1, source_target_pairs={{1,2},{2,1},{3,4},{4,3},{5,6},{6,5},{7,8},{8,7},{9,10},{10,9},{11,... | collective-permute-start | bytes 393224 | tf_op jit(solution)/shard_map/ppermute | solution.py:341
  60.8 10.8 %copy-start.6 = (bf16[1,6,2,256,256]{4,3,2,1,0:T(8,128)(2,1)S(1)}, bf16[1,6,2,256,256]{4,3,2,1,0:T(8,128)(2,1)}, u32[]{:S(2)}) copy-start(bf16[1,6,2,256,256]{4,3,2,1,0:T(8,128)(2,1)} %left.5) | copy-start | bytes 4718596
  62.5 31.9 %copy-start.7 = (f32[2,256,256]{2,1,0:T(8,128)}, f32[2,256,256]{2,1,0:T(8,128)S(1)}, u32[]{:S(2)}) copy-start(f32[2,256,256]{2,1,0:T(8,128)S(1)} %get-tuple-element.93.x.refs_5_.refs_9_.refs_2_) | copy-start | bytes 1572868
  62.5 9.1 %collective-permute-start.11 = (bf16[2,272,256]{2,1,0:T(8,128)(2,1)S(1)}, bf16[2,272,256]{2,1,0:T(8,128)(2,1)S(1)}, u32[]{:S(2)}, u32[]{:S(2)}) collective-permute-start(bf16[2,272,256]{2,1,0:T(8,128)(2,1)S(1)} %get-tuple-element.94.factor), channel_id=1, source_target_pairs={{0,16},{16,32},{32,48},{48,64},{64,80},{80,96},{96,112},{112,128},... | collective-permute-start | bytes 835592 | tf_op jit(solution)/shard_map/ppermute | solution.py:430
  75.6 7.7 %collective-permute-start.12 = (bf16[256,256]{1,0:T(8,128)(2,1)S(1)}, bf16[256,256]{1,0:T(8,128)(2,1)S(1)}, u32[]{:S(2)}, u32[]{:S(2)}) collective-permute-start(bf16[256,256]{1,0:T(8,128)(2,1)S(1)} %get-tuple-element.101), channel_id=1, source_target_pairs={{0,1},{1,0},{2,3},{3,2},{4,5},{5,4},{6,7},{7,6},{8,9},{9,8},{10,11... | collective-permute-start | bytes 393224 | tf_op jit(solution)/shard_map/ppermute | solution.py:341
  76.3 7.1 %collective-permute-start.13 = (bf16[256,256]{1,0:T(8,128)(2,1)S(1)}, bf16[256,256]{1,0:T(8,128)(2,1)S(1)}, u32[]{:S(2)}, u32[]{:S(2)}) collective-permute-start(bf16[256,256]{1,0:T(8,128)(2,1)S(1)} %get-tuple-element.102), channel_id=1, source_target_pairs={{1,2},{2,1},{3,4},{4,3},{5,6},{6,5},{7,8},{8,7},{9,10},{10,9},{11,... | collective-permute-start | bytes 393224 | tf_op jit(solution)/shard_map/ppermute | solution.py:341
  79.3 15.0 %copy-start.9 = (f32[2,256,256]{2,1,0:T(8,128)}, f32[2,256,256]{2,1,0:T(8,128)S(1)}, u32[]{:S(2)}) copy-start(f32[2,256,256]{2,1,0:T(8,128)S(1)} %get-tuple-element.100.refs_6_.refs_10_.refs_3_) | copy-start | bytes 1572868
  79.3 11.5 %collective-permute-start.14 = (bf16[256,256]{1,0:T(8,128)(2,1)S(1)}, bf16[256,256]{1,0:T(8,128)(2,1)S(1)}, u32[]{:S(2)}, u32[]{:S(2)}) collective-permute-start(bf16[256,256]{1,0:T(8,128)(2,1)S(1)} %get-tuple-element.105), channel_id=1, source_target_pairs={{0,1},{1,0},{2,3},{3,2},{4,5},{5,4},{6,7},{7,6},{8,9},{9,8},{10,11... | collective-permute-start | bytes 393224 | tf_op jit(solution)/shard_map/ppermute | solution.py:341
  82.7 8.1 %collective-permute-start.15 = (bf16[256,256]{1,0:T(8,128)(2,1)S(1)}, bf16[256,256]{1,0:T(8,128)(2,1)S(1)}, u32[]{:S(2)}, u32[]{:S(2)}) collective-permute-start(bf16[256,256]{1,0:T(8,128)(2,1)S(1)} %get-tuple-element.106), channel_id=1, source_target_pairs={{1,2},{2,1},{3,4},{4,3},{5,6},{6,5},{7,8},{8,7},{9,10},{10,9},{11,... | collective-permute-start | bytes 393224 | tf_op jit(solution)/shard_map/ppermute | solution.py:341
  86.2 8.2 %copy-start.11 = (f32[2,256,256]{2,1,0:T(8,128)}, f32[2,256,256]{2,1,0:T(8,128)S(1)}, u32[]{:S(2)}) copy-start(f32[2,256,256]{2,1,0:T(8,128)S(1)} %get-tuple-element.104.refs_7_.refs_11_.refs_4_) | copy-start | bytes 1572868
  86.2 8.2 %collective-permute-start.16 = (bf16[256,256]{1,0:T(8,128)(2,1)S(1)}, bf16[256,256]{1,0:T(8,128)(2,1)S(1)}, u32[]{:S(2)}, u32[]{:S(2)}) collective-permute-start(bf16[256,256]{1,0:T(8,128)(2,1)S(1)} %get-tuple-element.109), channel_id=1, source_target_pairs={{0,1},{1,0},{2,3},{3,2},{4,5},{5,4},{6,7},{7,6},{8,9},{9,8},{10,11... | collective-permute-start | bytes 393224 | tf_op jit(solution)/shard_map/ppermute | solution.py:341
  90.1 4.2 %collective-permute-start.17 = (bf16[256,256]{1,0:T(8,128)(2,1)S(1)}, bf16[256,256]{1,0:T(8,128)(2,1)S(1)}, u32[]{:S(2)}, u32[]{:S(2)}) collective-permute-start(bf16[256,256]{1,0:T(8,128)(2,1)S(1)} %get-tuple-element.110), channel_id=1, source_target_pairs={{1,2},{2,1},{3,4},{4,3},{5,6},{6,5},{7,8},{8,7},{9,10},{10,9},{11,... | collective-permute-start | bytes 393224 | tf_op jit(solution)/shard_map/ppermute | solution.py:341
  97.5 16.4 %all-to-all-start.1 = ((f32[16,1,128]{2,1,0:T(1,128)}), f32[16,1,128]{2,1,0:T(1,128)S(1)}, u32[]{:S(2)}, u32[]{:S(2)}) async-start(f32[16,1,128]{2,1,0:T(1,128)} %get-tuple-element.115), calls=%async_computation.1 | async-start | bytes 16384 | tf_op jit(solution)/shard_map/all_to_all | solution.py:378
  (15 other events, 46.7 us)

commit v3 on v0

v3 whole, which is shorter than its diff:
```python
import functools

import jax
import jax.numpy as jnp
from jax import lax
from jax.experimental import pallas as pl
from jax.experimental.pallas import tpu as pltpu
from jax.sharding import PartitionSpec as P

ITERS = 4
TAU = 0.05
F32 = jnp.float32
BF16 = jnp.bfloat16
LANES = 128
VMEM_LIMIT = 24 << 20
ROWS = 8

VMEM = pl.BlockSpec(memory_space=pltpu.VMEM)
SMEM = pl.BlockSpec(memory_space=pltpu.SMEM)
HBM = pl.BlockSpec(memory_space=pltpu.HBM)


def nn(a, b):
    return lax.dot_general(a, b, (((1,), (0,)), ((), ())), preferred_element_type=F32)


def nt(a, b):
    return lax.dot_general(a, b, (((1,), (1,)), ((), ())), preferred_element_type=F32)


def hop(block, inner, outer):
    return nn(outer, nt(block, inner).astype(BF16))


def masked(block, dim):
    rows = lax.broadcasted_iota(jnp.int32, block.shape, 0)
    cols = lax.broadcasted_iota(jnp.int32, block.shape, 1)
    return jnp.where(jnp.logical_and(rows < dim, cols < dim), block, 0.0)


def local_part(v, env, right, outer, inner, shift):
    held = len(v)
    terms = right.shape[1]
    b = [x.astype(BF16) for x in v]
    half = [[nt(b[s], right[0, w, s]).astype(BF16) for s in range(held)] for w in range(terms)]
    image = [None] * held
    for s in range(held):
        if s > 0:
            image[s] = hop(b[s - 1], inner[0, 0, s], outer[0, 0, s])
        if s + 1 < held:
            above = hop(b[s + 1], inner[0, 1, s], outer[0, 1, s])
            image[s] = above if image[s] is None else image[s] + above
    for w in range(terms):
        for s in range(held):
            term = nn(env(w, s), half[w][s])
            image[s] = term if image[s] is None else image[s] + term
    return [v[s] * (1.0 + TAU * shift) - TAU * image[s] for s in range(held)]


def dot_rows(basis, last):
    rows = lax.broadcasted_iota(jnp.int32, (ROWS, LANES), 0)
    out = jnp.zeros((ROWS, LANES), F32)
    for i, other in enumerate(basis):
        total = sum(jnp.sum(a * b, axis=0, keepdims=True) for a, b in zip(other, last))
        total = sum(total[:, n : n + LANES] for n in range(0, total.shape[1], LANES))
        out = jnp.where(rows == i, total, out)
    return out


class Facts:
    ODD, FIRST, LIVE, INSIDE, ACROSS, DIM = range(6)

    def __init__(self, ref):
        self.ref = ref

    def row(self, n):
        return self.ref[n : n + 1, 0:1]

    @property
    def odd(self):
        return self.row(self.ODD) == 1

    def dim(self, s):
        return self.row(self.DIM + s)


def swapped(odd, low, high):
    return jnp.where(odd, low, high), jnp.where(odd, high, low)


def start_kernel(
    place, dims, psi_at, outer_at, inner_at, v0, inside, across, facts, psi, blocks, arrived
):
    held, cap, _ = psi.shape
    copies = [pltpu.make_async_copy(psi_at.at[0, s], psi.at[s], arrived.at[s]) for s in range(held)]
    for n, (side, s) in enumerate(((0, 0), (1, held - 1))):
        for m, array in enumerate((outer_at, inner_at)):
            copies.append(
                pltpu.make_async_copy(
                    array.at[0, side, s], blocks.at[2 * n + m], arrived.at[held + 2 * n + m]
                )
            )
    for copy in copies:
        copy.start()
    first = place[0] * held
    last = dims.shape[1] - 1
    odd = place[0] % 2
    low_dim = dims[0, jnp.maximum(first - 1, 0)]
    high_dim = dims[0, jnp.minimum(first + held, last)]
    live = jnp.int32(0)
    for s in range(dims.shape[1]):
        live = live + dims[0, s] * dims[0, s]
    rows = [
        odd,
        jnp.where(place[1] == 0, 1, 0),
        live,
        jnp.where(odd == 1, low_dim, high_dim),
        jnp.where(odd == 1, high_dim, low_dim),
    ] + [dims[0, first + s] for s in range(held)]
    for n, value in enumerate(rows):
        facts[n : n + 1, :] = jnp.full((1, LANES), value, jnp.int32)
    for copy in copies[:held]:
        copy.wait()
    edges = [masked(psi[s], dims[0, first + s]) for s in range(held)]
    for s in range(held):
        v0[s] = edges[s]
    low = edges[0].astype(BF16)
    high = edges[-1].astype(BF16)
    inside[0] = jnp.where(odd == 1, low, high)
    across[0] = jnp.where(odd == 1, high, low)
    for copy in copies[held:]:
        copy.wait()
    for m in range(2):
        inside[1 + m] = jnp.where(odd == 1, blocks[m], blocks[2 + m])
        across[1 + m] = jnp.where(odd == 1, blocks[2 + m], blocks[m])


def put_local(v, env, r, shift):
    facts = Facts(r["facts"])
    out = local_part(v, env, r["right"], r["outer"], r["inner"], shift)
    for s, block in enumerate(out):
        r["q"][s] = block
    inside, across = swapped(facts.odd, out[0], out[-1])
    r["inside"][...] = inside.astype(BF16)
    r["across"][...] = across.astype(BF16)


def local_kernel(shift, names, *refs):
    r = dict(zip(names, refs))
    v = [r["v0"][s] for s in range(r["v0"].shape[0])]
    put_local(v, lambda w, s: r["left"][0, w, s], r, shift)
    r["dots"][...] = dot_rows([v], v)


def ghosts(k, facts, r):
    came = [r["came_inside"], r["came_across"]]
    came = [(c[0] if len(c.shape) == 3 else c[...]).astype(F32) for c in came]
    if k > 0:
        before = r[f"v{k - 1}"]
        sent = swapped(facts.odd, before[0], before[before.shape[0] - 1])
        dims = (facts.row(facts.INSIDE), facts.row(facts.ACROSS))
        hops = (r["hops_inside"], r["hops_across"])
        came = [
            masked(c - TAU * hop(b.astype(BF16), h[2], h[1]), d)
            for c, b, h, d in zip(came, sent, hops, dims)
        ]
    low, high = swapped(facts.odd, *came)
    return low.astype(BF16), high.astype(BF16)


def step_kernel(k, shift, names, *refs):
    r = dict(zip(names, refs))
    facts = Facts(r["facts"])
    outer, inner = r["outer"], r["inner"]
    held = r["part"].shape[0]
    low, high = ghosts(k, facts, r)
    v = [r["part"][s] for s in range(held)]
    v[0] = v[0] - TAU * hop(low, inner[0, 0, 0], outer[0, 0, 0])
    v[-1] = v[-1] - TAU * hop(high, inner[0, 1, held - 1], outer[0, 1, held - 1])
    v = [masked(block, facts.dim(s)) for s, block in enumerate(v)]
    for s in range(held):
        r["v"][s] = v[s]
    basis = [[r[f"v{i}"][s] for s in range(held)] for i in range(k + 1)]
    if k + 1 < ITERS:
        left = r["left"]
        env = (lambda w, s: left[0, w, s]) if len(left.shape) == 5 else (lambda w, s: left[w, s])
        put_local(v, env, r, shift)
        r["dots"][...] = dot_rows(basis + [v], v)
    else:
        lanes = lax.broadcasted_iota(jnp.int32, (ROWS, LANES), 1)
        rows = lax.broadcasted_iota(jnp.int32, (ROWS, LANES), 0)
        line = jnp.zeros((1, LANES), F32)
        for j in range(ITERS + 1):
            part = r[f"dots{j}"][...] if j < ITERS else dot_rows(basis + [v], v)
            part = jnp.sum(part, axis=1, keepdims=True)
            line = line + jnp.sum(
                jnp.where(lanes == ROWS * j + rows, part, 0.0), axis=0, keepdims=True
            )
        for n in range(r["line"].shape[0]):
            r["line"][n] = line


def combination(line, live_count, shift):
    lanes = lax.broadcasted_iota(jnp.int32, (1, LANES), 1)
    gram = {}
    for j in range(ITERS + 1):
        for i in range(j + 1):
            gram[i, j] = jnp.sum(
                jnp.where(lanes == ROWS * j + i, line, 0.0), axis=1, keepdims=True
            )
            gram[j, i] = gram[i, j]
    coefs = [jnp.ones((1, 1), F32)]
    energy = None
    for _ in range(ITERS):
        n = len(coefs)
        onto = [sum(coefs[i] * gram[i, j] for i in range(n)) for j in range(n + 1)]
        raised = [sum(coefs[i] * gram[i + 1, j] for i in range(n)) for j in range(1, n + 1)]
        self_dot = sum(coefs[j] * onto[j] for j in range(n))
        cross = sum(coefs[j] * onto[j + 1] for j in range(n))
        square = sum(coefs[j] * raised[j] for j in range(n))
        ratio = cross / self_dot
        gain = 1.0 - ratio
        energy = shift + gain / TAU
        norm = square + gain * (2.0 * cross + gain * self_dot)
        scale = jnp.sqrt(live_count / norm)
        moved = [gain * c for c in coefs] + [jnp.zeros((1, 1), F32)]
        moved = [moved[0]] + [moved[i + 1] + coefs[i] for i in range(n)]
        coefs = [scale * c for c in moved]
    return coefs, energy


def join_kernel(shift, names, *refs):
    r = dict(zip(names, refs))
    facts = Facts(r["facts"])
    line = jnp.sum(r["lines"][...], axis=0)
    coefs, _ = combination(line, facts.row(facts.LIVE).astype(F32), shift)
    held, cap, _ = r["v0"].shape
    pad = r["factor"].shape[1] - cap
    blocks = [sum(c * r[f"v{k}"][s] for k, c in enumerate(coefs)) for s in range(held)]
    for s, block in enumerate(blocks):
        r["x"][s] = block
        r["factor"][s, :cap] = block.astype(BF16)
        dim = jnp.broadcast_to(facts.dim(s).astype(F32), (pad, cap))
        r["factor"][s, cap:] = dim.astype(BF16)
    inside, across = swapped(facts.odd, blocks[0], blocks[-1])
    r["inside"][...] = inside.astype(BF16)
    r["across"][...] = across.astype(BF16)


def grown(env, factor):
    cap = env.shape[0]
    block = factor[:cap]
    product = nn(block.T, nn(env, block).astype(BF16))
    return (product / factor[cap : cap + 1].astype(F32)).astype(BF16)


def grow_kernel(left, factor, out, token):
    for s in range(left.shape[2]):
        for w in range(left.shape[1]):
            out[0, w, s] = grown(left[0, w, s], factor[s])
    token[...] = jnp.zeros_like(token)


def second_kernel(shift, names, *refs):
    r = dict(zip(names, refs))
    facts = Facts(r["facts"])
    held = r["v0"].shape[0]
    first = facts.row(facts.FIRST) == 1
    for s in range(held):
        for w in range(r["left"].shape[1]):
            new = grown(r["earlier"][0, w, s], r["factor"][s]).astype(F32)
            kept = r["left"][0, w, s].astype(F32)
            r["env"][w, s] = jnp.where(first, kept, new).astype(BF16)
    v = [r["v0"][s] for s in range(held)]
    put_local(v, lambda w, s: r["env"][w, s], r, shift)
    r["dots"][...] = dot_rows([v], v)


def finish_kernel(shift, names, *refs):
    r = dict(zip(names, refs))
    facts = Facts(r["facts"])
    line = jnp.sum(r["lines"][...], axis=0)
    coefs, energy = combination(line, facts.row(facts.LIVE).astype(F32), shift)
    for s in range(r["v0"].shape[0]):
        r["x"][0, s] = sum(c * r[f"v{k}"][s] for k, c in enumerate(coefs))
    r["energy"][0] = energy[0, 0]


def struct(shape, dtype):
    return jax.ShapeDtypeStruct(shape, dtype)


def call(kernel, name, ins, outs, flops=0, specs=None, scratch=()):
    args = tuple(ins.values())
    values = pl.pallas_call(
        kernel,
        out_shape=tuple(outs.values()),
        in_specs=specs or [VMEM] * len(args),
        out_specs=tuple(SMEM if o.shape == (1,) else VMEM for o in outs.values()),
        scratch_shapes=scratch,
        name=name,
        compiler_params=pltpu.CompilerParams(vmem_limit_bytes=VMEM_LIMIT),
        cost_estimate=pl.CostEstimate(
            flops=flops,
            transcendentals=0,
            bytes_accessed=sum(a.size * a.dtype.itemsize for a in args),
        ),
    )(*args)
    return dict(zip(outs, values))


def body(psi, left_env, right_env, hop_outer, hop_inner, dims):
    _, terms, held, cap, _ = left_env.shape
    shift = float(terms)
    size = lax.axis_size("sec")
    place = jnp.stack([lax.axis_index("sec"), lax.axis_index("seg")]).astype(jnp.int32)
    block = struct((cap, cap), BF16)
    blocks = struct((held, cap, cap), F32)
    triple = struct((3, cap, cap), BF16)
    dots_of = struct((ROWS, LANES), F32)
    local_outs = {"q": blocks, "inside": block, "across": block, "dots": dots_of}
    pairs = [(i, i ^ 1) for i in range(size)]
    others = [(i, i + 1 if i % 2 else i - 1) for i in range(1, size - 1)]
    onward = [(i, i + 1) for i in range(lax.axis_size("seg") - 1)]
    one = 2 * cap**3

    def exchange(got):
        return {
            "came_inside": lax.ppermute(got["inside"], "sec", pairs),
            "came_across": lax.ppermute(got["across"], "sec", others),
        }

    def made(kernel, name, ins, outs, flops=0):
        names = tuple(ins) + tuple(outs)
        return call(functools.partial(kernel, names), name, ins, outs, flops)

    start = call(
        start_kernel,
        "start",
        {"place": place, "dims": dims, "psi": psi, "outer": hop_outer, "inner": hop_inner},
        {
            "v0": blocks,
            "inside": triple,
            "across": triple,
            "facts": struct((ROWS * (1 + (4 + held) // ROWS), LANES), jnp.int32),
        },
        specs=[SMEM, SMEM, HBM, HBM, HBM],
        scratch=[
            pltpu.VMEM((held, cap, cap), F32),
            pltpu.VMEM((4, cap, cap), BF16),
            pltpu.SemaphoreType.DMA((held + 4,)),
        ],
    )
    facts = start["facts"]
    common = {"facts": facts, "outer": hop_outer, "inner": hop_inner, "right": right_env}
    came = exchange(start)
    hops = {"hops_inside": came["came_inside"], "hops_across": came["came_across"]}
    earlier = lax.ppermute(left_env, "seg", onward)

    def relaxed(v0, came, got, env):
        basis = {"v0": v0}
        dots = {"dots0": got["dots"]}
        for k in range(ITERS):
            ins = {"part": got["q"], **common, **basis, **came}
            if k > 0:
                ins.update(hops)
            if k + 1 < ITERS:
                came = exchange(got)
                ins.update(left=env)
                outs = {"v": blocks, **local_outs}
            else:
                del ins["right"]
                ins.update(dots)
                outs = {"v": blocks, "line": struct((size, 1, LANES), F32)}
            kernel = functools.partial(step_kernel, k, shift)
            got = made(kernel, f"step{k}", ins, outs, flops=one * 36)
            basis[f"v{k + 1}"] = got["v"]
            if k + 1 < ITERS:
                dots[f"dots{k + 1}"] = got["dots"]
        return basis, lax.all_to_all(got["line"], "sec", 0, 0)

    got = made(
        functools.partial(local_kernel, shift),
        "local",
        {"v0": start["v0"], "left": left_env, **common},
        local_outs,
        flops=one * 28,
    )
    basis, lines = relaxed(start["v0"], came, got, left_env)
    joined = made(
        functools.partial(join_kernel, shift),
        "join",
        {"facts": facts, "lines": lines, **basis},
        {
            "x": blocks,
            "factor": struct((held, cap + 16, cap), BF16),
            "inside": block,
            "across": block,
        },
    )
    factor = joined["factor"]
    earlier_factor = lax.ppermute(factor, "seg", onward)
    came = exchange(joined)
    renewed = call(
        grow_kernel,
        "grow",
        {"left": left_env, "factor": factor},
        {"out": struct(left_env.shape, BF16), "token": dots_of},
        flops=one * 24,
    )
    got = made(
        functools.partial(second_kernel, shift),
        "second",
        {
            "v0": joined["x"],
            "left": left_env,
            "earlier": earlier,
            "factor": earlier_factor,
            "token": renewed["token"],
            **common,
        },
        {"env": struct((terms, held, cap, cap), BF16), **local_outs},
        flops=one * 52,
    )
    basis, lines = relaxed(joined["x"], came, got, got["env"])
    done = made(
        functools.partial(finish_kernel, shift),
        "finish",
        {"facts": facts, "lines": lines, **basis},
        {"x": struct(psi.shape, F32), "energy": struct((1,), F32)},
    )
    return (done["x"], done["energy"], renewed["out"])


def solution(mesh):
    return jax.shard_map(
        body,
        mesh=mesh,
        in_specs=(
            P("seg", "sec", None, None),
            P("seg", None, "sec", None, None),
            P("seg", None, "sec", None, None),
            P("seg", None, "sec", None, None),
            P("seg", None, "sec", None, None),
            P("seg", None),
        ),
        out_specs=(P("seg", "sec", None, None), P("seg"), P("seg", None, "sec", None, None)),
        check_vma=False,
    )
```

time: 802 us -> 108 us (0.13)
  blocking collectives: 597 us -> 34.8 us
  matrix products: 68 us -> 0 us
  waiting for transfers between devices: 36.8 us -> 3.58 us
  Pallas kernels: 0 us -> 26.3 us
  other arithmetic: 24.8 us -> 0.08 us
  between operations: 23.8 us -> 1.08 us
    psum x16 -> x0, blocking collectives: 597 us -> none  [the longest x8 303 us: relax(): step_norm = lax.psum(jnp.sum(step * step), 'sec')]
    dot_general x25 -> x0, matrix products: 68 us -> none  [the longest x8 29 us: apply_operator(): jnp.einsum('wsik,wskj->sij', env_left, halfway, preferred_element_type=jn...]
    all_to_all x0 -> x2, blocking collectives: none -> 34.8 us  [relaxed(): return (basis, lax.all_to_all(got['line'], 'sec', 0, 0))]
    ppermute x17 -> x18, waiting for transfers between devices: 36.8 us -> 3.58 us  [the longest x1 3.34 us: body(): earlier_factor = lax.ppermute(factor, 'seg', onward)]
    pallas_call x0 -> x14, Pallas kernels: none -> 26.3 us  [call(): pl.pallas_call(kernel, out_shape=tuple(outs.values()), in_specs=specs or...]
    reduce_sum x9 -> x0, other arithmetic: 17 us -> none  [the longest x8 16.3 us: relax(): step_norm = lax.psum(jnp.sum(step * step), 'sec')]
    ppermute x17 -> x18, starting transfers between devices: 36 us -> 34.2 us  [the longest x8 24.6 us: exchange(): lax.ppermute(got['inside'], 'sec', pairs)]
  transfers between devices with their start and end apart: 17 -> 18, of which waited for: 12 -> 2; matrix products, arithmetic and copies ran while one was open for 5% -> 0% of each run, Pallas kernels for 0% -> 22%
where the time goes in v3:
time: 108 us; the launch traced here: 107 us
  blocking collectives  34.8 us (32%)
  starting transfers between devices  34.2 us (32%)
  Pallas kernels  26.3 us (24%)
  local copies, waits for them, and re-layouts  7.28 us (7%)
  waiting for transfers between devices  3.58 us (3%)
  between operations  1.08 us (1%)
    all_to_all x2, blocking collectives, relaxed(): return (basis, lax.all_to_all(got['line'], 'sec', 0, 0))  34.8 us
    pallas_call x14, Pallas kernels, call(): pl.pallas_call(kernel, out_shape=tuple(outs.values()), in_specs=specs or...  26.3 us
    ppermute x8, starting transfers between devices, exchange(): lax.ppermute(got['inside'], 'sec', pairs)  24.6 us
    unnamed x22, local copies, waits for them, and re-layouts  7.28 us
    ppermute x8, starting transfers between devices, exchange(): lax.ppermute(got['across'], 'sec', others)  5.45 us
    ppermute x1, waiting for transfers between devices, body(): earlier_factor = lax.ppermute(factor, 'seg', onward)  3.34 us
  transfers between devices with their start and end apart: 18, of which 2 were waited for; matrix products, arithmetic and copies ran while one was open for 0% of the time, Pallas kernels for 22%

profile of v3, /device:TPU:128, one launch (start us, length us, event | category | flops | bytes accessed | tf_op | source)
XLA Modules:
  0.0 107.4 jit_solution(8189490305203236632)
XLA Ops:
  0.6 2.1 %collective-permute-start.8 = (bf16[1,6,2,256,256]{4,3,2,1,0:T(8,128)(2,1)}, bf16[1,6,2,256,256]{4,3,2,1,0:T(8,128)(2,1)S(1)}, u32[]{:S(2)}, u32[]{:S(2)}) collective-permute-start(bf16[1,6,2,256,256]{4,3,2,1,0:T(8,128)(2,1)} %refs_1_.3), channel_id=1, source_target_pairs={{0,16},{16,32},{32,48},{48,64},{64,80},{80,96},{96,112},{112,128},... | collective-permute-start | bytes 4718600 | tf_op jit(solution)/shard_map/ppermute | solution.py:358
  6.6 1.5 %start.1 = (f32[2,256,256]{2,1,0:T(8,128)S(1)}, bf16[3,256,256]{2,1,0:T(8,128)(2,1)S(1)}, bf16[3,256,256]{2,1,0:T(8,128)(2,1)S(1)}, s32[8,128]{1,0:T(8,128)S(1)}) custom-call(s32[2]{0:T(128)S(1)} %pad_add_fusion.place, s32[1,32]{1,0:T(1,128)S(1)} %copy-done.10, f32[1,2,256,256]{3,2,1,0:T(8,128)S(1)} %copy-done.9, bf16[1,2,2,256,256]{4,3,2,1,0:T(8,128)(2,1)S(1)} %copy-done.1, ...), custom_call_target="tpu_custom_call" | custom-call | bytes 1573000 | tf_op jit(solution)/shard_map/start/pallas_call | solution.py:295
  8.0 1.6 %collective-permute-start = (bf16[3,256,256]{2,1,0:T(8,128)(2,1)S(1)}, bf16[3,256,256]{2,1,0:T(8,128)(2,1)S(1)}, u32[]{:S(2)}, u32[]{:S(2)}) collective-permute-start(bf16[3,256,256]{2,1,0:T(8,128)(2,1)S(1)} %get-tuple-element.57), channel_id=1, source_target_pairs={{0,1},{1,0},{2,3},{3,2},{4,5},{5,4},{6,7},{7,6},{8,9},{9,8},{10,11... | collective-permute-start | bytes 1179656 | tf_op jit(solution)/shard_map/ppermute | solution.py:329
  12.4 1.4 %copy-done.7 = bf16[1,6,2,256,256]{4,3,2,1,0:T(8,128)(2,1)S(1)} copy-done((bf16[1,6,2,256,256]{4,3,2,1,0:T(8,128)(2,1)S(1)}, bf16[1,6,2,256,256]{4,3,2,1,0:T(8,128)(2,1)}, u32[]{:S(2)}) %copy-start.7) | copy-done | bytes 1572888
  15.1 4.0 %collective-permute-start.2 = (bf16[256,256]{1,0:T(8,128)(2,1)S(1)}, bf16[256,256]{1,0:T(8,128)(2,1)S(1)}, u32[]{:S(2)}, u32[]{:S(2)}) collective-permute-start(bf16[256,256]{1,0:T(8,128)(2,1)S(1)} %get-tuple-element.61), channel_id=1, source_target_pairs={{0,1},{1,0},{2,3},{3,2},{4,5},{5,4},{6,7},{7,6},{8,9},{9,8},{10,11... | collective-permute-start | bytes 393224 | tf_op jit(solution)/shard_map/ppermute | solution.py:329
  20.0 1.8 %step0.2 = (f32[2,256,256]{2,1,0:T(8,128)S(1)}, f32[2,256,256]{2,1,0:T(8,128)S(1)}, bf16[256,256]{1,0:T(8,128)(2,1)S(1)}, bf16[256,256]{1,0:T(8,128)(2,1)S(1)}, f32[8,128]{1,0:T(8,128)S(1)}) custom-call(f32[2,256,256]{2,1,0:T(8,128)S(1)} %get-tuple-element.56.refs_0_, s32[8,128]{1,0:T(8,128)S(1)} %get-tuple-element.54.refs_2_.refs_1_.refs_0_.refs_5_, ...), custom_call_target="tpu_custom_call" | custom-call | flops 1207959552 | bytes 6033408 | tf_op jit(solution)/shard_map/step0/pallas_call | solution.py:295
  21.8 4.1 %collective-permute-start.4 = (bf16[256,256]{1,0:T(8,128)(2,1)S(1)}, bf16[256,256]{1,0:T(8,128)(2,1)S(1)}, u32[]{:S(2)}, u32[]{:S(2)}) collective-permute-start(bf16[256,256]{1,0:T(8,128)(2,1)S(1)} %get-tuple-element.65), channel_id=1, source_target_pairs={{0,1},{1,0},{2,3},{3,2},{4,5},{5,4},{6,7},{7,6},{8,9},{9,8},{10,11... | collective-permute-start | bytes 393224 | tf_op jit(solution)/shard_map/ppermute | solution.py:329
  26.6 2.3 %step1.2 = (f32[2,256,256]{2,1,0:T(8,128)S(1)}, f32[2,256,256]{2,1,0:T(8,128)S(1)}, bf16[256,256]{1,0:T(8,128)(2,1)S(1)}, bf16[256,256]{1,0:T(8,128)(2,1)S(1)}, f32[8,128]{1,0:T(8,128)S(1)}) custom-call(f32[2,256,256]{2,1,0:T(8,128)S(1)} %get-tuple-element.59.refs_0_, s32[8,128]{1,0:T(8,128)S(1)} %get-tuple-element.54.refs_2_.refs_1_.refs_0_.refs_5_, ...), custom_call_target="tpu_custom_call" | custom-call | flops 1207959552 | bytes 6819840 | tf_op jit(solution)/shard_map/step1/pallas_call | solution.py:295
  28.9 6.3 %collective-permute-start.6 = (bf16[256,256]{1,0:T(8,128)(2,1)S(1)}, bf16[256,256]{1,0:T(8,128)(2,1)S(1)}, u32[]{:S(2)}, u32[]{:S(2)}) collective-permute-start(bf16[256,256]{1,0:T(8,128)(2,1)S(1)} %get-tuple-element.69), channel_id=1, source_target_pairs={{0,1},{1,0},{2,3},{3,2},{4,5},{5,4},{6,7},{7,6},{8,9},{9,8},{10,11... | collective-permute-start | bytes 393224 | tf_op jit(solution)/shard_map/ppermute | solution.py:329
  35.9 3.0 %step2.2 = (f32[2,256,256]{2,1,0:T(8,128)S(1)}, f32[2,256,256]{2,1,0:T(8,128)S(1)}, bf16[256,256]{1,0:T(8,128)(2,1)}, bf16[256,256]{1,0:T(8,128)(2,1)}, f32[8,128]{1,0:T(8,128)S(1)}) custom-call(f32[2,256,256]{2,1,0:T(8,128)S(1)} %get-tuple-element.63.refs_0_, s32[8,128]{1,0:T(8,128)S(1)} %get-tuple-element.54.refs_2_.refs_1_.refs_0_.refs_5_, ...), custom_call_target="tpu_custom_call" | custom-call | flops 1207959552 | bytes 7344128 | tf_op jit(solution)/shard_map/step2/pallas_call | solution.py:295
  38.9 1.4 %step3.2 = (f32[2,256,256]{2,1,0:T(8,128)S(1)}, f32[16,1,128]{2,1,0:T(1,128)S(1)}) custom-call(f32[2,256,256]{2,1,0:T(8,128)S(1)} %get-tuple-element.67.refs_0_, s32[8,128]{1,0:T(8,128)S(1)} %get-tuple-element.54.refs_2_.refs_1_.refs_0_.refs_5_, bf16[1,2,2,256,256]{4,3,2,1,0:T(8,128)(2,1)S(1)} %copy-done.2, bf16[1,2,2,256,256]{4,3,2,1,0:T(8,128)(2,1)S(1)} %copy-done.5, ...), custom_call_target="tpu_custom_call" | custom-call | flops 1207959552 | bytes 4739072 | tf_op jit(solution)/shard_map/step3/pallas_call | solution.py:295
  40.3 17.9 %all_to_all.10.refs_1_ = f32[16,1,128]{2,1,0:T(1,128)S(1)} all-to-all(f32[16,1,128]{2,1,0:T(1,128)S(1)} %get-tuple-element.75), channel_id=1, replica_groups=mesh['seg'=16,'sec'=16] {'sec'}, dimensions={0} | all-to-all | bytes 16384 | tf_op jit(solution)/shard_map/all_to_all | solution.py:380
  58.9 2.1 %collective-permute-start.9 = (bf16[2,272,256]{2,1,0:T(8,128)(2,1)S(1)}, bf16[2,272,256]{2,1,0:T(8,128)(2,1)S(1)}, u32[]{:S(2)}, u32[]{:S(2)}) collective-permute-start(bf16[2,272,256]{2,1,0:T(8,128)(2,1)S(1)} %get-tuple-element.78.factor), channel_id=1, source_target_pairs={{0,16},{16,32},{32,48},{48,64},{64,80},{80,96},{96,112},{112,128},... | collective-permute-start | bytes 835592 | tf_op jit(solution)/shard_map/ppermute | solution.py:402
  62.5 2.3 %grow.1 = (bf16[1,6,2,256,256]{4,3,2,1,0:T(8,128)(2,1)}, f32[8,128]{1,0:T(8,128)S(1)}) custom-call(bf16[1,6,2,256,256]{4,3,2,1,0:T(8,128)(2,1)S(1)} %copy-done.8, bf16[2,272,256]{2,1,0:T(8,128)(2,1)S(1)} %get-tuple-element.78.factor), custom_call_target="tpu_custom_call" | custom-call | flops 805306368 | bytes 1851392 | tf_op jit(solution)/shard_map/grow/pallas_call | solution.py:295
  64.8 3.3 %collective-permute-done.9.refs_3_ = bf16[2,272,256]{2,1,0:T(8,128)(2,1)S(1)} collective-permute-done((bf16[2,272,256]{2,1,0:T(8,128)(2,1)S(1)}, bf16[2,272,256]{2,1,0:T(8,128)(2,1)S(1)}, u32[]{:S(2)}, u32[]{:S(2)}) %collective-permute-start.9) | collective-permute-done | bytes 278560 | tf_op jit(solution)/shard_map/ppermute | solution.py:402
  68.1 2.2 %second.1 = (bf16[6,2,256,256]{3,2,1,0:T(8,128)(2,1)S(1)}, f32[2,256,256]{2,1,0:T(8,128)S(1)}, bf16[256,256]{1,0:T(8,128)(2,1)S(1)}, bf16[256,256]{1,0:T(8,128)(2,1)S(1)}, f32[8,128]{1,0:T(8,128)S(1)}) custom-call(f32[2,256,256]{2,1,0:T(8,128)S(1)} %get-tuple-element.77.refs_0_.refs_5_.refs_4_.refs_2_, bf16[1,6,2,256,256]{4,3,2,1,0:T(8,128)(2,1)S(1)} %copy-done.8, ...), custom_call_target="tpu_custom_call" | custom-call | flops 1744830464 | bytes 6578176 | tf_op jit(solution)/shard_map/second/pallas_call | solution.py:295
  71.7 1.8 %step0.3 = (f32[2,256,256]{2,1,0:T(8,128)S(1)}, f32[2,256,256]{2,1,0:T(8,128)S(1)}, bf16[256,256]{1,0:T(8,128)(2,1)S(1)}, bf16[256,256]{1,0:T(8,128)(2,1)S(1)}, f32[8,128]{1,0:T(8,128)S(1)}) custom-call(f32[2,256,256]{2,1,0:T(8,128)S(1)} %get-tuple-element.80.refs_0_, s32[8,128]{1,0:T(8,128)S(1)} %get-tuple-element.54.refs_2_.refs_1_.refs_0_.refs_5_, ...), custom_call_target="tpu_custom_call" | custom-call | flops 1207959552 | bytes 5509120 | tf_op jit(solution)/shard_map/step0/pallas_call | solution.py:295
  73.5 3.4 %collective-permute-start.14 = (bf16[256,256]{1,0:T(8,128)(2,1)S(1)}, bf16[256,256]{1,0:T(8,128)(2,1)S(1)}, u32[]{:S(2)}, u32[]{:S(2)}) collective-permute-start(bf16[256,256]{1,0:T(8,128)(2,1)S(1)} %get-tuple-element.90), channel_id=1, source_target_pairs={{0,1},{1,0},{2,3},{3,2},{4,5},{5,4},{6,7},{7,6},{8,9},{9,8},{10,11... | collective-permute-start | bytes 393224 | tf_op jit(solution)/shard_map/ppermute | solution.py:329
  77.6 2.3 %step1.3 = (f32[2,256,256]{2,1,0:T(8,128)S(1)}, f32[2,256,256]{2,1,0:T(8,128)S(1)}, bf16[256,256]{1,0:T(8,128)(2,1)S(1)}, bf16[256,256]{1,0:T(8,128)(2,1)S(1)}, f32[8,128]{1,0:T(8,128)S(1)}) custom-call(f32[2,256,256]{2,1,0:T(8,128)S(1)} %get-tuple-element.84.refs_0_, s32[8,128]{1,0:T(8,128)S(1)} %get-tuple-element.54.refs_2_.refs_1_.refs_0_.refs_5_, ...), custom_call_target="tpu_custom_call" | custom-call | flops 1207959552 | bytes 6819840 | tf_op jit(solution)/shard_map/step1/pallas_call | solution.py:295
  79.9 4.0 %collective-permute-start.16 = (bf16[256,256]{1,0:T(8,128)(2,1)S(1)}, bf16[256,256]{1,0:T(8,128)(2,1)S(1)}, u32[]{:S(2)}, u32[]{:S(2)}) collective-permute-start(bf16[256,256]{1,0:T(8,128)(2,1)S(1)} %get-tuple-element.94), channel_id=1, source_target_pairs={{0,1},{1,0},{2,3},{3,2},{4,5},{5,4},{6,7},{7,6},{8,9},{9,8},{10,11... | collective-permute-start | bytes 393224 | tf_op jit(solution)/shard_map/ppermute | solution.py:329
  84.5 3.0 %step2.3 = (f32[2,256,256]{2,1,0:T(8,128)S(1)}, f32[2,256,256]{2,1,0:T(8,128)S(1)}, bf16[256,256]{1,0:T(8,128)(2,1)}, bf16[256,256]{1,0:T(8,128)(2,1)}, f32[8,128]{1,0:T(8,128)S(1)}) custom-call(f32[2,256,256]{2,1,0:T(8,128)S(1)} %get-tuple-element.88.refs_0_, s32[8,128]{1,0:T(8,128)S(1)} %get-tuple-element.54.refs_2_.refs_1_.refs_0_.refs_5_, ...), custom_call_target="tpu_custom_call" | custom-call | flops 1207959552 | bytes 7344128 | tf_op jit(solution)/shard_map/step2/pallas_call | solution.py:295
  87.5 1.4 %step3.3 = (f32[2,256,256]{2,1,0:T(8,128)S(1)}, f32[16,1,128]{2,1,0:T(1,128)S(1)}) custom-call(f32[2,256,256]{2,1,0:T(8,128)S(1)} %get-tuple-element.92.refs_0_, s32[8,128]{1,0:T(8,128)S(1)} %get-tuple-element.54.refs_2_.refs_1_.refs_0_.refs_5_, bf16[1,2,2,256,256]{4,3,2,1,0:T(8,128)(2,1)S(1)} %copy-done.3, bf16[1,2,2,256,256]{4,3,2,1,0:T(8,128)(2,1)S(1)} %copy-done.6, ...), custom_call_target="tpu_custom_call" | custom-call | flops 1207959552 | bytes 4739072 | tf_op jit(solution)/shard_map/step3/pallas_call | solution.py:295
  88.9 16.9 %all_to_all.11.refs_1_ = f32[16,1,128]{2,1,0:T(1,128)S(1)} all-to-all(f32[16,1,128]{2,1,0:T(1,128)S(1)} %get-tuple-element.100), channel_id=1, replica_groups=mesh['seg'=16,'sec'=16] {'sec'}, dimensions={0} | all-to-all | bytes 16384 | tf_op jit(solution)/shard_map/all_to_all | solution.py:380
  105.8 1.4 %finish.1 = (f32[1,2,256,256]{3,2,1,0:T(8,128)}, f32[1]{0:T(128)}) custom-call(s32[8,128]{1,0:T(8,128)S(1)} %get-tuple-element.54.refs_2_.refs_1_.refs_0_.refs_5_, f32[16,1,128]{2,1,0:T(1,128)S(1)} %all_to_all.11.refs_1_, f32[2,256,256]{2,1,0:T(8,128)S(1)} %get-tuple-element.77.refs_0_.refs_5_.refs_4_.refs_2_, ...), custom_call_target="tpu_custom_call" | custom-call | bytes 2633728 | tf_op jit(solution)/shard_map/finish/pallas_call | solution.py:295
  (51 shorter events, 14.9 us)
Async XLA Ops:
  0.6 9.7 %copy-start = (bf16[1,6,2,256,256]{4,3,2,1,0:T(8,128)(2,1)S(1)}, bf16[1,6,2,256,256]{4,3,2,1,0:T(8,128)(2,1)}, u32[]{:S(2)}) copy-start(bf16[1,6,2,256,256]{4,3,2,1,0:T(8,128)(2,1)} %refs_4_.13) | copy-start | bytes 4718596
  0.6 67.5 %collective-permute-start.8 = (bf16[1,6,2,256,256]{4,3,2,1,0:T(8,128)(2,1)}, bf16[1,6,2,256,256]{4,3,2,1,0:T(8,128)(2,1)S(1)}, u32[]{:S(2)}, u32[]{:S(2)}) collective-permute-start(bf16[1,6,2,256,256]{4,3,2,1,0:T(8,128)(2,1)} %refs_1_.3), channel_id=1, source_target_pairs={{0,16},{16,32},{32,48},{48,64},{64,80},{80,96},{96,112},{112,128},... | collective-permute-start | bytes 4718600 | tf_op jit(solution)/shard_map/ppermute | solution.py:358
  8.0 11.9 %collective-permute-start = (bf16[3,256,256]{2,1,0:T(8,128)(2,1)S(1)}, bf16[3,256,256]{2,1,0:T(8,128)(2,1)S(1)}, u32[]{:S(2)}, u32[]{:S(2)}) collective-permute-start(bf16[3,256,256]{2,1,0:T(8,128)(2,1)S(1)} %get-tuple-element.57), channel_id=1, source_target_pairs={{0,1},{1,0},{2,3},{3,2},{4,5},{5,4},{6,7},{7,6},{8,9},{9,8},{10,11... | collective-permute-start | bytes 1179656 | tf_op jit(solution)/shard_map/ppermute | solution.py:329
  9.6 10.3 %collective-permute-start.1 = (bf16[3,256,256]{2,1,0:T(8,128)(2,1)S(1)}, bf16[3,256,256]{2,1,0:T(8,128)(2,1)S(1)}, u32[]{:S(2)}, u32[]{:S(2)}) collective-permute-start(bf16[3,256,256]{2,1,0:T(8,128)(2,1)S(1)} %get-tuple-element.58), channel_id=1, source_target_pairs={{1,2},{2,1},{3,4},{4,3},{5,6},{6,5},{7,8},{8,7},{9,10},{10,9},{11,... | collective-permute-start | bytes 1179656 | tf_op jit(solution)/shard_map/ppermute | solution.py:330
  10.3 1.0 copy-start.2
  12.4 1.4 %copy-start.7 = (bf16[1,6,2,256,256]{4,3,2,1,0:T(8,128)(2,1)S(1)}, bf16[1,6,2,256,256]{4,3,2,1,0:T(8,128)(2,1)}, u32[]{:S(2)}) copy-start(bf16[1,6,2,256,256]{4,3,2,1,0:T(8,128)(2,1)} %refs_1_.3) | copy-start | bytes 4718596
  15.1 11.5 %collective-permute-start.2 = (bf16[256,256]{1,0:T(8,128)(2,1)S(1)}, bf16[256,256]{1,0:T(8,128)(2,1)S(1)}, u32[]{:S(2)}, u32[]{:S(2)}) collective-permute-start(bf16[256,256]{1,0:T(8,128)(2,1)S(1)} %get-tuple-element.61), channel_id=1, source_target_pairs={{0,1},{1,0},{2,3},{3,2},{4,5},{5,4},{6,7},{7,6},{8,9},{9,8},{10,11... | collective-permute-start | bytes 393224 | tf_op jit(solution)/shard_map/ppermute | solution.py:329
  19.1 7.5 %collective-permute-start.3 = (bf16[256,256]{1,0:T(8,128)(2,1)S(1)}, bf16[256,256]{1,0:T(8,128)(2,1)S(1)}, u32[]{:S(2)}, u32[]{:S(2)}) collective-permute-start(bf16[256,256]{1,0:T(8,128)(2,1)S(1)} %get-tuple-element.62), channel_id=1, source_target_pairs={{1,2},{2,1},{3,4},{4,3},{5,6},{6,5},{7,8},{8,7},{9,10},{10,9},{11,... | collective-permute-start | bytes 393224 | tf_op jit(solution)/shard_map/ppermute | solution.py:330
  21.8 14.1 %collective-permute-start.4 = (bf16[256,256]{1,0:T(8,128)(2,1)S(1)}, bf16[256,256]{1,0:T(8,128)(2,1)S(1)}, u32[]{:S(2)}, u32[]{:S(2)}) collective-permute-start(bf16[256,256]{1,0:T(8,128)(2,1)S(1)} %get-tuple-element.65), channel_id=1, source_target_pairs={{0,1},{1,0},{2,3},{3,2},{4,5},{5,4},{6,7},{7,6},{8,9},{9,8},{10,11... | collective-permute-start | bytes 393224 | tf_op jit(solution)/shard_map/ppermute | solution.py:329
  25.9 10.0 %collective-permute-start.5 = (bf16[256,256]{1,0:T(8,128)(2,1)S(1)}, bf16[256,256]{1,0:T(8,128)(2,1)S(1)}, u32[]{:S(2)}, u32[]{:S(2)}) collective-permute-start(bf16[256,256]{1,0:T(8,128)(2,1)S(1)} %get-tuple-element.66), channel_id=1, source_target_pairs={{1,2},{2,1},{3,4},{4,3},{5,6},{6,5},{7,8},{8,7},{9,10},{10,9},{11,... | collective-permute-start | bytes 393224 | tf_op jit(solution)/shard_map/ppermute | solution.py:330
  28.9 10.0 %collective-permute-start.6 = (bf16[256,256]{1,0:T(8,128)(2,1)S(1)}, bf16[256,256]{1,0:T(8,128)(2,1)S(1)}, u32[]{:S(2)}, u32[]{:S(2)}) collective-permute-start(bf16[256,256]{1,0:T(8,128)(2,1)S(1)} %get-tuple-element.69), channel_id=1, source_target_pairs={{0,1},{1,0},{2,3},{3,2},{4,5},{5,4},{6,7},{7,6},{8,9},{9,8},{10,11... | collective-permute-start | bytes 393224 | tf_op jit(solution)/shard_map/ppermute | solution.py:329
  35.2 3.7 %collective-permute-start.7 = (bf16[256,256]{1,0:T(8,128)(2,1)S(1)}, bf16[256,256]{1,0:T(8,128)(2,1)S(1)}, u32[]{:S(2)}, u32[]{:S(2)}) collective-permute-start(bf16[256,256]{1,0:T(8,128)(2,1)S(1)} %get-tuple-element.70), channel_id=1, source_target_pairs={{1,2},{2,1},{3,4},{4,3},{5,6},{6,5},{7,8},{8,7},{9,10},{10,9},{11,... | collective-permute-start | bytes 393224 | tf_op jit(solution)/shard_map/ppermute | solution.py:330
  40.3 22.1 %copy-start.8 = (bf16[1,6,2,256,256]{4,3,2,1,0:T(8,128)(2,1)S(1)}, bf16[1,6,2,256,256]{4,3,2,1,0:T(8,128)(2,1)}, u32[]{:S(2)}) copy-start(bf16[1,6,2,256,256]{4,3,2,1,0:T(8,128)(2,1)} %refs_1_.3) | copy-start | bytes 4718596
  58.9 9.2 %copy-start.3 = (bf16[1,2,2,256,256]{4,3,2,1,0:T(8,128)(2,1)S(1)}, bf16[1,2,2,256,256]{4,3,2,1,0:T(8,128)(2,1)}, u32[]{:S(2)}) copy-start(bf16[1,2,2,256,256]{4,3,2,1,0:T(8,128)(2,1)} %refs_2_.15) | copy-start | bytes 1572868
  58.9 9.2 %copy-start.6 = (bf16[1,2,2,256,256]{4,3,2,1,0:T(8,128)(2,1)S(1)}, bf16[1,2,2,256,256]{4,3,2,1,0:T(8,128)(2,1)}, u32[]{:S(2)}) copy-start(bf16[1,2,2,256,256]{4,3,2,1,0:T(8,128)(2,1)} %refs_3_.17) | copy-start | bytes 1572868
  58.9 9.2 %collective-permute-start.9 = (bf16[2,272,256]{2,1,0:T(8,128)(2,1)S(1)}, bf16[2,272,256]{2,1,0:T(8,128)(2,1)S(1)}, u32[]{:S(2)}, u32[]{:S(2)}) collective-permute-start(bf16[2,272,256]{2,1,0:T(8,128)(2,1)S(1)} %get-tuple-element.78.factor), channel_id=1, source_target_pairs={{0,16},{16,32},{32,48},{48,64},{64,80},{80,96},{96,112},{112,128},... | collective-permute-start | bytes 835592 | tf_op jit(solution)/shard_map/ppermute | solution.py:402
  61.0 10.7 %collective-permute-start.10 = (bf16[256,256]{1,0:T(8,128)(2,1)S(1)}, bf16[256,256]{1,0:T(8,128)(2,1)S(1)}, u32[]{:S(2)}, u32[]{:S(2)}) collective-permute-start(bf16[256,256]{1,0:T(8,128)(2,1)S(1)} %get-tuple-element.81), channel_id=1, source_target_pairs={{0,1},{1,0},{2,3},{3,2},{4,5},{5,4},{6,7},{7,6},{8,9},{9,8},{10,11... | collective-permute-start | bytes 393224 | tf_op jit(solution)/shard_map/ppermute | solution.py:329
  61.6 10.1 %collective-permute-start.11 = (bf16[256,256]{1,0:T(8,128)(2,1)S(1)}, bf16[256,256]{1,0:T(8,128)(2,1)S(1)}, u32[]{:S(2)}, u32[]{:S(2)}) collective-permute-start(bf16[256,256]{1,0:T(8,128)(2,1)S(1)} %get-tuple-element.82), channel_id=1, source_target_pairs={{1,2},{2,1},{3,4},{4,3},{5,6},{6,5},{7,8},{8,7},{9,10},{10,9},{11,... | collective-permute-start | bytes 393224 | tf_op jit(solution)/shard_map/ppermute | solution.py:330
  70.4 7.2 %collective-permute-start.12 = (bf16[256,256]{1,0:T(8,128)(2,1)S(1)}, bf16[256,256]{1,0:T(8,128)(2,1)S(1)}, u32[]{:S(2)}, u32[]{:S(2)}) collective-permute-start(bf16[256,256]{1,0:T(8,128)(2,1)S(1)} %get-tuple-element.86), channel_id=1, source_target_pairs={{0,1},{1,0},{2,3},{3,2},{4,5},{5,4},{6,7},{7,6},{8,9},{9,8},{10,11... | collective-permute-start | bytes 393224 | tf_op jit(solution)/shard_map/ppermute | solution.py:329
  71.0 6.6 %collective-permute-start.13 = (bf16[256,256]{1,0:T(8,128)(2,1)S(1)}, bf16[256,256]{1,0:T(8,128)(2,1)S(1)}, u32[]{:S(2)}, u32[]{:S(2)}) collective-permute-start(bf16[256,256]{1,0:T(8,128)(2,1)S(1)} %get-tuple-element.87), channel_id=1, source_target_pairs={{1,2},{2,1},{3,4},{4,3},{5,6},{6,5},{7,8},{8,7},{9,10},{10,9},{11,... | collective-permute-start | bytes 393224 | tf_op jit(solution)/shard_map/ppermute | solution.py:330
  73.5 11.0 %collective-permute-start.14 = (bf16[256,256]{1,0:T(8,128)(2,1)S(1)}, bf16[256,256]{1,0:T(8,128)(2,1)S(1)}, u32[]{:S(2)}, u32[]{:S(2)}) collective-permute-start(bf16[256,256]{1,0:T(8,128)(2,1)S(1)} %get-tuple-element.90), channel_id=1, source_target_pairs={{0,1},{1,0},{2,3},{3,2},{4,5},{5,4},{6,7},{7,6},{8,9},{9,8},{10,11... | collective-permute-start | bytes 393224 | tf_op jit(solution)/shard_map/ppermute | solution.py:329
  76.9 7.6 %collective-permute-start.15 = (bf16[256,256]{1,0:T(8,128)(2,1)S(1)}, bf16[256,256]{1,0:T(8,128)(2,1)S(1)}, u32[]{:S(2)}, u32[]{:S(2)}) collective-permute-start(bf16[256,256]{1,0:T(8,128)(2,1)S(1)} %get-tuple-element.91), channel_id=1, source_target_pairs={{1,2},{2,1},{3,4},{4,3},{5,6},{6,5},{7,8},{8,7},{9,10},{10,9},{11,... | collective-permute-start | bytes 393224 | tf_op jit(solution)/shard_map/ppermute | solution.py:330
  79.9 7.7 %collective-permute-start.16 = (bf16[256,256]{1,0:T(8,128)(2,1)S(1)}, bf16[256,256]{1,0:T(8,128)(2,1)S(1)}, u32[]{:S(2)}, u32[]{:S(2)}) collective-permute-start(bf16[256,256]{1,0:T(8,128)(2,1)S(1)} %get-tuple-element.94), channel_id=1, source_target_pairs={{0,1},{1,0},{2,3},{3,2},{4,5},{5,4},{6,7},{7,6},{8,9},{9,8},{10,11... | collective-permute-start | bytes 393224 | tf_op jit(solution)/shard_map/ppermute | solution.py:329
  83.8 3.7 %collective-permute-start.17 = (bf16[256,256]{1,0:T(8,128)(2,1)S(1)}, bf16[256,256]{1,0:T(8,128)(2,1)S(1)}, u32[]{:S(2)}, u32[]{:S(2)}) collective-permute-start(bf16[256,256]{1,0:T(8,128)(2,1)S(1)} %get-tuple-element.95), channel_id=1, source_target_pairs={{1,2},{2,1},{3,4},{4,3},{5,6},{6,5},{7,8},{8,7},{9,10},{10,9},{11,... | collective-permute-start | bytes 393224 | tf_op jit(solution)/shard_map/ppermute | solution.py:330
  (5 other events, 4.8 us)

commit v4 on v3

--- a/solution.py
+++ b/solution.py
@@ -38,12 +38,16 @@
     return jnp.where(jnp.logical_and(rows < dim, cols < dim), block, 0.0)
 
 
-def local_part(v, env, right, outer, inner, shift):
+def local_part(v, env, right, outer, inner, shift, ready=lambda *what: None):
     held = len(v)
     terms = right.shape[1]
     b = [x.astype(BF16) for x in v]
-    half = [[nt(b[s], right[0, w, s]).astype(BF16) for s in range(held)] for w in range(terms)]
+    half = []
+    for w in range(terms):
+        ready("right", w)
+        half.append([nt(b[s], right[0, w, s]).astype(BF16) for s in range(held)])
     image = [None] * held
+    ready("hops")
     for s in range(held):
         if s > 0:
             image[s] = hop(b[s - 1], inner[0, 0, s], outer[0, 0, s])
@@ -51,6 +55,7 @@
             above = hop(b[s + 1], inner[0, 1, s], outer[0, 1, s])
             image[s] = above if image[s] is None else image[s] + above
     for w in range(terms):
+        ready("left", w)
         for s in range(held):
             term = nn(env(w, s), half[w][s])
             image[s] = term if image[s] is None else image[s] + term
@@ -89,9 +94,11 @@
 
 
 def start_kernel(
-    place, dims, psi_at, outer_at, inner_at, v0, inside, across, facts, psi, blocks, arrived
+    place, dims_at, psi_at, outer_at, inner_at, v0, inside, across, facts, dims, psi, blocks, arrived
 ):
     held, cap, _ = psi.shape
+    known = pltpu.make_async_copy(dims_at, dims, arrived.at[held + 4])
+    known.start()
     copies = [pltpu.make_async_copy(psi_at.at[0, s], psi.at[s], arrived.at[s]) for s in range(held)]
     for n, (side, s) in enumerate(((0, 0), (1, held - 1))):
         for m, array in enumerate((outer_at, inner_at)):
@@ -102,6 +109,7 @@
             )
     for copy in copies:
         copy.start()
+    known.wait()
     first = place[0] * held
     last = dims.shape[1] - 1
     odd = place[0] % 2
@@ -135,11 +143,13 @@
         across[1 + m] = jnp.where(odd == 1, blocks[2 + m], blocks[m])
 
 
-def put_local(v, env, r, shift):
+def put_local(v, env, r, shift, **ready):
     facts = Facts(r["facts"])
-    out = local_part(v, env, r["right"], r["outer"], r["inner"], shift)
+    out = local_part(v, env, r["right"], r["outer"], r["inner"], shift, **ready)
     for s, block in enumerate(out):
         r["q"][s] = block
+    if "inside" not in r:
+        return
     inside, across = swapped(facts.odd, out[0], out[-1])
     r["inside"][...] = inside.astype(BF16)
     r["across"][...] = across.astype(BF16)
@@ -147,8 +157,26 @@
 
 def local_kernel(shift, names, *refs):
     r = dict(zip(names, refs))
+    arrived = refs[-1]
+    copies = {}
+    for n in ("outer", "inner"):
+        copies[n] = pltpu.make_async_copy(r[n + "_at"], r[n], arrived.at[len(copies)])
+    for n in ("right", "left"):
+        for w in range(r[n].shape[1]):
+            copies[n, w] = pltpu.make_async_copy(
+                r[n + "_at"].at[0, w], r[n].at[0, w], arrived.at[len(copies)]
+            )
+    order = [("right", w) for w in range(r["right"].shape[1])] + ["outer", "inner"]
+    order += [("left", w) for w in range(r["left"].shape[1])]
+    for key in order:
+        copies[key].start()
+
+    def ready(*what):
+        for key in ("outer", "inner") if what == ("hops",) else (what,):
+            copies[key].wait()
+
     v = [r["v0"][s] for s in range(r["v0"].shape[0])]
-    put_local(v, lambda w, s: r["left"][0, w, s], r, shift)
+    put_local(v, lambda w, s: r["left"][0, w, s], r, shift, ready=ready)
     r["dots"][...] = dot_rows([v], v)
 
 
@@ -254,11 +282,16 @@
     return (product / factor[cap : cap + 1].astype(F32)).astype(BF16)
 
 
-def grow_kernel(left, factor, out, token):
-    for s in range(left.shape[2]):
-        for w in range(left.shape[1]):
-            out[0, w, s] = grown(left[0, w, s], factor[s])
+def grow_kernel(left, factor, out, token, held_out, sent):
+    copies = []
+    for w in range(left.shape[1]):
+        for s in range(left.shape[2]):
+            held_out[w, s] = grown(left[0, w, s], factor[s])
+        copies.append(pltpu.make_async_copy(held_out.at[w], out.at[0, w], sent.at[w]))
+        copies[-1].start()
     token[...] = jnp.zeros_like(token)
+    for copy in copies:
+        copy.wait()
 
 
 def second_kernel(shift, names, *refs):
@@ -281,22 +314,34 @@
     facts = Facts(r["facts"])
     line = jnp.sum(r["lines"][...], axis=0)
     coefs, energy = combination(line, facts.row(facts.LIVE).astype(F32), shift)
+    held_out, sent = refs[-2:]
+    copies = []
     for s in range(r["v0"].shape[0]):
-        r["x"][0, s] = sum(c * r[f"v{k}"][s] for k, c in enumerate(coefs))
+        held_out[s] = sum(c * r[f"v{k}"][s] for k, c in enumerate(coefs))
+        copies.append(pltpu.make_async_copy(held_out.at[s], r["x"].at[0, s], sent.at[s]))
+        copies[-1].start()
     r["energy"][0] = energy[0, 0]
+    for copy in copies:
+        copy.wait()
+
+
+def in_hbm(array):
+    return pltpu.with_memory_space_constraint(array, pltpu.HBM)
 
 
 def struct(shape, dtype):
     return jax.ShapeDtypeStruct(shape, dtype)
 
 
-def call(kernel, name, ins, outs, flops=0, specs=None, scratch=()):
+def call(kernel, name, ins, outs, flops=0, specs=None, scratch=(), outside=()):
     args = tuple(ins.values())
     values = pl.pallas_call(
         kernel,
         out_shape=tuple(outs.values()),
         in_specs=specs or [VMEM] * len(args),
-        out_specs=tuple(SMEM if o.shape == (1,) else VMEM for o in outs.values()),
+        out_specs=tuple(
+            SMEM if o.shape == (1,) else HBM if n in outside else VMEM for n, o in outs.items()
+        ),
         scratch_shapes=scratch,
         name=name,
         compiler_params=pltpu.CompilerParams(vmem_limit_bytes=VMEM_LIMIT),
@@ -330,29 +375,35 @@
             "came_across": lax.ppermute(got["across"], "sec", others),
         }
 
-    def made(kernel, name, ins, outs, flops=0):
+    def made(kernel, name, ins, outs, flops=0, **more):
         names = tuple(ins) + tuple(outs)
-        return call(functools.partial(kernel, names), name, ins, outs, flops)
+        return call(functools.partial(kernel, names), name, ins, outs, flops, **more)
 
     start = call(
         start_kernel,
         "start",
-        {"place": place, "dims": dims, "psi": psi, "outer": hop_outer, "inner": hop_inner},
+        {
+            "place": place,
+            "dims": in_hbm(dims),
+            "psi": in_hbm(psi),
+            "outer": in_hbm(hop_outer),
+            "inner": in_hbm(hop_inner),
+        },
         {
             "v0": blocks,
             "inside": triple,
             "across": triple,
             "facts": struct((ROWS * (1 + (4 + held) // ROWS), LANES), jnp.int32),
         },
-        specs=[SMEM, SMEM, HBM, HBM, HBM],
+        specs=[SMEM, HBM, HBM, HBM, HBM],
         scratch=[
+            pltpu.SMEM(dims.shape, jnp.int32),
             pltpu.VMEM((held, cap, cap), F32),
             pltpu.VMEM((4, cap, cap), BF16),
-            pltpu.SemaphoreType.DMA((held + 4,)),
+            pltpu.SemaphoreType.DMA((held + 5,)),
         ],
     )
     facts = start["facts"]
-    common = {"facts": facts, "outer": hop_outer, "inner": hop_inner, "right": right_env}
     came = exchange(start)
     hops = {"hops_inside": came["came_inside"], "hops_across": came["came_across"]}
     earlier = lax.ppermute(left_env, "seg", onward)
@@ -368,6 +419,8 @@
                 came = exchange(got)
                 ins.update(left=env)
                 outs = {"v": blocks, **local_outs}
+                if k + 2 == ITERS:
+                    del outs["inside"], outs["across"]
             else:
                 del ins["right"]
                 ins.update(dots)
@@ -382,11 +435,28 @@
     got = made(
         functools.partial(local_kernel, shift),
         "local",
-        {"v0": start["v0"], "left": left_env, **common},
-        local_outs,
+        {
+            "facts": facts,
+            "v0": start["v0"],
+            "left_at": in_hbm(left_env),
+            "right_at": in_hbm(right_env),
+            "outer_at": in_hbm(hop_outer),
+            "inner_at": in_hbm(hop_inner),
+        },
+        {
+            "left": struct(left_env.shape, BF16),
+            "right": struct(right_env.shape, BF16),
+            "outer": struct(hop_outer.shape, BF16),
+            "inner": struct(hop_inner.shape, BF16),
+            **local_outs,
+        },
         flops=one * 28,
-    )
-    basis, lines = relaxed(start["v0"], came, got, left_env)
+        specs=[VMEM, VMEM, HBM, HBM, HBM, HBM],
+        scratch=[pltpu.SemaphoreType.DMA((2 + 2 * terms,))],
+    )
+    left = got["left"]
+    common = {"facts": facts, **{n: got[n] for n in ("outer", "inner", "right")}}
+    basis, lines = relaxed(start["v0"], came, got, left)
     joined = made(
         functools.partial(join_kernel, shift),
         "join",
@@ -404,16 +474,21 @@
     renewed = call(
         grow_kernel,
         "grow",
-        {"left": left_env, "factor": factor},
+        {"left": left, "factor": factor},
         {"out": struct(left_env.shape, BF16), "token": dots_of},
         flops=one * 24,
+        scratch=[
+            pltpu.VMEM((terms, held, cap, cap), BF16),
+            pltpu.SemaphoreType.DMA((terms,)),
+        ],
+        outside=("out",),
     )
     got = made(
         functools.partial(second_kernel, shift),
         "second",
         {
             "v0": joined["x"],
-            "left": left_env,
+            "left": left,
             "earlier": earlier,
             "factor": earlier_factor,
             "token": renewed["token"],
@@ -428,6 +503,8 @@
         "finish",
         {"facts": facts, "lines": lines, **basis},
         {"x": struct(psi.shape, F32), "energy": struct((1,), F32)},
+        scratch=[pltpu.VMEM((held, cap, cap), F32), pltpu.SemaphoreType.DMA((held,))],
+        outside=("x",),
     )
     return (done["x"], done["energy"], renewed["out"])
 

time: 108 us -> 105 us (0.972)
  local copies, waits for them, and re-layouts: 7.28 us -> 0 us
  Pallas kernels: 26.3 us -> 27.9 us
  waiting for transfers between devices: 3.58 us -> 4.92 us
    unnamed x22 -> x0, local copies, waits for them, and re-layouts: 7.28 us -> none
    pallas_call x14, Pallas kernels: 26.3 us -> 27.9 us  [call(): pl.pallas_call(kernel, out_shape=tuple(outs.values()), in_specs=specs or...]
  transfers between devices with their start and end apart: 18 -> 18, of which waited for: 2 -> 2; matrix products, arithmetic and copies ran while one was open for 0% -> 0% of each run, Pallas kernels for 22% -> 24%
where the time goes in v4:
time: 105 us; the launch traced here: 104 us
  blocking collectives  35.8 us (34%)
  starting transfers between devices  34.1 us (32%)
  Pallas kernels  27.9 us (27%)
  waiting for transfers between devices  4.92 us (5%)
  between operations  1.07 us (1%)
    all_to_all x2, blocking collectives, relaxed(): return (basis, lax.all_to_all(got['line'], 'sec', 0, 0))  35.8 us
    pallas_call x14, Pallas kernels, call(): pl.pallas_call(kernel, out_shape=tuple(outs.values()), in_specs=specs or...  27.9 us
    ppermute x8, starting transfers between devices, exchange(): lax.ppermute(got['inside'], 'sec', pairs)  24.8 us
    ppermute x8, starting transfers between devices, exchange(): lax.ppermute(got['across'], 'sec', others)  5.45 us
    ppermute x1, waiting for transfers between devices, body(): earlier_factor = lax.ppermute(factor, 'seg', onward)  3.73 us
  transfers between devices with their start and end apart: 18, of which 2 were waited for; matrix products, arithmetic and copies ran while one was open for 0% of the time, Pallas kernels for 24%

profile of v4, /device:TPU:128, one launch (start us, length us, event | category | flops | bytes accessed | tf_op | source)
XLA Modules:
  0.0 103.8 jit_solution(12503690057281971373)
XLA Ops:
  0.6 1.9 %collective-permute-start.8 = (bf16[1,6,2,256,256]{4,3,2,1,0:T(8,128)(2,1)}, bf16[1,6,2,256,256]{4,3,2,1,0:T(8,128)(2,1)S(1)}, u32[]{:S(2)}, u32[]{:S(2)}) collective-permute-start(bf16[1,6,2,256,256]{4,3,2,1,0:T(8,128)(2,1)} %refs_2_.1), channel_id=1, source_target_pairs={{0,16},{16,32},{32,48},{48,64},{64,80},{80,96},{96,112},{112,128},... | collective-permute-start | bytes 4718600 | tf_op jit(solution)/shard_map/ppermute | solution.py:409
  2.6 1.8 %start.1 = (f32[2,256,256]{2,1,0:T(8,128)S(1)}, bf16[3,256,256]{2,1,0:T(8,128)(2,1)S(1)}, bf16[3,256,256]{2,1,0:T(8,128)(2,1)S(1)}, s32[8,128]{1,0:T(8,128)S(1)}) custom-call(s32[2]{0:T(128)S(1)} %pad_add_fusion.place, s32[1,32]{1,0:T(1,128)} %dims_at.1, f32[1,2,256,256]{3,2,1,0:T(8,128)} %psi_at.1, bf16[1,2,2,256,256]{4,3,2,1,0:T(8,128)(2,1)} %refs_4_.1, ...), custom_call_target="tpu_custom_call" | custom-call | bytes 1573000 | tf_op jit(solution)/shard_map/start/pallas_call | solution.py:338
  4.5 1.6 %collective-permute-start = (bf16[3,256,256]{2,1,0:T(8,128)(2,1)S(1)}, bf16[3,256,256]{2,1,0:T(8,128)(2,1)S(1)}, u32[]{:S(2)}, u32[]{:S(2)}) collective-permute-start(bf16[3,256,256]{2,1,0:T(8,128)(2,1)S(1)} %get-tuple-element.64), channel_id=1, source_target_pairs={{0,1},{1,0},{2,3},{3,2},{4,5},{5,4},{6,7},{7,6},{8,9},{9,8},{10,11... | collective-permute-start | bytes 1179656 | tf_op jit(solution)/shard_map/ppermute | solution.py:374
  6.7 3.8 %local.1 = (bf16[1,6,2,256,256]{4,3,2,1,0:T(8,128)(2,1)S(1)}, bf16[1,6,2,256,256]{4,3,2,1,0:T(8,128)(2,1)S(1)}, bf16[1,2,2,256,256]{4,3,2,1,0:T(8,128)(2,1)S(1)}...) custom-call(s32[8,128]{1,0:T(8,128)S(1)} %get-tuple-element.58.refs_, ...), custom_call_target="tpu_custom_call" | custom-call | flops 939524096 | bytes 4722688 | tf_op jit(solution)/shard_map/local/pallas_call | solution.py:338
  10.6 4.0 %collective-permute-start.2 = (bf16[256,256]{1,0:T(8,128)(2,1)S(1)}, bf16[256,256]{1,0:T(8,128)(2,1)S(1)}, u32[]{:S(2)}, u32[]{:S(2)}) collective-permute-start(bf16[256,256]{1,0:T(8,128)(2,1)S(1)} %get-tuple-element.69), channel_id=1, source_target_pairs={{0,1},{1,0},{2,3},{3,2},{4,5},{5,4},{6,7},{7,6},{8,9},{9,8},{10,11... | collective-permute-start | bytes 393224 | tf_op jit(solution)/shard_map/ppermute | solution.py:374
  16.4 1.8 %step0.2 = (f32[2,256,256]{2,1,0:T(8,128)S(1)}, f32[2,256,256]{2,1,0:T(8,128)S(1)}, bf16[256,256]{1,0:T(8,128)(2,1)S(1)}, bf16[256,256]{1,0:T(8,128)(2,1)S(1)}, f32[8,128]{1,0:T(8,128)S(1)}) custom-call(f32[2,256,256]{2,1,0:T(8,128)S(1)} %get-tuple-element.60.refs_0_, s32[8,128]{1,0:T(8,128)S(1)} %get-tuple-element.58.refs_0_.refs_1_.refs_5_, ...), custom_call_target="tpu_custom_call" | custom-call | flops 1207959552 | bytes 6033408 | tf_op jit(solution)/shard_map/step0/pallas_call | solution.py:338
  18.2 4.1 %collective-permute-start.4 = (bf16[256,256]{1,0:T(8,128)(2,1)S(1)}, bf16[256,256]{1,0:T(8,128)(2,1)S(1)}, u32[]{:S(2)}, u32[]{:S(2)}) collective-permute-start(bf16[256,256]{1,0:T(8,128)(2,1)S(1)} %get-tuple-element.73), channel_id=1, source_target_pairs={{0,1},{1,0},{2,3},{3,2},{4,5},{5,4},{6,7},{7,6},{8,9},{9,8},{10,11... | collective-permute-start | bytes 393224 | tf_op jit(solution)/shard_map/ppermute | solution.py:374
  23.0 2.3 %step1.2 = (f32[2,256,256]{2,1,0:T(8,128)S(1)}, f32[2,256,256]{2,1,0:T(8,128)S(1)}, bf16[256,256]{1,0:T(8,128)(2,1)S(1)}, bf16[256,256]{1,0:T(8,128)(2,1)S(1)}, f32[8,128]{1,0:T(8,128)S(1)}) custom-call(f32[2,256,256]{2,1,0:T(8,128)S(1)} %get-tuple-element.67.refs_0_, s32[8,128]{1,0:T(8,128)S(1)} %get-tuple-element.58.refs_0_.refs_1_.refs_5_, ...), custom_call_target="tpu_custom_call" | custom-call | flops 1207959552 | bytes 6819840 | tf_op jit(solution)/shard_map/step1/pallas_call | solution.py:338
  25.3 6.4 %collective-permute-start.6 = (bf16[256,256]{1,0:T(8,128)(2,1)S(1)}, bf16[256,256]{1,0:T(8,128)(2,1)S(1)}, u32[]{:S(2)}, u32[]{:S(2)}) collective-permute-start(bf16[256,256]{1,0:T(8,128)(2,1)S(1)} %get-tuple-element.77), channel_id=1, source_target_pairs={{0,1},{1,0},{2,3},{3,2},{4,5},{5,4},{6,7},{7,6},{8,9},{9,8},{10,11... | collective-permute-start | bytes 393224 | tf_op jit(solution)/shard_map/ppermute | solution.py:374
  32.5 2.4 %step2.2 = (f32[2,256,256]{2,1,0:T(8,128)S(1)}, f32[2,256,256]{2,1,0:T(8,128)S(1)}, f32[8,128]{1,0:T(8,128)S(1)}) custom-call(f32[2,256,256]{2,1,0:T(8,128)S(1)} %get-tuple-element.71.refs_0_, s32[8,128]{1,0:T(8,128)S(1)} %get-tuple-element.58.refs_0_.refs_1_.refs_5_, bf16[1,2,2,256,256]{4,3,2,1,0:T(8,128)(2,1)S(1)} %get-tuple-element.61.refs_2_.refs_6_, ...), custom_call_target="tpu_custom_call" | custom-call | flops 1207959552 | bytes 7344128 | tf_op jit(solution)/shard_map/step2/pallas_call | solution.py:338
  34.8 1.4 %step3.2 = (f32[2,256,256]{2,1,0:T(8,128)S(1)}, f32[16,1,128]{2,1,0:T(1,128)S(1)}) custom-call(f32[2,256,256]{2,1,0:T(8,128)S(1)} %get-tuple-element.75.refs_0_, s32[8,128]{1,0:T(8,128)S(1)} %get-tuple-element.58.refs_0_.refs_1_.refs_5_, bf16[1,2,2,256,256]{4,3,2,1,0:T(8,128)(2,1)S(1)} %get-tuple-element.61.refs_2_.refs_6_, ...), custom_call_target="tpu_custom_call" | custom-call | flops 1207959552 | bytes 4739072 | tf_op jit(solution)/shard_map/step3/pallas_call | solution.py:338
  36.2 18.4 %all_to_all.10.refs_1_ = f32[16,1,128]{2,1,0:T(1,128)S(1)} all-to-all(f32[16,1,128]{2,1,0:T(1,128)S(1)} %get-tuple-element.83), channel_id=1, replica_groups=mesh['seg'=16,'sec'=16] {'sec'}, dimensions={0} | all-to-all | bytes 16384 | tf_op jit(solution)/shard_map/all_to_all | solution.py:433
  55.3 1.9 %collective-permute-start.9 = (bf16[2,272,256]{2,1,0:T(8,128)(2,1)S(1)}, bf16[2,272,256]{2,1,0:T(8,128)(2,1)S(1)}, u32[]{:S(2)}, u32[]{:S(2)}) collective-permute-start(bf16[2,272,256]{2,1,0:T(8,128)(2,1)S(1)} %get-tuple-element.86.factor), channel_id=1, source_target_pairs={{0,16},{16,32},{32,48},{48,64},{64,80},{80,96},{96,112},{112,128},... | collective-permute-start | bytes 835592 | tf_op jit(solution)/shard_map/ppermute | solution.py:472
  58.7 1.9 %grow.1 = (bf16[1,6,2,256,256]{4,3,2,1,0:T(8,128)(2,1)}, f32[8,128]{1,0:T(8,128)S(1)}) custom-call(bf16[1,6,2,256,256]{4,3,2,1,0:T(8,128)(2,1)S(1)} %get-tuple-element.66.refs_8_.refs_11_.refs_12_.left.refs_1_, bf16[2,272,256]{2,1,0:T(8,128)(2,1)S(1)} %get-tuple-element.86.factor), custom_call_target="tpu_custom_call" | custom-call | flops 805306368 | bytes 1851392 | tf_op jit(solution)/shard_map/grow/pallas_call | solution.py:338
  60.6 3.7 %collective-permute-done.9.refs_3_ = bf16[2,272,256]{2,1,0:T(8,128)(2,1)S(1)} collective-permute-done((bf16[2,272,256]{2,1,0:T(8,128)(2,1)S(1)}, bf16[2,272,256]{2,1,0:T(8,128)(2,1)S(1)}, u32[]{:S(2)}, u32[]{:S(2)}) %collective-permute-start.9) | collective-permute-done | bytes 278560 | tf_op jit(solution)/shard_map/ppermute | solution.py:472
  64.4 2.2 %second.1 = (bf16[6,2,256,256]{3,2,1,0:T(8,128)(2,1)S(1)}, f32[2,256,256]{2,1,0:T(8,128)S(1)}, bf16[256,256]{1,0:T(8,128)(2,1)S(1)}, bf16[256,256]{1,0:T(8,128)(2,1)S(1)}, f32[8,128]{1,0:T(8,128)S(1)}) custom-call(f32[2,256,256]{2,1,0:T(8,128)S(1)} %get-tuple-element.85.refs_0_.refs_5_.refs_4_.refs_2_, ...), custom_call_target="tpu_custom_call" | custom-call | flops 1744830464 | bytes 6578176 | tf_op jit(solution)/shard_map/second/pallas_call | solution.py:338
  67.9 1.8 %step0.3 = (f32[2,256,256]{2,1,0:T(8,128)S(1)}, f32[2,256,256]{2,1,0:T(8,128)S(1)}, bf16[256,256]{1,0:T(8,128)(2,1)S(1)}, bf16[256,256]{1,0:T(8,128)(2,1)S(1)}, f32[8,128]{1,0:T(8,128)S(1)}) custom-call(f32[2,256,256]{2,1,0:T(8,128)S(1)} %get-tuple-element.88.refs_0_, s32[8,128]{1,0:T(8,128)S(1)} %get-tuple-element.58.refs_0_.refs_1_.refs_5_, ...), custom_call_target="tpu_custom_call" | custom-call | flops 1207959552 | bytes 5509120 | tf_op jit(solution)/shard_map/step0/pallas_call | solution.py:338
  69.8 3.4 %collective-permute-start.14 = (bf16[256,256]{1,0:T(8,128)(2,1)S(1)}, bf16[256,256]{1,0:T(8,128)(2,1)S(1)}, u32[]{:S(2)}, u32[]{:S(2)}) collective-permute-start(bf16[256,256]{1,0:T(8,128)(2,1)S(1)} %get-tuple-element.98), channel_id=1, source_target_pairs={{0,1},{1,0},{2,3},{3,2},{4,5},{5,4},{6,7},{7,6},{8,9},{9,8},{10,11... | collective-permute-start | bytes 393224 | tf_op jit(solution)/shard_map/ppermute | solution.py:374
  73.8 2.3 %step1.3 = (f32[2,256,256]{2,1,0:T(8,128)S(1)}, f32[2,256,256]{2,1,0:T(8,128)S(1)}, bf16[256,256]{1,0:T(8,128)(2,1)S(1)}, bf16[256,256]{1,0:T(8,128)(2,1)S(1)}, f32[8,128]{1,0:T(8,128)S(1)}) custom-call(f32[2,256,256]{2,1,0:T(8,128)S(1)} %get-tuple-element.92.refs_0_, s32[8,128]{1,0:T(8,128)S(1)} %get-tuple-element.58.refs_0_.refs_1_.refs_5_, ...), custom_call_target="tpu_custom_call" | custom-call | flops 1207959552 | bytes 6819840 | tf_op jit(solution)/shard_map/step1/pallas_call | solution.py:338
  76.1 4.0 %collective-permute-start.16 = (bf16[256,256]{1,0:T(8,128)(2,1)S(1)}, bf16[256,256]{1,0:T(8,128)(2,1)S(1)}, u32[]{:S(2)}, u32[]{:S(2)}) collective-permute-start(bf16[256,256]{1,0:T(8,128)(2,1)S(1)} %get-tuple-element.102), channel_id=1, source_target_pairs={{0,1},{1,0},{2,3},{3,2},{4,5},{5,4},{6,7},{7,6},{8,9},{9,8},{10,11... | collective-permute-start | bytes 393224 | tf_op jit(solution)/shard_map/ppermute | solution.py:374
  80.8 2.3 %step2.3 = (f32[2,256,256]{2,1,0:T(8,128)S(1)}, f32[2,256,256]{2,1,0:T(8,128)S(1)}, f32[8,128]{1,0:T(8,128)S(1)}) custom-call(f32[2,256,256]{2,1,0:T(8,128)S(1)} %get-tuple-element.96.refs_0_, s32[8,128]{1,0:T(8,128)S(1)} %get-tuple-element.58.refs_0_.refs_1_.refs_5_, bf16[1,2,2,256,256]{4,3,2,1,0:T(8,128)(2,1)S(1)} %get-tuple-element.61.refs_2_.refs_6_, ...), custom_call_target="tpu_custom_call" | custom-call | flops 1207959552 | bytes 7344128 | tf_op jit(solution)/shard_map/step2/pallas_call | solution.py:338
  83.1 1.4 %step3.3 = (f32[2,256,256]{2,1,0:T(8,128)S(1)}, f32[16,1,128]{2,1,0:T(1,128)S(1)}) custom-call(f32[2,256,256]{2,1,0:T(8,128)S(1)} %get-tuple-element.100.refs_0_, s32[8,128]{1,0:T(8,128)S(1)} %get-tuple-element.58.refs_0_.refs_1_.refs_5_, bf16[1,2,2,256,256]{4,3,2,1,0:T(8,128)(2,1)S(1)} %get-tuple-element.61.refs_2_.refs_6_, ...), custom_call_target="tpu_custom_call" | custom-call | flops 1207959552 | bytes 4739072 | tf_op jit(solution)/shard_map/step3/pallas_call | solution.py:338
  84.5 17.3 %all_to_all.11.refs_1_ = f32[16,1,128]{2,1,0:T(1,128)S(1)} all-to-all(f32[16,1,128]{2,1,0:T(1,128)S(1)} %get-tuple-element.108), channel_id=1, replica_groups=mesh['seg'=16,'sec'=16] {'sec'}, dimensions={0} | all-to-all | bytes 16384 | tf_op jit(solution)/shard_map/all_to_all | solution.py:433
  101.9 1.8 %finish.1 = (f32[1,2,256,256]{3,2,1,0:T(8,128)}, f32[1]{0:T(128)}) custom-call(s32[8,128]{1,0:T(8,128)S(1)} %get-tuple-element.58.refs_0_.refs_1_.refs_5_, f32[16,1,128]{2,1,0:T(1,128)S(1)} %all_to_all.11.refs_1_, f32[2,256,256]{2,1,0:T(8,128)S(1)} %get-tuple-element.85.refs_0_.refs_5_.refs_4_.refs_2_, ...), custom_call_target="tpu_custom_call" | custom-call | bytes 2633728 | tf_op jit(solution)/shard_map/finish/pallas_call | solution.py:338
  (29 shorter events, 8.7 us)
Async XLA Ops:
  0.6 63.8 %collective-permute-start.8 = (bf16[1,6,2,256,256]{4,3,2,1,0:T(8,128)(2,1)}, bf16[1,6,2,256,256]{4,3,2,1,0:T(8,128)(2,1)S(1)}, u32[]{:S(2)}, u32[]{:S(2)}) collective-permute-start(bf16[1,6,2,256,256]{4,3,2,1,0:T(8,128)(2,1)} %refs_2_.1), channel_id=1, source_target_pairs={{0,16},{16,32},{32,48},{48,64},{64,80},{80,96},{96,112},{112,128},... | collective-permute-start | bytes 4718600 | tf_op jit(solution)/shard_map/ppermute | solution.py:409
  4.5 11.9 %collective-permute-start = (bf16[3,256,256]{2,1,0:T(8,128)(2,1)S(1)}, bf16[3,256,256]{2,1,0:T(8,128)(2,1)S(1)}, u32[]{:S(2)}, u32[]{:S(2)}) collective-permute-start(bf16[3,256,256]{2,1,0:T(8,128)(2,1)S(1)} %get-tuple-element.64), channel_id=1, source_target_pairs={{0,1},{1,0},{2,3},{3,2},{4,5},{5,4},{6,7},{7,6},{8,9},{9,8},{10,11... | collective-permute-start | bytes 1179656 | tf_op jit(solution)/shard_map/ppermute | solution.py:374
  6.0 10.3 %collective-permute-start.1 = (bf16[3,256,256]{2,1,0:T(8,128)(2,1)S(1)}, bf16[3,256,256]{2,1,0:T(8,128)(2,1)S(1)}, u32[]{:S(2)}, u32[]{:S(2)}) collective-permute-start(bf16[3,256,256]{2,1,0:T(8,128)(2,1)S(1)} %get-tuple-element.65), channel_id=1, source_target_pairs={{1,2},{2,1},{3,4},{4,3},{5,6},{6,5},{7,8},{8,7},{9,10},{10,9},{11,... | collective-permute-start | bytes 1179656 | tf_op jit(solution)/shard_map/ppermute | solution.py:375
  10.6 12.5 %collective-permute-start.2 = (bf16[256,256]{1,0:T(8,128)(2,1)S(1)}, bf16[256,256]{1,0:T(8,128)(2,1)S(1)}, u32[]{:S(2)}, u32[]{:S(2)}) collective-permute-start(bf16[256,256]{1,0:T(8,128)(2,1)S(1)} %get-tuple-element.69), channel_id=1, source_target_pairs={{0,1},{1,0},{2,3},{3,2},{4,5},{5,4},{6,7},{7,6},{8,9},{9,8},{10,11... | collective-permute-start | bytes 393224 | tf_op jit(solution)/shard_map/ppermute | solution.py:374
  14.6 8.5 %collective-permute-start.3 = (bf16[256,256]{1,0:T(8,128)(2,1)S(1)}, bf16[256,256]{1,0:T(8,128)(2,1)S(1)}, u32[]{:S(2)}, u32[]{:S(2)}) collective-permute-start(bf16[256,256]{1,0:T(8,128)(2,1)S(1)} %get-tuple-element.70), channel_id=1, source_target_pairs={{1,2},{2,1},{3,4},{4,3},{5,6},{6,5},{7,8},{8,7},{9,10},{10,9},{11,... | collective-permute-start | bytes 393224 | tf_op jit(solution)/shard_map/ppermute | solution.py:375
  18.2 14.2 %collective-permute-start.4 = (bf16[256,256]{1,0:T(8,128)(2,1)S(1)}, bf16[256,256]{1,0:T(8,128)(2,1)S(1)}, u32[]{:S(2)}, u32[]{:S(2)}) collective-permute-start(bf16[256,256]{1,0:T(8,128)(2,1)S(1)} %get-tuple-element.73), channel_id=1, source_target_pairs={{0,1},{1,0},{2,3},{3,2},{4,5},{5,4},{6,7},{7,6},{8,9},{9,8},{10,11... | collective-permute-start | bytes 393224 | tf_op jit(solution)/shard_map/ppermute | solution.py:374
  22.4 10.1 %collective-permute-start.5 = (bf16[256,256]{1,0:T(8,128)(2,1)S(1)}, bf16[256,256]{1,0:T(8,128)(2,1)S(1)}, u32[]{:S(2)}, u32[]{:S(2)}) collective-permute-start(bf16[256,256]{1,0:T(8,128)(2,1)S(1)} %get-tuple-element.74), channel_id=1, source_target_pairs={{1,2},{2,1},{3,4},{4,3},{5,6},{6,5},{7,8},{8,7},{9,10},{10,9},{11,... | collective-permute-start | bytes 393224 | tf_op jit(solution)/shard_map/ppermute | solution.py:375
  25.3 9.5 %collective-permute-start.6 = (bf16[256,256]{1,0:T(8,128)(2,1)S(1)}, bf16[256,256]{1,0:T(8,128)(2,1)S(1)}, u32[]{:S(2)}, u32[]{:S(2)}) collective-permute-start(bf16[256,256]{1,0:T(8,128)(2,1)S(1)} %get-tuple-element.77), channel_id=1, source_target_pairs={{0,1},{1,0},{2,3},{3,2},{4,5},{5,4},{6,7},{7,6},{8,9},{9,8},{10,11... | collective-permute-start | bytes 393224 | tf_op jit(solution)/shard_map/ppermute | solution.py:374
  31.8 3.1 %collective-permute-start.7 = (bf16[256,256]{1,0:T(8,128)(2,1)S(1)}, bf16[256,256]{1,0:T(8,128)(2,1)S(1)}, u32[]{:S(2)}, u32[]{:S(2)}) collective-permute-start(bf16[256,256]{1,0:T(8,128)(2,1)S(1)} %get-tuple-element.78), channel_id=1, source_target_pairs={{1,2},{2,1},{3,4},{4,3},{5,6},{6,5},{7,8},{8,7},{9,10},{10,9},{11,... | collective-permute-start | bytes 393224 | tf_op jit(solution)/shard_map/ppermute | solution.py:375
  55.3 9.1 %collective-permute-start.9 = (bf16[2,272,256]{2,1,0:T(8,128)(2,1)S(1)}, bf16[2,272,256]{2,1,0:T(8,128)(2,1)S(1)}, u32[]{:S(2)}, u32[]{:S(2)}) collective-permute-start(bf16[2,272,256]{2,1,0:T(8,128)(2,1)S(1)} %get-tuple-element.86.factor), channel_id=1, source_target_pairs={{0,16},{16,32},{32,48},{48,64},{64,80},{80,96},{96,112},{112,128},... | collective-permute-start | bytes 835592 | tf_op jit(solution)/shard_map/ppermute | solution.py:472
  57.2 10.7 %collective-permute-start.10 = (bf16[256,256]{1,0:T(8,128)(2,1)S(1)}, bf16[256,256]{1,0:T(8,128)(2,1)S(1)}, u32[]{:S(2)}, u32[]{:S(2)}) collective-permute-start(bf16[256,256]{1,0:T(8,128)(2,1)S(1)} %get-tuple-element.89), channel_id=1, source_target_pairs={{0,1},{1,0},{2,3},{3,2},{4,5},{5,4},{6,7},{7,6},{8,9},{9,8},{10,11... | collective-permute-start | bytes 393224 | tf_op jit(solution)/shard_map/ppermute | solution.py:374
  57.9 10.1 %collective-permute-start.11 = (bf16[256,256]{1,0:T(8,128)(2,1)S(1)}, bf16[256,256]{1,0:T(8,128)(2,1)S(1)}, u32[]{:S(2)}, u32[]{:S(2)}) collective-permute-start(bf16[256,256]{1,0:T(8,128)(2,1)S(1)} %get-tuple-element.90), channel_id=1, source_target_pairs={{1,2},{2,1},{3,4},{4,3},{5,6},{6,5},{7,8},{8,7},{9,10},{10,9},{11,... | collective-permute-start | bytes 393224 | tf_op jit(solution)/shard_map/ppermute | solution.py:375
  66.6 7.2 %collective-permute-start.12 = (bf16[256,256]{1,0:T(8,128)(2,1)S(1)}, bf16[256,256]{1,0:T(8,128)(2,1)S(1)}, u32[]{:S(2)}, u32[]{:S(2)}) collective-permute-start(bf16[256,256]{1,0:T(8,128)(2,1)S(1)} %get-tuple-element.94), channel_id=1, source_target_pairs={{0,1},{1,0},{2,3},{3,2},{4,5},{5,4},{6,7},{7,6},{8,9},{9,8},{10,11... | collective-permute-start | bytes 393224 | tf_op jit(solution)/shard_map/ppermute | solution.py:374
  67.3 6.6 %collective-permute-start.13 = (bf16[256,256]{1,0:T(8,128)(2,1)S(1)}, bf16[256,256]{1,0:T(8,128)(2,1)S(1)}, u32[]{:S(2)}, u32[]{:S(2)}) collective-permute-start(bf16[256,256]{1,0:T(8,128)(2,1)S(1)} %get-tuple-element.95), channel_id=1, source_target_pairs={{1,2},{2,1},{3,4},{4,3},{5,6},{6,5},{7,8},{8,7},{9,10},{10,9},{11,... | collective-permute-start | bytes 393224 | tf_op jit(solution)/shard_map/ppermute | solution.py:375
  69.8 11.0 %collective-permute-start.14 = (bf16[256,256]{1,0:T(8,128)(2,1)S(1)}, bf16[256,256]{1,0:T(8,128)(2,1)S(1)}, u32[]{:S(2)}, u32[]{:S(2)}) collective-permute-start(bf16[256,256]{1,0:T(8,128)(2,1)S(1)} %get-tuple-element.98), channel_id=1, source_target_pairs={{0,1},{1,0},{2,3},{3,2},{4,5},{5,4},{6,7},{7,6},{8,9},{9,8},{10,11... | collective-permute-start | bytes 393224 | tf_op jit(solution)/shard_map/ppermute | solution.py:374
  73.1 7.6 %collective-permute-start.15 = (bf16[256,256]{1,0:T(8,128)(2,1)S(1)}, bf16[256,256]{1,0:T(8,128)(2,1)S(1)}, u32[]{:S(2)}, u32[]{:S(2)}) collective-permute-start(bf16[256,256]{1,0:T(8,128)(2,1)S(1)} %get-tuple-element.99), channel_id=1, source_target_pairs={{1,2},{2,1},{3,4},{4,3},{5,6},{6,5},{7,8},{8,7},{9,10},{10,9},{11,... | collective-permute-start | bytes 393224 | tf_op jit(solution)/shard_map/ppermute | solution.py:375
  76.1 7.0 %collective-permute-start.16 = (bf16[256,256]{1,0:T(8,128)(2,1)S(1)}, bf16[256,256]{1,0:T(8,128)(2,1)S(1)}, u32[]{:S(2)}, u32[]{:S(2)}) collective-permute-start(bf16[256,256]{1,0:T(8,128)(2,1)S(1)} %get-tuple-element.102), channel_id=1, source_target_pairs={{0,1},{1,0},{2,3},{3,2},{4,5},{5,4},{6,7},{7,6},{8,9},{9,8},{10,11... | collective-permute-start | bytes 393224 | tf_op jit(solution)/shard_map/ppermute | solution.py:374
  80.1 3.0 %collective-permute-start.17 = (bf16[256,256]{1,0:T(8,128)(2,1)S(1)}, bf16[256,256]{1,0:T(8,128)(2,1)S(1)}, u32[]{:S(2)}, u32[]{:S(2)}) collective-permute-start(bf16[256,256]{1,0:T(8,128)(2,1)S(1)} %get-tuple-element.103), channel_id=1, source_target_pairs={{1,2},{2,1},{3,4},{4,3},{5,6},{6,5},{7,8},{8,7},{9,10},{10,9},{11,... | collective-permute-start | bytes 393224 | tf_op jit(solution)/shard_map/ppermute | solution.py:375

commit v5 on v4

--- a/solution.py
+++ b/solution.py
@@ -113,8 +113,8 @@
     first = place[0] * held
     last = dims.shape[1] - 1
     odd = place[0] % 2
-    low_dim = dims[0, jnp.maximum(first - 1, 0)]
-    high_dim = dims[0, jnp.minimum(first + held, last)]
+    low_dim = jnp.where(first == 0, 0, dims[0, jnp.maximum(first - 1, 0)])
+    high_dim = jnp.where(first + held > last, 0, dims[0, jnp.minimum(first + held, last)])
     live = jnp.int32(0)
     for s in range(dims.shape[1]):
         live = live + dims[0, s] * dims[0, s]
@@ -181,19 +181,21 @@
 
 
 def ghosts(k, facts, r):
-    came = [r["came_inside"], r["came_across"]]
-    came = [(c[0] if len(c.shape) == 3 else c[...]).astype(F32) for c in came]
-    if k > 0:
-        before = r[f"v{k - 1}"]
-        sent = swapped(facts.odd, before[0], before[before.shape[0] - 1])
-        dims = (facts.row(facts.INSIDE), facts.row(facts.ACROSS))
-        hops = (r["hops_inside"], r["hops_across"])
-        came = [
-            masked(c - TAU * hop(b.astype(BF16), h[2], h[1]), d)
-            for c, b, h, d in zip(came, sent, hops, dims)
-        ]
+    came = []
+    for n, (name, row) in enumerate((("inside", facts.INSIDE), ("across", facts.ACROSS))):
+        ref = r["came_" + name]
+        block = (ref[0] if len(ref.shape) == 3 else ref[...]).astype(F32)
+        if k > 0:
+            block = block - r["given"][n]
+        came.append(masked(block, facts.row(row)))
     low, high = swapped(facts.odd, *came)
     return low.astype(BF16), high.astype(BF16)
+
+
+def put_given(v, facts, r):
+    sent = swapped(facts.odd, v[0], v[-1])
+    for n, (block, name) in enumerate(zip(sent, ("hops_inside", "hops_across"))):
+        r["gives"][n] = TAU * hop(block.astype(BF16), r[name][2], r[name][1])
 
 
 def step_kernel(k, shift, names, *refs):
@@ -210,6 +212,7 @@
         r["v"][s] = v[s]
     basis = [[r[f"v{i}"][s] for s in range(held)] for i in range(k + 1)]
     if k + 1 < ITERS:
+        put_given(basis[k], facts, r)
         left = r["left"]
         env = (lambda w, s: left[0, w, s]) if len(left.shape) == 5 else (lambda w, s: left[w, s])
         put_local(v, env, r, shift)
@@ -314,15 +317,9 @@
     facts = Facts(r["facts"])
     line = jnp.sum(r["lines"][...], axis=0)
     coefs, energy = combination(line, facts.row(facts.LIVE).astype(F32), shift)
-    held_out, sent = refs[-2:]
-    copies = []
     for s in range(r["v0"].shape[0]):
-        held_out[s] = sum(c * r[f"v{k}"][s] for k, c in enumerate(coefs))
-        copies.append(pltpu.make_async_copy(held_out.at[s], r["x"].at[0, s], sent.at[s]))
-        copies[-1].start()
+        r["x"][0, s] = sum(c * r[f"v{k}"][s] for k, c in enumerate(coefs))
     r["energy"][0] = energy[0, 0]
-    for copy in copies:
-        copy.wait()
 
 
 def in_hbm(array):
@@ -361,12 +358,14 @@
     place = jnp.stack([lax.axis_index("sec"), lax.axis_index("seg")]).astype(jnp.int32)
     block = struct((cap, cap), BF16)
     blocks = struct((held, cap, cap), F32)
+    pair = struct((2, cap, cap), F32)
     triple = struct((3, cap, cap), BF16)
     dots_of = struct((ROWS, LANES), F32)
     local_outs = {"q": blocks, "inside": block, "across": block, "dots": dots_of}
     pairs = [(i, i ^ 1) for i in range(size)]
-    others = [(i, i + 1 if i % 2 else i - 1) for i in range(1, size - 1)]
-    onward = [(i, i + 1) for i in range(lax.axis_size("seg") - 1)]
+    others = [(i, min(i + 1, size - 1) if i % 2 else max(i - 1, 0)) for i in range(size)]
+    segments = lax.axis_size("seg")
+    onward = [(i, (i + 1) % segments) for i in range(segments)]
     one = 2 * cap**3
 
     def exchange(got):
@@ -414,11 +413,11 @@
         for k in range(ITERS):
             ins = {"part": got["q"], **common, **basis, **came}
             if k > 0:
-                ins.update(hops)
+                ins["given"] = got["gives"]
             if k + 1 < ITERS:
                 came = exchange(got)
-                ins.update(left=env)
-                outs = {"v": blocks, **local_outs}
+                ins.update(left=env, **hops)
+                outs = {"v": blocks, "gives": pair, **local_outs}
                 if k + 2 == ITERS:
                     del outs["inside"], outs["across"]
             else:
@@ -503,8 +502,6 @@
         "finish",
         {"facts": facts, "lines": lines, **basis},
         {"x": struct(psi.shape, F32), "energy": struct((1,), F32)},
-        scratch=[pltpu.VMEM((held, cap, cap), F32), pltpu.SemaphoreType.DMA((held,))],
-        outside=("x",),
     )
     return (done["x"], done["energy"], renewed["out"])
 

time: 105 us -> 99.3 us (0.946)
  starting transfers between devices: 34.1 us -> 30.2 us
  Pallas kernels: 27.9 us -> 25.7 us
    pallas_call x14, Pallas kernels: 27.9 us -> 25.7 us  [call(): pl.pallas_call(kernel, out_shape=tuple(outs.values()), in_specs=specs or...]
    ppermute x1, starting transfers between devices: 1.92 us -> 0.02 us  [body(): earlier = lax.ppermute(left_env, 'seg', onward)]
    ppermute x1, starting transfers between devices: 1.92 us -> 0.02 us  [body(): earlier_factor = lax.ppermute(factor, 'seg', onward)]
  transfers between devices with their start and end apart: 18 -> 18, of which waited for: 2 -> 4; matrix products, arithmetic and copies ran while one was open for 0% -> 0% of each run, Pallas kernels for 24% -> 24%
where the time goes in v5:
time: 99.3 us; the launch traced here: 98.4 us
  blocking collectives  36 us (36%)
  starting transfers between devices  30.2 us (30%)
  Pallas kernels  25.7 us (26%)
  waiting for transfers between devices  5.38 us (5%)
  between operations  1.05 us (1%)
    all_to_all x2, blocking collectives, relaxed(): return (basis, lax.all_to_all(got['line'], 'sec', 0, 0))  36 us
    pallas_call x14, Pallas kernels, call(): pl.pallas_call(kernel, out_shape=tuple(outs.values()), in_specs=specs or...  25.7 us
    ppermute x8, starting transfers between devices, exchange(): lax.ppermute(got['inside'], 'sec', pairs)  24.7 us
    ppermute x8, starting transfers between devices, exchange(): lax.ppermute(got['across'], 'sec', others)  5.45 us
    ppermute x1, waiting for transfers between devices, body(): earlier_factor = lax.ppermute(factor, 'seg', onward)  3.75 us
  transfers between devices with their start and end apart: 18, of which 4 were waited for; matrix products, arithmetic and copies ran while one was open for 0% of the time, Pallas kernels for 24%

profile of v5, /device:TPU:128, one launch (start us, length us, event | category | flops | bytes accessed | tf_op | source)
XLA Modules:
  0.0 98.4 jit_solution(4427573958917159026)
XLA Ops:
  0.7 1.8 %start.1 = (f32[2,256,256]{2,1,0:T(8,128)S(1)}, bf16[3,256,256]{2,1,0:T(8,128)(2,1)S(1)}, bf16[3,256,256]{2,1,0:T(8,128)(2,1)S(1)}, s32[8,128]{1,0:T(8,128)S(1)}) custom-call(s32[2]{0:T(128)S(1)} %pad_add_fusion.place, s32[1,32]{1,0:T(1,128)} %dims_at.1, f32[1,2,256,256]{3,2,1,0:T(8,128)} %psi_at.1, bf16[1,2,2,256,256]{4,3,2,1,0:T(8,128)(2,1)} %refs_4_.1, ...), custom_call_target="tpu_custom_call" | custom-call | bytes 1573000 | tf_op jit(solution)/shard_map/start/pallas_call | solution.py:335
  2.6 1.6 %collective-permute-start = (bf16[3,256,256]{2,1,0:T(8,128)(2,1)S(1)}, bf16[3,256,256]{2,1,0:T(8,128)(2,1)S(1)}, u32[]{:S(2)}, u32[]{:S(2)}) collective-permute-start(bf16[3,256,256]{2,1,0:T(8,128)(2,1)S(1)} %get-tuple-element.70), channel_id=1, source_target_pairs={{0,1},{1,0},{2,3},{3,2},{4,5},{5,4},{6,7},{7,6},{8,9},{9,8},{10,11... | collective-permute-start | bytes 1179656 | tf_op jit(solution)/shard_map/ppermute | solution.py:373
  4.8 3.8 %local.1 = (bf16[1,6,2,256,256]{4,3,2,1,0:T(8,128)(2,1)S(1)}, bf16[1,6,2,256,256]{4,3,2,1,0:T(8,128)(2,1)S(1)}, bf16[1,2,2,256,256]{4,3,2,1,0:T(8,128)(2,1)S(1)}...) custom-call(s32[8,128]{1,0:T(8,128)S(1)} %get-tuple-element.64.refs_, ...), custom_call_target="tpu_custom_call" | custom-call | flops 939524096 | bytes 4722688 | tf_op jit(solution)/shard_map/local/pallas_call | solution.py:335
  8.7 4.0 %collective-permute-start.2 = (bf16[256,256]{1,0:T(8,128)(2,1)S(1)}, bf16[256,256]{1,0:T(8,128)(2,1)S(1)}, u32[]{:S(2)}, u32[]{:S(2)}) collective-permute-start(bf16[256,256]{1,0:T(8,128)(2,1)S(1)} %get-tuple-element.75), channel_id=1, source_target_pairs={{0,1},{1,0},{2,3},{3,2},{4,5},{5,4},{6,7},{7,6},{8,9},{9,8},{10,11... | collective-permute-start | bytes 393224 | tf_op jit(solution)/shard_map/ppermute | solution.py:373
  13.3 1.2 %collective-permute-done.refs_6_.refs_9_.refs_11_.refs_12_ = bf16[3,256,256]{2,1,0:T(8,128)(2,1)S(1)} collective-permute-done((bf16[3,256,256]{2,1,0:T(8,128)(2,1)S(1)}, bf16[3,256,256]{2,1,0:T(8,128)(2,1)S(1)}, u32[]{:S(2)}, u32[]{:S(2)}) %collective-permute-start) | collective-permute-done | bytes 393248 | tf_op jit(solution)/shard_map/ppermute | solution.py:373
  14.5 2.0 %step0.2 = (f32[2,256,256]{2,1,0:T(8,128)S(1)}, f32[2,256,256]{2,1,0:T(8,128)S(1)}, f32[2,256,256]{2,1,0:T(8,128)S(1)}, bf16[256,256]{1,0:T(8,128)(2,1)S(1)}, bf...) custom-call(f32[2,256,256]{2,1,0:T(8,128)S(1)} %get-tuple-element.66.refs_0_, ...), custom_call_target="tpu_custom_call" | custom-call | flops 1207959552 | bytes 6819840 | tf_op jit(solution)/shard_map/step0/pallas_call | solution.py:335
  16.5 4.1 %collective-permute-start.4 = (bf16[256,256]{1,0:T(8,128)(2,1)S(1)}, bf16[256,256]{1,0:T(8,128)(2,1)S(1)}, u32[]{:S(2)}, u32[]{:S(2)}) collective-permute-start(bf16[256,256]{1,0:T(8,128)(2,1)S(1)} %get-tuple-element.80), channel_id=1, source_target_pairs={{0,1},{1,0},{2,3},{3,2},{4,5},{5,4},{6,7},{7,6},{8,9},{9,8},{10,11... | collective-permute-start | bytes 393224 | tf_op jit(solution)/shard_map/ppermute | solution.py:373
  21.3 2.0 %step1.2 = (f32[2,256,256]{2,1,0:T(8,128)S(1)}, f32[2,256,256]{2,1,0:T(8,128)S(1)}, f32[2,256,256]{2,1,0:T(8,128)S(1)}, bf16[256,256]{1,0:T(8,128)(2,1)S(1)}, bf...) custom-call(f32[2,256,256]{2,1,0:T(8,128)S(1)} %get-tuple-element.73.refs_0_, ...), custom_call_target="tpu_custom_call" | custom-call | flops 1207959552 | bytes 7344128 | tf_op jit(solution)/shard_map/step1/pallas_call | solution.py:335
  23.3 6.4 %collective-permute-start.6 = (bf16[256,256]{1,0:T(8,128)(2,1)S(1)}, bf16[256,256]{1,0:T(8,128)(2,1)S(1)}, u32[]{:S(2)}, u32[]{:S(2)}) collective-permute-start(bf16[256,256]{1,0:T(8,128)(2,1)S(1)} %get-tuple-element.85), channel_id=1, source_target_pairs={{0,1},{1,0},{2,3},{3,2},{4,5},{5,4},{6,7},{7,6},{8,9},{9,8},{10,11... | collective-permute-start | bytes 393224 | tf_op jit(solution)/shard_map/ppermute | solution.py:373
  30.4 2.1 %step2.2 = (f32[2,256,256]{2,1,0:T(8,128)S(1)}, f32[2,256,256]{2,1,0:T(8,128)S(1)}, f32[2,256,256]{2,1,0:T(8,128)S(1)}, f32[8,128]{1,0:T(8,128)S(1)}) custom-call(f32[2,256,256]{2,1,0:T(8,128)S(1)} %get-tuple-element.78.refs_0_, s32[8,128]{1,0:T(8,128)S(1)} %get-tuple-element.64.refs_0_.refs_1_.refs_5_, ...), custom_call_target="tpu_custom_call" | custom-call | flops 1207959552 | bytes 7868416 | tf_op jit(solution)/shard_map/step2/pallas_call | solution.py:335
  32.7 0.9 step3.2
  33.6 18.5 %all_to_all.10.refs_1_ = f32[16,1,128]{2,1,0:T(1,128)S(1)} all-to-all(f32[16,1,128]{2,1,0:T(1,128)S(1)} %get-tuple-element.92), channel_id=1, replica_groups=mesh['seg'=16,'sec'=16] {'sec'}, dimensions={0} | all-to-all | bytes 16384 | tf_op jit(solution)/shard_map/all_to_all | solution.py:432
  53.5 0.8 collective-permute-start.11
  54.3 1.9 %grow.1 = (bf16[1,6,2,256,256]{4,3,2,1,0:T(8,128)(2,1)}, f32[8,128]{1,0:T(8,128)S(1)}) custom-call(bf16[1,6,2,256,256]{4,3,2,1,0:T(8,128)(2,1)S(1)} %get-tuple-element.72.refs_8_.refs_10_.refs_11_.left.refs_1_, bf16[2,272,256]{2,1,0:T(8,128)(2,1)S(1)} %get-tuple-element.95.factor), custom_call_target="tpu_custom_call" | custom-call | flops 805306368 | bytes 1851392 | tf_op jit(solution)/shard_map/grow/pallas_call | solution.py:335
  56.3 3.8 %collective-permute-done.9.refs_3_ = bf16[2,272,256]{2,1,0:T(8,128)(2,1)S(1)} collective-permute-done((bf16[2,272,256]{2,1,0:T(8,128)(2,1)S(1)}, bf16[2,272,256]{2,1,0:T(8,128)(2,1)S(1)}, u32[]{:S(2)}, u32[]{:S(2)}) %collective-permute-start.9) | collective-permute-done | bytes 278560 | tf_op jit(solution)/shard_map/ppermute | solution.py:471
  60.0 2.2 %second.1 = (bf16[6,2,256,256]{3,2,1,0:T(8,128)(2,1)S(1)}, f32[2,256,256]{2,1,0:T(8,128)S(1)}, bf16[256,256]{1,0:T(8,128)(2,1)S(1)}, bf16[256,256]{1,0:T(8,128)(2,1)S(1)}, f32[8,128]{1,0:T(8,128)S(1)}) custom-call(f32[2,256,256]{2,1,0:T(8,128)S(1)} %get-tuple-element.94.refs_0_.refs_5_.refs_4_.refs_2_, ...), custom_call_target="tpu_custom_call" | custom-call | flops 1744830464 | bytes 6578176 | tf_op jit(solution)/shard_map/second/pallas_call | solution.py:335
  63.6 2.0 %step0.3 = (f32[2,256,256]{2,1,0:T(8,128)S(1)}, f32[2,256,256]{2,1,0:T(8,128)S(1)}, f32[2,256,256]{2,1,0:T(8,128)S(1)}, bf16[256,256]{1,0:T(8,128)(2,1)S(1)}, bf...) custom-call(f32[2,256,256]{2,1,0:T(8,128)S(1)} %get-tuple-element.97.refs_0_, ...), custom_call_target="tpu_custom_call" | custom-call | flops 1207959552 | bytes 6295552 | tf_op jit(solution)/shard_map/step0/pallas_call | solution.py:335
  65.6 3.4 %collective-permute-start.14 = (bf16[256,256]{1,0:T(8,128)(2,1)S(1)}, bf16[256,256]{1,0:T(8,128)(2,1)S(1)}, u32[]{:S(2)}, u32[]{:S(2)}) collective-permute-start(bf16[256,256]{1,0:T(8,128)(2,1)S(1)} %get-tuple-element.108), channel_id=1, source_target_pairs={{0,1},{1,0},{2,3},{3,2},{4,5},{5,4},{6,7},{7,6},{8,9},{9,8},{10,11... | collective-permute-start | bytes 393224 | tf_op jit(solution)/shard_map/ppermute | solution.py:373
  69.6 2.0 %step1.3 = (f32[2,256,256]{2,1,0:T(8,128)S(1)}, f32[2,256,256]{2,1,0:T(8,128)S(1)}, f32[2,256,256]{2,1,0:T(8,128)S(1)}, bf16[256,256]{1,0:T(8,128)(2,1)S(1)}, bf...) custom-call(f32[2,256,256]{2,1,0:T(8,128)S(1)} %get-tuple-element.101.refs_0_, ...), custom_call_target="tpu_custom_call" | custom-call | flops 1207959552 | bytes 7344128 | tf_op jit(solution)/shard_map/step1/pallas_call | solution.py:335
  71.6 4.0 %collective-permute-start.16 = (bf16[256,256]{1,0:T(8,128)(2,1)S(1)}, bf16[256,256]{1,0:T(8,128)(2,1)S(1)}, u32[]{:S(2)}, u32[]{:S(2)}) collective-permute-start(bf16[256,256]{1,0:T(8,128)(2,1)S(1)} %get-tuple-element.113), channel_id=1, source_target_pairs={{0,1},{1,0},{2,3},{3,2},{4,5},{5,4},{6,7},{7,6},{8,9},{9,8},{10,11... | collective-permute-start | bytes 393224 | tf_op jit(solution)/shard_map/ppermute | solution.py:373
  76.3 2.0 %step2.3 = (f32[2,256,256]{2,1,0:T(8,128)S(1)}, f32[2,256,256]{2,1,0:T(8,128)S(1)}, f32[2,256,256]{2,1,0:T(8,128)S(1)}, f32[8,128]{1,0:T(8,128)S(1)}) custom-call(f32[2,256,256]{2,1,0:T(8,128)S(1)} %get-tuple-element.106.refs_0_, s32[8,128]{1,0:T(8,128)S(1)} %get-tuple-element.64.refs_0_.refs_1_.refs_5_, ...), custom_call_target="tpu_custom_call" | custom-call | flops 1207959552 | bytes 7868416 | tf_op jit(solution)/shard_map/step2/pallas_call | solution.py:335
  78.5 1.0 step3.3
  79.5 17.4 %all_to_all.11.refs_1_ = f32[16,1,128]{2,1,0:T(1,128)S(1)} all-to-all(f32[16,1,128]{2,1,0:T(1,128)S(1)} %get-tuple-element.120), channel_id=1, replica_groups=mesh['seg'=16,'sec'=16] {'sec'}, dimensions={0} | all-to-all | bytes 16384 | tf_op jit(solution)/shard_map/all_to_all | solution.py:432
  96.9 1.4 %finish.1 = (f32[1,2,256,256]{3,2,1,0:T(8,128)}, f32[1]{0:T(128)}) custom-call(s32[8,128]{1,0:T(8,128)S(1)} %get-tuple-element.64.refs_0_.refs_1_.refs_5_, f32[16,1,128]{2,1,0:T(1,128)S(1)} %all_to_all.11.refs_1_, f32[2,256,256]{2,1,0:T(8,128)S(1)} %get-tuple-element.94.refs_0_.refs_5_.refs_4_.refs_2_, ...), custom_call_target="tpu_custom_call" | custom-call | bytes 2633728 | tf_op jit(solution)/shard_map/finish/pallas_call | solution.py:335
  (29 shorter events, 7.1 us)
Async XLA Ops:
  0.6 59.4 %collective-permute-start.8 = (bf16[1,6,2,256,256]{4,3,2,1,0:T(8,128)(2,1)}, bf16[1,6,2,256,256]{4,3,2,1,0:T(8,128)(2,1)S(1)}, u32[]{:S(2)}, u32[]{:S(2)}) collective-permute-start(bf16[1,6,2,256,256]{4,3,2,1,0:T(8,128)(2,1)} %refs_2_.1), channel_id=1, source_target_pairs={{0,16},{16,32},{32,48},{48,64},{64,80},{80,96},{96,112},{112,128},... | collective-permute-start | bytes 4718600 | tf_op jit(solution)/shard_map/ppermute | solution.py:408
  2.6 11.9 %collective-permute-start = (bf16[3,256,256]{2,1,0:T(8,128)(2,1)S(1)}, bf16[3,256,256]{2,1,0:T(8,128)(2,1)S(1)}, u32[]{:S(2)}, u32[]{:S(2)}) collective-permute-start(bf16[3,256,256]{2,1,0:T(8,128)(2,1)S(1)} %get-tuple-element.70), channel_id=1, source_target_pairs={{0,1},{1,0},{2,3},{3,2},{4,5},{5,4},{6,7},{7,6},{8,9},{9,8},{10,11... | collective-permute-start | bytes 1179656 | tf_op jit(solution)/shard_map/ppermute | solution.py:373
  4.1 10.4 %collective-permute-start.1 = (bf16[3,256,256]{2,1,0:T(8,128)(2,1)S(1)}, bf16[3,256,256]{2,1,0:T(8,128)(2,1)S(1)}, u32[]{:S(2)}, u32[]{:S(2)}) collective-permute-start(bf16[3,256,256]{2,1,0:T(8,128)(2,1)S(1)} %get-tuple-element.71), channel_id=1, source_target_pairs={{0,0},{1,2},{2,1},{3,4},{4,3},{5,6},{6,5},{7,8},{8,7},{9,10},{10,9... | collective-permute-start | bytes 1179656 | tf_op jit(solution)/shard_map/ppermute | solution.py:374
  8.7 12.6 %collective-permute-start.2 = (bf16[256,256]{1,0:T(8,128)(2,1)S(1)}, bf16[256,256]{1,0:T(8,128)(2,1)S(1)}, u32[]{:S(2)}, u32[]{:S(2)}) collective-permute-start(bf16[256,256]{1,0:T(8,128)(2,1)S(1)} %get-tuple-element.75), channel_id=1, source_target_pairs={{0,1},{1,0},{2,3},{3,2},{4,5},{5,4},{6,7},{7,6},{8,9},{9,8},{10,11... | collective-permute-start | bytes 393224 | tf_op jit(solution)/shard_map/ppermute | solution.py:373
  12.7 8.6 %collective-permute-start.3 = (bf16[256,256]{1,0:T(8,128)(2,1)S(1)}, bf16[256,256]{1,0:T(8,128)(2,1)S(1)}, u32[]{:S(2)}, u32[]{:S(2)}) collective-permute-start(bf16[256,256]{1,0:T(8,128)(2,1)S(1)} %get-tuple-element.76), channel_id=1, source_target_pairs={{0,0},{1,2},{2,1},{3,4},{4,3},{5,6},{6,5},{7,8},{8,7},{9,10},{10,9... | collective-permute-start | bytes 393224 | tf_op jit(solution)/shard_map/ppermute | solution.py:374
  16.5 13.9 %collective-permute-start.4 = (bf16[256,256]{1,0:T(8,128)(2,1)S(1)}, bf16[256,256]{1,0:T(8,128)(2,1)S(1)}, u32[]{:S(2)}, u32[]{:S(2)}) collective-permute-start(bf16[256,256]{1,0:T(8,128)(2,1)S(1)} %get-tuple-element.80), channel_id=1, source_target_pairs={{0,1},{1,0},{2,3},{3,2},{4,5},{5,4},{6,7},{7,6},{8,9},{9,8},{10,11... | collective-permute-start | bytes 393224 | tf_op jit(solution)/shard_map/ppermute | solution.py:373
  20.6 9.8 %collective-permute-start.5 = (bf16[256,256]{1,0:T(8,128)(2,1)S(1)}, bf16[256,256]{1,0:T(8,128)(2,1)S(1)}, u32[]{:S(2)}, u32[]{:S(2)}) collective-permute-start(bf16[256,256]{1,0:T(8,128)(2,1)S(1)} %get-tuple-element.81), channel_id=1, source_target_pairs={{0,0},{1,2},{2,1},{3,4},{4,3},{5,6},{6,5},{7,8},{8,7},{9,10},{10,9... | collective-permute-start | bytes 393224 | tf_op jit(solution)/shard_map/ppermute | solution.py:374
  23.3 9.4 %collective-permute-start.6 = (bf16[256,256]{1,0:T(8,128)(2,1)S(1)}, bf16[256,256]{1,0:T(8,128)(2,1)S(1)}, u32[]{:S(2)}, u32[]{:S(2)}) collective-permute-start(bf16[256,256]{1,0:T(8,128)(2,1)S(1)} %get-tuple-element.85), channel_id=1, source_target_pairs={{0,1},{1,0},{2,3},{3,2},{4,5},{5,4},{6,7},{7,6},{8,9},{9,8},{10,11... | collective-permute-start | bytes 393224 | tf_op jit(solution)/shard_map/ppermute | solution.py:373
  29.7 3.0 %collective-permute-start.7 = (bf16[256,256]{1,0:T(8,128)(2,1)S(1)}, bf16[256,256]{1,0:T(8,128)(2,1)S(1)}, u32[]{:S(2)}, u32[]{:S(2)}) collective-permute-start(bf16[256,256]{1,0:T(8,128)(2,1)S(1)} %get-tuple-element.86), channel_id=1, source_target_pairs={{0,0},{1,2},{2,1},{3,4},{4,3},{5,6},{6,5},{7,8},{8,7},{9,10},{10,9... | collective-permute-start | bytes 393224 | tf_op jit(solution)/shard_map/ppermute | solution.py:374
  52.8 7.2 %collective-permute-start.9 = (bf16[2,272,256]{2,1,0:T(8,128)(2,1)S(1)}, bf16[2,272,256]{2,1,0:T(8,128)(2,1)S(1)}, u32[]{:S(2)}, u32[]{:S(2)}) collective-permute-start(bf16[2,272,256]{2,1,0:T(8,128)(2,1)S(1)} %get-tuple-element.95.factor), channel_id=1, source_target_pairs={{0,16},{16,32},{32,48},{48,64},{64,80},{80,96},{96,112},{112,128},... | collective-permute-start | bytes 835592 | tf_op jit(solution)/shard_map/ppermute | solution.py:471
  52.8 10.7 %collective-permute-start.10 = (bf16[256,256]{1,0:T(8,128)(2,1)S(1)}, bf16[256,256]{1,0:T(8,128)(2,1)S(1)}, u32[]{:S(2)}, u32[]{:S(2)}) collective-permute-start(bf16[256,256]{1,0:T(8,128)(2,1)S(1)} %get-tuple-element.98), channel_id=1, source_target_pairs={{0,1},{1,0},{2,3},{3,2},{4,5},{5,4},{6,7},{7,6},{8,9},{9,8},{10,11... | collective-permute-start | bytes 393224 | tf_op jit(solution)/shard_map/ppermute | solution.py:373
  53.5 10.1 %collective-permute-start.11 = (bf16[256,256]{1,0:T(8,128)(2,1)S(1)}, bf16[256,256]{1,0:T(8,128)(2,1)S(1)}, u32[]{:S(2)}, u32[]{:S(2)}) collective-permute-start(bf16[256,256]{1,0:T(8,128)(2,1)S(1)} %get-tuple-element.99), channel_id=1, source_target_pairs={{0,0},{1,2},{2,1},{3,4},{4,3},{5,6},{6,5},{7,8},{8,7},{9,10},{10,9... | collective-permute-start | bytes 393224 | tf_op jit(solution)/shard_map/ppermute | solution.py:374
  62.3 7.3 %collective-permute-start.12 = (bf16[256,256]{1,0:T(8,128)(2,1)S(1)}, bf16[256,256]{1,0:T(8,128)(2,1)S(1)}, u32[]{:S(2)}, u32[]{:S(2)}) collective-permute-start(bf16[256,256]{1,0:T(8,128)(2,1)S(1)} %get-tuple-element.103), channel_id=1, source_target_pairs={{0,1},{1,0},{2,3},{3,2},{4,5},{5,4},{6,7},{7,6},{8,9},{9,8},{10,11... | collective-permute-start | bytes 393224 | tf_op jit(solution)/shard_map/ppermute | solution.py:373
  62.9 6.7 %collective-permute-start.13 = (bf16[256,256]{1,0:T(8,128)(2,1)S(1)}, bf16[256,256]{1,0:T(8,128)(2,1)S(1)}, u32[]{:S(2)}, u32[]{:S(2)}) collective-permute-start(bf16[256,256]{1,0:T(8,128)(2,1)S(1)} %get-tuple-element.104), channel_id=1, source_target_pairs={{0,0},{1,2},{2,1},{3,4},{4,3},{5,6},{6,5},{7,8},{8,7},{9,10},{10,9... | collective-permute-start | bytes 393224 | tf_op jit(solution)/shard_map/ppermute | solution.py:374
  65.6 10.7 %collective-permute-start.14 = (bf16[256,256]{1,0:T(8,128)(2,1)S(1)}, bf16[256,256]{1,0:T(8,128)(2,1)S(1)}, u32[]{:S(2)}, u32[]{:S(2)}) collective-permute-start(bf16[256,256]{1,0:T(8,128)(2,1)S(1)} %get-tuple-element.108), channel_id=1, source_target_pairs={{0,1},{1,0},{2,3},{3,2},{4,5},{5,4},{6,7},{7,6},{8,9},{9,8},{10,11... | collective-permute-start | bytes 393224 | tf_op jit(solution)/shard_map/ppermute | solution.py:373
  68.9 7.3 %collective-permute-start.15 = (bf16[256,256]{1,0:T(8,128)(2,1)S(1)}, bf16[256,256]{1,0:T(8,128)(2,1)S(1)}, u32[]{:S(2)}, u32[]{:S(2)}) collective-permute-start(bf16[256,256]{1,0:T(8,128)(2,1)S(1)} %get-tuple-element.109), channel_id=1, source_target_pairs={{0,0},{1,2},{2,1},{3,4},{4,3},{5,6},{6,5},{7,8},{8,7},{9,10},{10,9... | collective-permute-start | bytes 393224 | tf_op jit(solution)/shard_map/ppermute | solution.py:374
  71.6 6.9 %collective-permute-start.16 = (bf16[256,256]{1,0:T(8,128)(2,1)S(1)}, bf16[256,256]{1,0:T(8,128)(2,1)S(1)}, u32[]{:S(2)}, u32[]{:S(2)}) collective-permute-start(bf16[256,256]{1,0:T(8,128)(2,1)S(1)} %get-tuple-element.113), channel_id=1, source_target_pairs={{0,1},{1,0},{2,3},{3,2},{4,5},{5,4},{6,7},{7,6},{8,9},{9,8},{10,11... | collective-permute-start | bytes 393224 | tf_op jit(solution)/shard_map/ppermute | solution.py:373
  75.6 3.0 %collective-permute-start.17 = (bf16[256,256]{1,0:T(8,128)(2,1)S(1)}, bf16[256,256]{1,0:T(8,128)(2,1)S(1)}, u32[]{:S(2)}, u32[]{:S(2)}) collective-permute-start(bf16[256,256]{1,0:T(8,128)(2,1)S(1)} %get-tuple-element.114), channel_id=1, source_target_pairs={{0,0},{1,2},{2,1},{3,4},{4,3},{5,6},{6,5},{7,8},{8,7},{9,10},{10,9... | collective-permute-start | bytes 393224 | tf_op jit(solution)/shard_map/ppermute | solution.py:374

commit v6 on v5

--- a/solution.py
+++ b/solution.py
@@ -363,7 +363,7 @@
     dots_of = struct((ROWS, LANES), F32)
     local_outs = {"q": blocks, "inside": block, "across": block, "dots": dots_of}
     pairs = [(i, i ^ 1) for i in range(size)]
-    others = [(i, min(i + 1, size - 1) if i % 2 else max(i - 1, 0)) for i in range(size)]
+    others = [(i, (i + 1 if i % 2 else i - 1) % size) for i in range(size)]
     segments = lax.axis_size("seg")
     onward = [(i, (i + 1) % segments) for i in range(segments)]
     one = 2 * cap**3

time: 99.3 us -> 92.3 us (0.930)
  blocking collectives: 36 us -> 21.1 us
  waiting for transfers between devices: 5.38 us -> 18.1 us
  starting transfers between devices: 30.2 us -> 25 us
    ppermute x8, starting transfers between devices: 24.7 us -> 3.58 us  [exchange(): lax.ppermute(got['inside'], 'sec', pairs)]
    ppermute x8, starting transfers between devices: 5.45 us -> 21.4 us  [exchange(): lax.ppermute(got['across'], 'sec', others)]
    all_to_all x2, blocking collectives: 36 us -> 21.1 us  [relaxed(): return (basis, lax.all_to_all(got['line'], 'sec', 0, 0))]
    ppermute x8, waiting for transfers between devices: 0.02 us -> 12.8 us  [exchange(): lax.ppermute(got['across'], 'sec', others)]
  transfers between devices with their start and end apart: 18 -> 18, of which waited for: 4 -> 8; matrix products, arithmetic and copies ran while one was open for 0% -> 0% of each run, Pallas kernels for 24% -> 26%
where the time goes in v6:
time: 92.3 us; the launch traced here: 91 us
  Pallas kernels  25.7 us (28%)
  starting transfers between devices  25 us (27%)
  blocking collectives  21.1 us (23%)
  waiting for transfers between devices  18.1 us (20%)
  between operations  0.96 us (1%)
    pallas_call x14, Pallas kernels, call(): pl.pallas_call(kernel, out_shape=tuple(outs.values()), in_specs=specs or...  25.7 us
    ppermute x8, starting transfers between devices, exchange(): lax.ppermute(got['across'], 'sec', others)  21.4 us
    all_to_all x2, blocking collectives, relaxed(): return (basis, lax.all_to_all(got['line'], 'sec', 0, 0))  21.1 us
    ppermute x8, waiting for transfers between devices, exchange(): lax.ppermute(got['across'], 'sec', others)  12.8 us
    ppermute x8, starting transfers between devices, exchange(): lax.ppermute(got['inside'], 'sec', pairs)  3.58 us
    ppermute x1, waiting for transfers between devices, body(): earlier_factor = lax.ppermute(factor, 'seg', onward)  2.81 us
    ppermute x8, waiting for transfers between devices, exchange(): lax.ppermute(got['inside'], 'sec', pairs)  2.47 us
  transfers between devices with their start and end apart: 18, of which 8 were waited for; matrix products, arithmetic and copies ran while one was open for 0% of the time, Pallas kernels for 26%

profile of v6, /device:TPU:128, one launch (start us, length us, event | category | flops | bytes accessed | tf_op | source)
XLA Modules:
  0.0 91.0 jit_solution(6032431290091076873)
XLA Ops:
  0.7 1.8 %start.1 = (f32[2,256,256]{2,1,0:T(8,128)S(1)}, bf16[3,256,256]{2,1,0:T(8,128)(2,1)S(1)}, bf16[3,256,256]{2,1,0:T(8,128)(2,1)S(1)}, s32[8,128]{1,0:T(8,128)S(1)}) custom-call(s32[2]{0:T(128)S(1)} %pad_add_fusion.place, s32[1,32]{1,0:T(1,128)} %dims_at.1, f32[1,2,256,256]{3,2,1,0:T(8,128)} %psi_at.1, bf16[1,2,2,256,256]{4,3,2,1,0:T(8,128)(2,1)} %refs_4_.1, ...), custom_call_target="tpu_custom_call" | custom-call | bytes 1573000 | tf_op jit(solution)/shard_map/start/pallas_call | solution.py:335
  2.6 1.6 %collective-permute-start = (bf16[3,256,256]{2,1,0:T(8,128)(2,1)S(1)}, bf16[3,256,256]{2,1,0:T(8,128)(2,1)S(1)}, u32[]{:S(2)}, u32[]{:S(2)}) collective-permute-start(bf16[3,256,256]{2,1,0:T(8,128)(2,1)S(1)} %get-tuple-element.70), channel_id=1, source_target_pairs={{0,1},{1,0},{2,3},{3,2},{4,5},{5,4},{6,7},{7,6},{8,9},{9,8},{10,11... | collective-permute-start | bytes 1179656 | tf_op jit(solution)/shard_map/ppermute | solution.py:373
  4.1 4.5 %collective-permute-start.1 = (bf16[3,256,256]{2,1,0:T(8,128)(2,1)S(1)}, bf16[3,256,256]{2,1,0:T(8,128)(2,1)S(1)}, u32[]{:S(2)}, u32[]{:S(2)}) collective-permute-start(bf16[3,256,256]{2,1,0:T(8,128)(2,1)S(1)} %get-tuple-element.71), channel_id=1, source_target_pairs={{0,15},{1,2},{2,1},{3,4},{4,3},{5,6},{6,5},{7,8},{8,7},{9,10},{10,... | collective-permute-start | bytes 1179656 | tf_op jit(solution)/shard_map/ppermute | solution.py:374
  8.7 3.8 %local.1 = (bf16[1,6,2,256,256]{4,3,2,1,0:T(8,128)(2,1)S(1)}, bf16[1,6,2,256,256]{4,3,2,1,0:T(8,128)(2,1)S(1)}, bf16[1,2,2,256,256]{4,3,2,1,0:T(8,128)(2,1)S(1)}...) custom-call(s32[8,128]{1,0:T(8,128)S(1)} %get-tuple-element.64.refs_, ...), custom_call_target="tpu_custom_call" | custom-call | flops 939524096 | bytes 4722688 | tf_op jit(solution)/shard_map/local/pallas_call | solution.py:335
  14.5 4.9 %collective-permute-done.1.refs_7_.refs_10_.refs_12_.refs_13_ = bf16[3,256,256]{2,1,0:T(8,128)(2,1)S(1)} collective-permute-done((bf16[3,256,256]{2,1,0:T(8,128)(2,1)S(1)}, bf16[3,256,256]{2,1,0:T(8,128)(2,1)S(1)}, u32[]{:S(2)}, u32[]{:S(2)}) %collective-permute-start.1) | collective-permute-done | bytes 393248 | tf_op jit(solution)/shard_map/ppermute | solution.py:374
  19.4 2.0 %step0.2 = (f32[2,256,256]{2,1,0:T(8,128)S(1)}, f32[2,256,256]{2,1,0:T(8,128)S(1)}, f32[2,256,256]{2,1,0:T(8,128)S(1)}, bf16[256,256]{1,0:T(8,128)(2,1)S(1)}, bf...) custom-call(f32[2,256,256]{2,1,0:T(8,128)S(1)} %get-tuple-element.66.refs_0_, ...), custom_call_target="tpu_custom_call" | custom-call | flops 1207959552 | bytes 6819840 | tf_op jit(solution)/shard_map/step0/pallas_call | solution.py:335
  21.5 4.6 %collective-permute-start.5 = (bf16[256,256]{1,0:T(8,128)(2,1)S(1)}, bf16[256,256]{1,0:T(8,128)(2,1)S(1)}, u32[]{:S(2)}, u32[]{:S(2)}) collective-permute-start(bf16[256,256]{1,0:T(8,128)(2,1)S(1)} %get-tuple-element.81), channel_id=1, source_target_pairs={{0,15},{1,2},{2,1},{3,4},{4,3},{5,6},{6,5},{7,8},{8,7},{9,10},{10,... | collective-permute-start | bytes 393224 | tf_op jit(solution)/shard_map/ppermute | solution.py:374
  26.2 2.0 %step1.2 = (f32[2,256,256]{2,1,0:T(8,128)S(1)}, f32[2,256,256]{2,1,0:T(8,128)S(1)}, f32[2,256,256]{2,1,0:T(8,128)S(1)}, bf16[256,256]{1,0:T(8,128)(2,1)S(1)}, bf...) custom-call(f32[2,256,256]{2,1,0:T(8,128)S(1)} %get-tuple-element.73.refs_0_, ...), custom_call_target="tpu_custom_call" | custom-call | flops 1207959552 | bytes 7344128 | tf_op jit(solution)/shard_map/step1/pallas_call | solution.py:335
  28.3 1.9 %collective-permute-start.7 = (bf16[256,256]{1,0:T(8,128)(2,1)S(1)}, bf16[256,256]{1,0:T(8,128)(2,1)S(1)}, u32[]{:S(2)}, u32[]{:S(2)}) collective-permute-start(bf16[256,256]{1,0:T(8,128)(2,1)S(1)} %get-tuple-element.86), channel_id=1, source_target_pairs={{0,15},{1,2},{2,1},{3,4},{4,3},{5,6},{6,5},{7,8},{8,7},{9,10},{10,... | collective-permute-start | bytes 393224 | tf_op jit(solution)/shard_map/ppermute | solution.py:374
  30.2 2.1 %step2.2 = (f32[2,256,256]{2,1,0:T(8,128)S(1)}, f32[2,256,256]{2,1,0:T(8,128)S(1)}, f32[2,256,256]{2,1,0:T(8,128)S(1)}, f32[8,128]{1,0:T(8,128)S(1)}) custom-call(f32[2,256,256]{2,1,0:T(8,128)S(1)} %get-tuple-element.78.refs_0_, s32[8,128]{1,0:T(8,128)S(1)} %get-tuple-element.64.refs_0_.refs_1_.refs_5_, ...), custom_call_target="tpu_custom_call" | custom-call | flops 1207959552 | bytes 7868416 | tf_op jit(solution)/shard_map/step2/pallas_call | solution.py:335
  33.2 3.4 %collective-permute-done.7.refs_9_ = bf16[256,256]{1,0:T(8,128)(2,1)S(1)} collective-permute-done((bf16[256,256]{1,0:T(8,128)(2,1)S(1)}, bf16[256,256]{1,0:T(8,128)(2,1)S(1)}, u32[]{:S(2)}, u32[]{:S(2)}) %collective-permute-start.7) | collective-permute-done | bytes 131104 | tf_op jit(solution)/shard_map/ppermute | solution.py:374
  37.6 10.6 %all_to_all.10.refs_1_ = f32[16,1,128]{2,1,0:T(1,128)S(1)} all-to-all(f32[16,1,128]{2,1,0:T(1,128)S(1)} %get-tuple-element.92), channel_id=1, replica_groups=mesh['seg'=16,'sec'=16] {'sec'}, dimensions={0} | all-to-all | bytes 16384 | tf_op jit(solution)/shard_map/all_to_all | solution.py:432
  49.5 1.8 %collective-permute-start.11 = (bf16[256,256]{1,0:T(8,128)(2,1)S(1)}, bf16[256,256]{1,0:T(8,128)(2,1)S(1)}, u32[]{:S(2)}, u32[]{:S(2)}) collective-permute-start(bf16[256,256]{1,0:T(8,128)(2,1)S(1)} %get-tuple-element.99), channel_id=1, source_target_pairs={{0,15},{1,2},{2,1},{3,4},{4,3},{5,6},{6,5},{7,8},{8,7},{9,10},{10,... | collective-permute-start | bytes 393224 | tf_op jit(solution)/shard_map/ppermute | solution.py:374
  51.3 1.9 %grow.1 = (bf16[1,6,2,256,256]{4,3,2,1,0:T(8,128)(2,1)}, f32[8,128]{1,0:T(8,128)S(1)}) custom-call(bf16[1,6,2,256,256]{4,3,2,1,0:T(8,128)(2,1)S(1)} %get-tuple-element.72.refs_8_.refs_10_.refs_11_.left.refs_1_, bf16[2,272,256]{2,1,0:T(8,128)(2,1)S(1)} %get-tuple-element.95.factor), custom_call_target="tpu_custom_call" | custom-call | flops 805306368 | bytes 1851392 | tf_op jit(solution)/shard_map/grow/pallas_call | solution.py:335
  53.2 2.8 %collective-permute-done.9.refs_3_ = bf16[2,272,256]{2,1,0:T(8,128)(2,1)S(1)} collective-permute-done((bf16[2,272,256]{2,1,0:T(8,128)(2,1)S(1)}, bf16[2,272,256]{2,1,0:T(8,128)(2,1)S(1)}, u32[]{:S(2)}, u32[]{:S(2)}) %collective-permute-start.9) | collective-permute-done | bytes 278560 | tf_op jit(solution)/shard_map/ppermute | solution.py:471
  56.0 2.2 %second.1 = (bf16[6,2,256,256]{3,2,1,0:T(8,128)(2,1)S(1)}, f32[2,256,256]{2,1,0:T(8,128)S(1)}, bf16[256,256]{1,0:T(8,128)(2,1)S(1)}, bf16[256,256]{1,0:T(8,128)(2,1)S(1)}, f32[8,128]{1,0:T(8,128)S(1)}) custom-call(f32[2,256,256]{2,1,0:T(8,128)S(1)} %get-tuple-element.94.refs_0_.refs_5_.refs_4_.refs_2_, ...), custom_call_target="tpu_custom_call" | custom-call | flops 1744830464 | bytes 6578176 | tf_op jit(solution)/shard_map/second/pallas_call | solution.py:335
  58.9 1.8 %collective-permute-start.13 = (bf16[256,256]{1,0:T(8,128)(2,1)S(1)}, bf16[256,256]{1,0:T(8,128)(2,1)S(1)}, u32[]{:S(2)}, u32[]{:S(2)}) collective-permute-start(bf16[256,256]{1,0:T(8,128)(2,1)S(1)} %get-tuple-element.104), channel_id=1, source_target_pairs={{0,15},{1,2},{2,1},{3,4},{4,3},{5,6},{6,5},{7,8},{8,7},{9,10},{10,... | collective-permute-start | bytes 393224 | tf_op jit(solution)/shard_map/ppermute | solution.py:374
  60.7 2.0 %step0.3 = (f32[2,256,256]{2,1,0:T(8,128)S(1)}, f32[2,256,256]{2,1,0:T(8,128)S(1)}, f32[2,256,256]{2,1,0:T(8,128)S(1)}, bf16[256,256]{1,0:T(8,128)(2,1)S(1)}, bf...) custom-call(f32[2,256,256]{2,1,0:T(8,128)S(1)} %get-tuple-element.97.refs_0_, ...), custom_call_target="tpu_custom_call" | custom-call | flops 1207959552 | bytes 6295552 | tf_op jit(solution)/shard_map/step0/pallas_call | solution.py:335
  63.0 3.4 %collective-permute-start.15 = (bf16[256,256]{1,0:T(8,128)(2,1)S(1)}, bf16[256,256]{1,0:T(8,128)(2,1)S(1)}, u32[]{:S(2)}, u32[]{:S(2)}) collective-permute-start(bf16[256,256]{1,0:T(8,128)(2,1)S(1)} %get-tuple-element.109), channel_id=1, source_target_pairs={{0,15},{1,2},{2,1},{3,4},{4,3},{5,6},{6,5},{7,8},{8,7},{9,10},{10,... | collective-permute-start | bytes 393224 | tf_op jit(solution)/shard_map/ppermute | solution.py:374
  67.2 2.0 %step1.3 = (f32[2,256,256]{2,1,0:T(8,128)S(1)}, f32[2,256,256]{2,1,0:T(8,128)S(1)}, f32[2,256,256]{2,1,0:T(8,128)S(1)}, bf16[256,256]{1,0:T(8,128)(2,1)S(1)}, bf...) custom-call(f32[2,256,256]{2,1,0:T(8,128)S(1)} %get-tuple-element.101.refs_0_, ...), custom_call_target="tpu_custom_call" | custom-call | flops 1207959552 | bytes 7344128 | tf_op jit(solution)/shard_map/step1/pallas_call | solution.py:335
  69.3 2.1 %collective-permute-start.17 = (bf16[256,256]{1,0:T(8,128)(2,1)S(1)}, bf16[256,256]{1,0:T(8,128)(2,1)S(1)}, u32[]{:S(2)}, u32[]{:S(2)}) collective-permute-start(bf16[256,256]{1,0:T(8,128)(2,1)S(1)} %get-tuple-element.114), channel_id=1, source_target_pairs={{0,15},{1,2},{2,1},{3,4},{4,3},{5,6},{6,5},{7,8},{8,7},{9,10},{10,... | collective-permute-start | bytes 393224 | tf_op jit(solution)/shard_map/ppermute | solution.py:374
  71.4 2.0 %step2.3 = (f32[2,256,256]{2,1,0:T(8,128)S(1)}, f32[2,256,256]{2,1,0:T(8,128)S(1)}, f32[2,256,256]{2,1,0:T(8,128)S(1)}, f32[8,128]{1,0:T(8,128)S(1)}) custom-call(f32[2,256,256]{2,1,0:T(8,128)S(1)} %get-tuple-element.106.refs_0_, s32[8,128]{1,0:T(8,128)S(1)} %get-tuple-element.64.refs_0_.refs_1_.refs_5_, ...), custom_call_target="tpu_custom_call" | custom-call | flops 1207959552 | bytes 7868416 | tf_op jit(solution)/shard_map/step2/pallas_call | solution.py:335
  74.3 3.6 %collective-permute-done.17.refs_9_ = bf16[256,256]{1,0:T(8,128)(2,1)S(1)} collective-permute-done((bf16[256,256]{1,0:T(8,128)(2,1)S(1)}, bf16[256,256]{1,0:T(8,128)(2,1)S(1)}, u32[]{:S(2)}, u32[]{:S(2)}) %collective-permute-start.17) | collective-permute-done | bytes 131104 | tf_op jit(solution)/shard_map/ppermute | solution.py:374
  78.9 10.6 %all_to_all.11.refs_1_ = f32[16,1,128]{2,1,0:T(1,128)S(1)} all-to-all(f32[16,1,128]{2,1,0:T(1,128)S(1)} %get-tuple-element.120), channel_id=1, replica_groups=mesh['seg'=16,'sec'=16] {'sec'}, dimensions={0} | all-to-all | bytes 16384 | tf_op jit(solution)/shard_map/all_to_all | solution.py:432
  (29 shorter events, 10.4 us)
Async XLA Ops:
  0.6 55.4 %collective-permute-start.8 = (bf16[1,6,2,256,256]{4,3,2,1,0:T(8,128)(2,1)}, bf16[1,6,2,256,256]{4,3,2,1,0:T(8,128)(2,1)S(1)}, u32[]{:S(2)}, u32[]{:S(2)}) collective-permute-start(bf16[1,6,2,256,256]{4,3,2,1,0:T(8,128)(2,1)} %refs_2_.1), channel_id=1, source_target_pairs={{0,16},{16,32},{32,48},{48,64},{64,80},{80,96},{96,112},{112,128},... | collective-permute-start | bytes 4718600 | tf_op jit(solution)/shard_map/ppermute | solution.py:408
  2.6 11.9 %collective-permute-start = (bf16[3,256,256]{2,1,0:T(8,128)(2,1)S(1)}, bf16[3,256,256]{2,1,0:T(8,128)(2,1)S(1)}, u32[]{:S(2)}, u32[]{:S(2)}) collective-permute-start(bf16[3,256,256]{2,1,0:T(8,128)(2,1)S(1)} %get-tuple-element.70), channel_id=1, source_target_pairs={{0,1},{1,0},{2,3},{3,2},{4,5},{5,4},{6,7},{7,6},{8,9},{9,8},{10,11... | collective-permute-start | bytes 1179656 | tf_op jit(solution)/shard_map/ppermute | solution.py:373
  4.1 15.3 %collective-permute-start.1 = (bf16[3,256,256]{2,1,0:T(8,128)(2,1)S(1)}, bf16[3,256,256]{2,1,0:T(8,128)(2,1)S(1)}, u32[]{:S(2)}, u32[]{:S(2)}) collective-permute-start(bf16[3,256,256]{2,1,0:T(8,128)(2,1)S(1)} %get-tuple-element.71), channel_id=1, source_target_pairs={{0,15},{1,2},{2,1},{3,4},{4,3},{5,6},{6,5},{7,8},{8,7},{9,10},{10,... | collective-permute-start | bytes 1179656 | tf_op jit(solution)/shard_map/ppermute | solution.py:374
  12.5 13.6 %collective-permute-start.2 = (bf16[256,256]{1,0:T(8,128)(2,1)S(1)}, bf16[256,256]{1,0:T(8,128)(2,1)S(1)}, u32[]{:S(2)}, u32[]{:S(2)}) collective-permute-start(bf16[256,256]{1,0:T(8,128)(2,1)S(1)} %get-tuple-element.75), channel_id=1, source_target_pairs={{0,1},{1,0},{2,3},{3,2},{4,5},{5,4},{6,7},{7,6},{8,9},{9,8},{10,11... | collective-permute-start | bytes 393224 | tf_op jit(solution)/shard_map/ppermute | solution.py:373
  12.6 13.5 %collective-permute-start.3 = (bf16[256,256]{1,0:T(8,128)(2,1)S(1)}, bf16[256,256]{1,0:T(8,128)(2,1)S(1)}, u32[]{:S(2)}, u32[]{:S(2)}) collective-permute-start(bf16[256,256]{1,0:T(8,128)(2,1)S(1)} %get-tuple-element.76), channel_id=1, source_target_pairs={{0,15},{1,2},{2,1},{3,4},{4,3},{5,6},{6,5},{7,8},{8,7},{9,10},{10,... | collective-permute-start | bytes 393224 | tf_op jit(solution)/shard_map/ppermute | solution.py:374
  21.4 8.8 %collective-permute-start.4 = (bf16[256,256]{1,0:T(8,128)(2,1)S(1)}, bf16[256,256]{1,0:T(8,128)(2,1)S(1)}, u32[]{:S(2)}, u32[]{:S(2)}) collective-permute-start(bf16[256,256]{1,0:T(8,128)(2,1)S(1)} %get-tuple-element.80), channel_id=1, source_target_pairs={{0,1},{1,0},{2,3},{3,2},{4,5},{5,4},{6,7},{7,6},{8,9},{9,8},{10,11... | collective-permute-start | bytes 393224 | tf_op jit(solution)/shard_map/ppermute | solution.py:373
  21.5 8.7 %collective-permute-start.5 = (bf16[256,256]{1,0:T(8,128)(2,1)S(1)}, bf16[256,256]{1,0:T(8,128)(2,1)S(1)}, u32[]{:S(2)}, u32[]{:S(2)}) collective-permute-start(bf16[256,256]{1,0:T(8,128)(2,1)S(1)} %get-tuple-element.81), channel_id=1, source_target_pairs={{0,15},{1,2},{2,1},{3,4},{4,3},{5,6},{6,5},{7,8},{8,7},{9,10},{10,... | collective-permute-start | bytes 393224 | tf_op jit(solution)/shard_map/ppermute | solution.py:374
  28.2 5.1 %collective-permute-start.6 = (bf16[256,256]{1,0:T(8,128)(2,1)S(1)}, bf16[256,256]{1,0:T(8,128)(2,1)S(1)}, u32[]{:S(2)}, u32[]{:S(2)}) collective-permute-start(bf16[256,256]{1,0:T(8,128)(2,1)S(1)} %get-tuple-element.85), channel_id=1, source_target_pairs={{0,1},{1,0},{2,3},{3,2},{4,5},{5,4},{6,7},{7,6},{8,9},{9,8},{10,11... | collective-permute-start | bytes 393224 | tf_op jit(solution)/shard_map/ppermute | solution.py:373
  28.3 8.4 %collective-permute-start.7 = (bf16[256,256]{1,0:T(8,128)(2,1)S(1)}, bf16[256,256]{1,0:T(8,128)(2,1)S(1)}, u32[]{:S(2)}, u32[]{:S(2)}) collective-permute-start(bf16[256,256]{1,0:T(8,128)(2,1)S(1)} %get-tuple-element.86), channel_id=1, source_target_pairs={{0,15},{1,2},{2,1},{3,4},{4,3},{5,6},{6,5},{7,8},{8,7},{9,10},{10,... | collective-permute-start | bytes 393224 | tf_op jit(solution)/shard_map/ppermute | solution.py:374
  48.8 7.2 %collective-permute-start.9 = (bf16[2,272,256]{2,1,0:T(8,128)(2,1)S(1)}, bf16[2,272,256]{2,1,0:T(8,128)(2,1)S(1)}, u32[]{:S(2)}, u32[]{:S(2)}) collective-permute-start(bf16[2,272,256]{2,1,0:T(8,128)(2,1)S(1)} %get-tuple-element.95.factor), channel_id=1, source_target_pairs={{0,16},{16,32},{32,48},{48,64},{64,80},{80,96},{96,112},{112,128},... | collective-permute-start | bytes 835592 | tf_op jit(solution)/shard_map/ppermute | solution.py:471
  48.9 11.9 %collective-permute-start.10 = (bf16[256,256]{1,0:T(8,128)(2,1)S(1)}, bf16[256,256]{1,0:T(8,128)(2,1)S(1)}, u32[]{:S(2)}, u32[]{:S(2)}) collective-permute-start(bf16[256,256]{1,0:T(8,128)(2,1)S(1)} %get-tuple-element.98), channel_id=1, source_target_pairs={{0,1},{1,0},{2,3},{3,2},{4,5},{5,4},{6,7},{7,6},{8,9},{9,8},{10,11... | collective-permute-start | bytes 393224 | tf_op jit(solution)/shard_map/ppermute | solution.py:373
  49.5 11.2 %collective-permute-start.11 = (bf16[256,256]{1,0:T(8,128)(2,1)S(1)}, bf16[256,256]{1,0:T(8,128)(2,1)S(1)}, u32[]{:S(2)}, u32[]{:S(2)}) collective-permute-start(bf16[256,256]{1,0:T(8,128)(2,1)S(1)} %get-tuple-element.99), channel_id=1, source_target_pairs={{0,15},{1,2},{2,1},{3,4},{4,3},{5,6},{6,5},{7,8},{8,7},{9,10},{10,... | collective-permute-start | bytes 393224 | tf_op jit(solution)/shard_map/ppermute | solution.py:374
  58.3 8.2 %collective-permute-start.12 = (bf16[256,256]{1,0:T(8,128)(2,1)S(1)}, bf16[256,256]{1,0:T(8,128)(2,1)S(1)}, u32[]{:S(2)}, u32[]{:S(2)}) collective-permute-start(bf16[256,256]{1,0:T(8,128)(2,1)S(1)} %get-tuple-element.103), channel_id=1, source_target_pairs={{0,1},{1,0},{2,3},{3,2},{4,5},{5,4},{6,7},{7,6},{8,9},{9,8},{10,11... | collective-permute-start | bytes 393224 | tf_op jit(solution)/shard_map/ppermute | solution.py:373
  58.9 8.3 %collective-permute-start.13 = (bf16[256,256]{1,0:T(8,128)(2,1)S(1)}, bf16[256,256]{1,0:T(8,128)(2,1)S(1)}, u32[]{:S(2)}, u32[]{:S(2)}) collective-permute-start(bf16[256,256]{1,0:T(8,128)(2,1)S(1)} %get-tuple-element.104), channel_id=1, source_target_pairs={{0,15},{1,2},{2,1},{3,4},{4,3},{5,6},{6,5},{7,8},{8,7},{9,10},{10,... | collective-permute-start | bytes 393224 | tf_op jit(solution)/shard_map/ppermute | solution.py:374
  62.7 8.7 %collective-permute-start.14 = (bf16[256,256]{1,0:T(8,128)(2,1)S(1)}, bf16[256,256]{1,0:T(8,128)(2,1)S(1)}, u32[]{:S(2)}, u32[]{:S(2)}) collective-permute-start(bf16[256,256]{1,0:T(8,128)(2,1)S(1)} %get-tuple-element.108), channel_id=1, source_target_pairs={{0,1},{1,0},{2,3},{3,2},{4,5},{5,4},{6,7},{7,6},{8,9},{9,8},{10,11... | collective-permute-start | bytes 393224 | tf_op jit(solution)/shard_map/ppermute | solution.py:373
  63.0 8.4 %collective-permute-start.15 = (bf16[256,256]{1,0:T(8,128)(2,1)S(1)}, bf16[256,256]{1,0:T(8,128)(2,1)S(1)}, u32[]{:S(2)}, u32[]{:S(2)}) collective-permute-start(bf16[256,256]{1,0:T(8,128)(2,1)S(1)} %get-tuple-element.109), channel_id=1, source_target_pairs={{0,15},{1,2},{2,1},{3,4},{4,3},{5,6},{6,5},{7,8},{8,7},{9,10},{10,... | collective-permute-start | bytes 393224 | tf_op jit(solution)/shard_map/ppermute | solution.py:374
  69.2 5.1 %collective-permute-start.16 = (bf16[256,256]{1,0:T(8,128)(2,1)S(1)}, bf16[256,256]{1,0:T(8,128)(2,1)S(1)}, u32[]{:S(2)}, u32[]{:S(2)}) collective-permute-start(bf16[256,256]{1,0:T(8,128)(2,1)S(1)} %get-tuple-element.113), channel_id=1, source_target_pairs={{0,1},{1,0},{2,3},{3,2},{4,5},{5,4},{6,7},{7,6},{8,9},{9,8},{10,11... | collective-permute-start | bytes 393224 | tf_op jit(solution)/shard_map/ppermute | solution.py:373
  69.3 8.6 %collective-permute-start.17 = (bf16[256,256]{1,0:T(8,128)(2,1)S(1)}, bf16[256,256]{1,0:T(8,128)(2,1)S(1)}, u32[]{:S(2)}, u32[]{:S(2)}) collective-permute-start(bf16[256,256]{1,0:T(8,128)(2,1)S(1)} %get-tuple-element.114), channel_id=1, source_target_pairs={{0,15},{1,2},{2,1},{3,4},{4,3},{5,6},{6,5},{7,8},{8,7},{9,10},{10,... | collective-permute-start | bytes 393224 | tf_op jit(solution)/shard_map/ppermute | solution.py:374

commit v7 on v6

--- a/solution.py
+++ b/solution.py
@@ -177,7 +177,6 @@
 
     v = [r["v0"][s] for s in range(r["v0"].shape[0])]
     put_local(v, lambda w, s: r["left"][0, w, s], r, shift, ready=ready)
-    r["dots"][...] = dot_rows([v], v)
 
 
 def ghosts(k, facts, r):
@@ -216,13 +215,16 @@
         left = r["left"]
         env = (lambda w, s: left[0, w, s]) if len(left.shape) == 5 else (lambda w, s: left[w, s])
         put_local(v, env, r, shift)
-        r["dots"][...] = dot_rows(basis + [v], v)
+        if "dots" in r:
+            basis = basis + [v]
+            for j in range(k + 2):
+                r["dots"][j] = dot_rows(basis[: j + 1], basis[j])
     else:
         lanes = lax.broadcasted_iota(jnp.int32, (ROWS, LANES), 1)
         rows = lax.broadcasted_iota(jnp.int32, (ROWS, LANES), 0)
         line = jnp.zeros((1, LANES), F32)
         for j in range(ITERS + 1):
-            part = r[f"dots{j}"][...] if j < ITERS else dot_rows(basis + [v], v)
+            part = r["dots_before"][j] if j < ITERS else dot_rows(basis + [v], v)
             part = jnp.sum(part, axis=1, keepdims=True)
             line = line + jnp.sum(
                 jnp.where(lanes == ROWS * j + rows, part, 0.0), axis=0, keepdims=True
@@ -309,7 +311,6 @@
             r["env"][w, s] = jnp.where(first, kept, new).astype(BF16)
     v = [r["v0"][s] for s in range(held)]
     put_local(v, lambda w, s: r["env"][w, s], r, shift)
-    r["dots"][...] = dot_rows([v], v)
 
 
 def finish_kernel(shift, names, *refs):
@@ -360,8 +361,8 @@
     blocks = struct((held, cap, cap), F32)
     pair = struct((2, cap, cap), F32)
     triple = struct((3, cap, cap), BF16)
-    dots_of = struct((ROWS, LANES), F32)
-    local_outs = {"q": blocks, "inside": block, "across": block, "dots": dots_of}
+    token = struct((ROWS, LANES), F32)
+    local_outs = {"q": blocks, "inside": block, "across": block}
     pairs = [(i, i ^ 1) for i in range(size)]
     others = [(i, (i + 1 if i % 2 else i - 1) % size) for i in range(size)]
     segments = lax.axis_size("seg")
@@ -370,8 +371,8 @@
 
     def exchange(got):
         return {
+            "came_across": lax.ppermute(got["across"], "sec", others),
             "came_inside": lax.ppermute(got["inside"], "sec", pairs),
-            "came_across": lax.ppermute(got["across"], "sec", others),
         }
 
     def made(kernel, name, ins, outs, flops=0, **more):
@@ -409,7 +410,6 @@
 
     def relaxed(v0, came, got, env):
         basis = {"v0": v0}
-        dots = {"dots0": got["dots"]}
         for k in range(ITERS):
             ins = {"part": got["q"], **common, **basis, **came}
             if k > 0:
@@ -420,15 +420,14 @@
                 outs = {"v": blocks, "gives": pair, **local_outs}
                 if k + 2 == ITERS:
                     del outs["inside"], outs["across"]
+                    outs["dots"] = struct((ITERS, ROWS, LANES), F32)
             else:
                 del ins["right"]
-                ins.update(dots)
+                ins["dots_before"] = got["dots"]
                 outs = {"v": blocks, "line": struct((size, 1, LANES), F32)}
             kernel = functools.partial(step_kernel, k, shift)
             got = made(kernel, f"step{k}", ins, outs, flops=one * 36)
             basis[f"v{k + 1}"] = got["v"]
-            if k + 1 < ITERS:
-                dots[f"dots{k + 1}"] = got["dots"]
         return basis, lax.all_to_all(got["line"], "sec", 0, 0)
 
     got = made(
@@ -474,7 +473,7 @@
         grow_kernel,
         "grow",
         {"left": left, "factor": factor},
-        {"out": struct(left_env.shape, BF16), "token": dots_of},
+        {"out": struct(left_env.shape, BF16), "token": token},
         flops=one * 24,
         scratch=[
             pltpu.VMEM((terms, held, cap, cap), BF16),

time: 92.3 us -> 89.8 us (0.973)
  starting transfers between devices: 25 us -> 22.6 us
    ppermute x8, starting transfers between devices: 3.58 us -> 0.78 us  [exchange(): lax.ppermute(got['inside'], 'sec', pairs)]
where the time goes in v7:
time: 89.8 us; the launch traced here: 89.3 us
  Pallas kernels  25.6 us (29%)
  starting transfers between devices  22.6 us (25%)
  blocking collectives  21.3 us (24%)
  waiting for transfers between devices  18.8 us (21%)
  between operations  0.94 us (1%)
    pallas_call x14, Pallas kernels, call(): pl.pallas_call(kernel, out_shape=tuple(outs.values()), in_specs=specs or...  25.6 us
    ppermute x8, starting transfers between devices, exchange(): lax.ppermute(got['across'], 'sec', others)  21.7 us
    all_to_all x2, blocking collectives, relaxed(): return (basis, lax.all_to_all(got['line'], 'sec', 0, 0))  21.3 us
    ppermute x8, waiting for transfers between devices, exchange(): lax.ppermute(got['across'], 'sec', others)  13.1 us
    ppermute x1, waiting for transfers between devices, body(): earlier_factor = lax.ppermute(factor, 'seg', onward)  3.38 us
    ppermute x8, waiting for transfers between devices, exchange(): lax.ppermute(got['inside'], 'sec', pairs)  2.35 us
  transfers between devices with their start and end apart: 18, of which 8 were waited for; matrix products, arithmetic and copies ran while one was open for 0% of the time, Pallas kernels for 26%

profile of v7, /device:TPU:128, one launch (start us, length us, event | category | flops | bytes accessed | tf_op | source)
XLA Modules:
  0.0 89.3 jit_solution(2871317397192004758)
XLA Ops:
  0.7 1.8 %start.1 = (f32[2,256,256]{2,1,0:T(8,128)S(1)}, bf16[3,256,256]{2,1,0:T(8,128)(2,1)S(1)}, bf16[3,256,256]{2,1,0:T(8,128)(2,1)S(1)}, s32[8,128]{1,0:T(8,128)S(1)}) custom-call(s32[2]{0:T(128)S(1)} %pad_add_fusion.place, s32[1,32]{1,0:T(1,128)} %dims_at.1, f32[1,2,256,256]{3,2,1,0:T(8,128)} %psi_at.1, bf16[1,2,2,256,256]{4,3,2,1,0:T(8,128)(2,1)} %refs_4_.1, ...), custom_call_target="tpu_custom_call" | custom-call | bytes 1573000 | tf_op jit(solution)/shard_map/start/pallas_call | solution.py:336
  2.6 5.3 %collective-permute-start = (bf16[3,256,256]{2,1,0:T(8,128)(2,1)S(1)}, bf16[3,256,256]{2,1,0:T(8,128)(2,1)S(1)}, u32[]{:S(2)}, u32[]{:S(2)}) collective-permute-start(bf16[3,256,256]{2,1,0:T(8,128)(2,1)S(1)} %get-tuple-element.64), channel_id=1, source_target_pairs={{0,15},{1,2},{2,1},{3,4},{4,3},{5,6},{6,5},{7,8},{8,7},{9,10},{10,... | collective-permute-start | bytes 1179656 | tf_op jit(solution)/shard_map/ppermute | solution.py:374
  7.9 3.8 %local.1 = (bf16[1,6,2,256,256]{4,3,2,1,0:T(8,128)(2,1)S(1)}, bf16[1,6,2,256,256]{4,3,2,1,0:T(8,128)(2,1)S(1)}, bf16[1,2,2,256,256]{4,3,2,1,0:T(8,128)(2,1)S(1)}...) custom-call(s32[8,128]{1,0:T(8,128)S(1)} %get-tuple-element.58.refs_, ...), custom_call_target="tpu_custom_call" | custom-call | flops 939524096 | bytes 4722688 | tf_op jit(solution)/shard_map/local/pallas_call | solution.py:336
  13.9 3.8 %collective-permute-done.refs_6_.refs_10_.refs_12_.refs_13_ = bf16[3,256,256]{2,1,0:T(8,128)(2,1)S(1)} collective-permute-done((bf16[3,256,256]{2,1,0:T(8,128)(2,1)S(1)}, bf16[3,256,256]{2,1,0:T(8,128)(2,1)S(1)}, u32[]{:S(2)}, u32[]{:S(2)}) %collective-permute-start) | collective-permute-done | bytes 393248 | tf_op jit(solution)/shard_map/ppermute | solution.py:374
  17.7 2.2 %collective-permute-done.1.refs_7_.refs_9_.refs_11_.refs_12_ = bf16[3,256,256]{2,1,0:T(8,128)(2,1)S(1)} collective-permute-done((bf16[3,256,256]{2,1,0:T(8,128)(2,1)S(1)}, bf16[3,256,256]{2,1,0:T(8,128)(2,1)S(1)}, u32[]{:S(2)}, u32[]{:S(2)}) %collective-permute-start.1) | collective-permute-done | bytes 393248 | tf_op jit(solution)/shard_map/ppermute | solution.py:375
  19.8 1.9 %step0.2 = (f32[2,256,256]{2,1,0:T(8,128)S(1)}, f32[2,256,256]{2,1,0:T(8,128)S(1)}, f32[2,256,256]{2,1,0:T(8,128)S(1)}, bf16[256,256]{1,0:T(8,128)(2,1)S(1)}, bf16[256,256]{1,0:T(8,128)(2,1)S(1)}) custom-call(f32[2,256,256]{2,1,0:T(8,128)S(1)} %get-tuple-element.60.refs_0_, s32[8,128]{1,0:T(8,128)S(1)} %get-tuple-element.58.refs_0_.refs_1_.refs_5_, ...), custom_call_target="tpu_custom_call" | custom-call | flops 1207959552 | bytes 6819840 | tf_op jit(solution)/shard_map/step0/pallas_call | solution.py:336
  21.8 3.3 %collective-permute-start.4 = (bf16[256,256]{1,0:T(8,128)(2,1)S(1)}, bf16[256,256]{1,0:T(8,128)(2,1)S(1)}, u32[]{:S(2)}, u32[]{:S(2)}) collective-permute-start(bf16[256,256]{1,0:T(8,128)(2,1)S(1)} %get-tuple-element.74), channel_id=1, source_target_pairs={{0,15},{1,2},{2,1},{3,4},{4,3},{5,6},{6,5},{7,8},{8,7},{9,10},{10,... | collective-permute-start | bytes 393224 | tf_op jit(solution)/shard_map/ppermute | solution.py:374
  25.0 1.9 %step1.2 = (f32[2,256,256]{2,1,0:T(8,128)S(1)}, f32[2,256,256]{2,1,0:T(8,128)S(1)}, f32[2,256,256]{2,1,0:T(8,128)S(1)}, bf16[256,256]{1,0:T(8,128)(2,1)S(1)}, bf16[256,256]{1,0:T(8,128)(2,1)S(1)}) custom-call(f32[2,256,256]{2,1,0:T(8,128)S(1)} %get-tuple-element.67.refs_0_, s32[8,128]{1,0:T(8,128)S(1)} %get-tuple-element.58.refs_0_.refs_1_.refs_5_, ...), custom_call_target="tpu_custom_call" | custom-call | flops 1207959552 | bytes 7344128 | tf_op jit(solution)/shard_map/step1/pallas_call | solution.py:336
  27.0 2.3 %collective-permute-start.6 = (bf16[256,256]{1,0:T(8,128)(2,1)S(1)}, bf16[256,256]{1,0:T(8,128)(2,1)S(1)}, u32[]{:S(2)}, u32[]{:S(2)}) collective-permute-start(bf16[256,256]{1,0:T(8,128)(2,1)S(1)} %get-tuple-element.79), channel_id=1, source_target_pairs={{0,15},{1,2},{2,1},{3,4},{4,3},{5,6},{6,5},{7,8},{8,7},{9,10},{10,... | collective-permute-start | bytes 393224 | tf_op jit(solution)/shard_map/ppermute | solution.py:374
  30.5 2.2 %step2.2 = (f32[2,256,256]{2,1,0:T(8,128)S(1)}, f32[2,256,256]{2,1,0:T(8,128)S(1)}, f32[2,256,256]{2,1,0:T(8,128)S(1)}, f32[4,8,128]{2,1,0:T(8,128)S(1)}) custom-call(f32[2,256,256]{2,1,0:T(8,128)S(1)} %get-tuple-element.72.refs_0_, s32[8,128]{1,0:T(8,128)S(1)} %get-tuple-element.58.refs_0_.refs_1_.refs_5_, ...), custom_call_target="tpu_custom_call" | custom-call | flops 1207959552 | bytes 7868416 | tf_op jit(solution)/shard_map/step2/pallas_call | solution.py:336
  32.7 3.2 %collective-permute-done.6.refs_8_ = bf16[256,256]{1,0:T(8,128)(2,1)S(1)} collective-permute-done((bf16[256,256]{1,0:T(8,128)(2,1)S(1)}, bf16[256,256]{1,0:T(8,128)(2,1)S(1)}, u32[]{:S(2)}, u32[]{:S(2)}) %collective-permute-start.6) | collective-permute-done | bytes 131104 | tf_op jit(solution)/shard_map/ppermute | solution.py:374
  36.8 10.5 %all_to_all.10.refs_1_ = f32[16,1,128]{2,1,0:T(1,128)S(1)} all-to-all(f32[16,1,128]{2,1,0:T(1,128)S(1)} %get-tuple-element.83), channel_id=1, replica_groups=mesh['seg'=16,'sec'=16] {'sec'}, dimensions={0} | all-to-all | bytes 16384 | tf_op jit(solution)/shard_map/all_to_all | solution.py:431
  48.0 1.9 %collective-permute-start.10 = (bf16[256,256]{1,0:T(8,128)(2,1)S(1)}, bf16[256,256]{1,0:T(8,128)(2,1)S(1)}, u32[]{:S(2)}, u32[]{:S(2)}) collective-permute-start(bf16[256,256]{1,0:T(8,128)(2,1)S(1)} %get-tuple-element.89), channel_id=1, source_target_pairs={{0,15},{1,2},{2,1},{3,4},{4,3},{5,6},{6,5},{7,8},{8,7},{9,10},{10,... | collective-permute-start | bytes 393224 | tf_op jit(solution)/shard_map/ppermute | solution.py:374
  49.9 1.9 %grow.1 = (bf16[1,6,2,256,256]{4,3,2,1,0:T(8,128)(2,1)}, f32[8,128]{1,0:T(8,128)S(1)}) custom-call(bf16[1,6,2,256,256]{4,3,2,1,0:T(8,128)(2,1)S(1)} %get-tuple-element.66.refs_8_.refs_10_.refs_11_.left.refs_1_, bf16[2,272,256]{2,1,0:T(8,128)(2,1)S(1)} %get-tuple-element.86.factor), custom_call_target="tpu_custom_call" | custom-call | flops 805306368 | bytes 1851392 | tf_op jit(solution)/shard_map/grow/pallas_call | solution.py:336
  51.8 3.4 %collective-permute-done.9.refs_3_ = bf16[2,272,256]{2,1,0:T(8,128)(2,1)S(1)} collective-permute-done((bf16[2,272,256]{2,1,0:T(8,128)(2,1)S(1)}, bf16[2,272,256]{2,1,0:T(8,128)(2,1)S(1)}, u32[]{:S(2)}, u32[]{:S(2)}) %collective-permute-start.9) | collective-permute-done | bytes 278560 | tf_op jit(solution)/shard_map/ppermute | solution.py:470
  55.2 2.2 %second.1 = (bf16[6,2,256,256]{3,2,1,0:T(8,128)(2,1)S(1)}, f32[2,256,256]{2,1,0:T(8,128)S(1)}, bf16[256,256]{1,0:T(8,128)(2,1)S(1)}, bf16[256,256]{1,0:T(8,128)(2,1)S(1)}) custom-call(f32[2,256,256]{2,1,0:T(8,128)S(1)} %get-tuple-element.85.refs_0_.refs_5_.refs_4_.refs_2_, ...), custom_call_target="tpu_custom_call" | custom-call | flops 1744830464 | bytes 6578176 | tf_op jit(solution)/shard_map/second/pallas_call | solution.py:336
  57.4 1.9 %collective-permute-start.12 = (bf16[256,256]{1,0:T(8,128)(2,1)S(1)}, bf16[256,256]{1,0:T(8,128)(2,1)S(1)}, u32[]{:S(2)}, u32[]{:S(2)}) collective-permute-start(bf16[256,256]{1,0:T(8,128)(2,1)S(1)} %get-tuple-element.94), channel_id=1, source_target_pairs={{0,15},{1,2},{2,1},{3,4},{4,3},{5,6},{6,5},{7,8},{8,7},{9,10},{10,... | collective-permute-start | bytes 393224 | tf_op jit(solution)/shard_map/ppermute | solution.py:374
  59.3 1.9 %step0.3 = (f32[2,256,256]{2,1,0:T(8,128)S(1)}, f32[2,256,256]{2,1,0:T(8,128)S(1)}, f32[2,256,256]{2,1,0:T(8,128)S(1)}, bf16[256,256]{1,0:T(8,128)(2,1)S(1)}, bf16[256,256]{1,0:T(8,128)(2,1)S(1)}) custom-call(f32[2,256,256]{2,1,0:T(8,128)S(1)} %get-tuple-element.88.refs_0_, s32[8,128]{1,0:T(8,128)S(1)} %get-tuple-element.58.refs_0_.refs_1_.refs_5_, ...), custom_call_target="tpu_custom_call" | custom-call | flops 1207959552 | bytes 6295552 | tf_op jit(solution)/shard_map/step0/pallas_call | solution.py:336
  61.2 3.7 %collective-permute-start.14 = (bf16[256,256]{1,0:T(8,128)(2,1)S(1)}, bf16[256,256]{1,0:T(8,128)(2,1)S(1)}, u32[]{:S(2)}, u32[]{:S(2)}) collective-permute-start(bf16[256,256]{1,0:T(8,128)(2,1)S(1)} %get-tuple-element.99), channel_id=1, source_target_pairs={{0,15},{1,2},{2,1},{3,4},{4,3},{5,6},{6,5},{7,8},{8,7},{9,10},{10,... | collective-permute-start | bytes 393224 | tf_op jit(solution)/shard_map/ppermute | solution.py:374
  65.8 1.9 %step1.3 = (f32[2,256,256]{2,1,0:T(8,128)S(1)}, f32[2,256,256]{2,1,0:T(8,128)S(1)}, f32[2,256,256]{2,1,0:T(8,128)S(1)}, bf16[256,256]{1,0:T(8,128)(2,1)S(1)}, bf16[256,256]{1,0:T(8,128)(2,1)S(1)}) custom-call(f32[2,256,256]{2,1,0:T(8,128)S(1)} %get-tuple-element.92.refs_0_, s32[8,128]{1,0:T(8,128)S(1)} %get-tuple-element.58.refs_0_.refs_1_.refs_5_, ...), custom_call_target="tpu_custom_call" | custom-call | flops 1207959552 | bytes 7344128 | tf_op jit(solution)/shard_map/step1/pallas_call | solution.py:336
  67.7 2.1 %collective-permute-start.16 = (bf16[256,256]{1,0:T(8,128)(2,1)S(1)}, bf16[256,256]{1,0:T(8,128)(2,1)S(1)}, u32[]{:S(2)}, u32[]{:S(2)}) collective-permute-start(bf16[256,256]{1,0:T(8,128)(2,1)S(1)} %get-tuple-element.104), channel_id=1, source_target_pairs={{0,15},{1,2},{2,1},{3,4},{4,3},{5,6},{6,5},{7,8},{8,7},{9,10},{10,... | collective-permute-start | bytes 393224 | tf_op jit(solution)/shard_map/ppermute | solution.py:374
  69.8 2.2 %step2.3 = (f32[2,256,256]{2,1,0:T(8,128)S(1)}, f32[2,256,256]{2,1,0:T(8,128)S(1)}, f32[2,256,256]{2,1,0:T(8,128)S(1)}, f32[4,8,128]{2,1,0:T(8,128)S(1)}) custom-call(f32[2,256,256]{2,1,0:T(8,128)S(1)} %get-tuple-element.97.refs_0_, s32[8,128]{1,0:T(8,128)S(1)} %get-tuple-element.58.refs_0_.refs_1_.refs_5_, ...), custom_call_target="tpu_custom_call" | custom-call | flops 1207959552 | bytes 7868416 | tf_op jit(solution)/shard_map/step2/pallas_call | solution.py:336
  72.0 4.1 %collective-permute-done.16.refs_8_ = bf16[256,256]{1,0:T(8,128)(2,1)S(1)} collective-permute-done((bf16[256,256]{1,0:T(8,128)(2,1)S(1)}, bf16[256,256]{1,0:T(8,128)(2,1)S(1)}, u32[]{:S(2)}, u32[]{:S(2)}) %collective-permute-start.16) | collective-permute-done | bytes 131104 | tf_op jit(solution)/shard_map/ppermute | solution.py:374
  77.0 10.8 %all_to_all.11.refs_1_ = f32[16,1,128]{2,1,0:T(1,128)S(1)} all-to-all(f32[16,1,128]{2,1,0:T(1,128)S(1)} %get-tuple-element.108), channel_id=1, replica_groups=mesh['seg'=16,'sec'=16] {'sec'}, dimensions={0} | all-to-all | bytes 16384 | tf_op jit(solution)/shard_map/all_to_all | solution.py:431
  (29 shorter events, 8.4 us)
Async XLA Ops:
  0.6 54.5 %collective-permute-start.8 = (bf16[1,6,2,256,256]{4,3,2,1,0:T(8,128)(2,1)}, bf16[1,6,2,256,256]{4,3,2,1,0:T(8,128)(2,1)S(1)}, u32[]{:S(2)}, u32[]{:S(2)}) collective-permute-start(bf16[1,6,2,256,256]{4,3,2,1,0:T(8,128)(2,1)} %refs_2_.1), channel_id=1, source_target_pairs={{0,16},{16,32},{32,48},{48,64},{64,80},{80,96},{96,112},{112,128},... | collective-permute-start | bytes 4718600 | tf_op jit(solution)/shard_map/ppermute | solution.py:409
  2.6 15.1 %collective-permute-start = (bf16[3,256,256]{2,1,0:T(8,128)(2,1)S(1)}, bf16[3,256,256]{2,1,0:T(8,128)(2,1)S(1)}, u32[]{:S(2)}, u32[]{:S(2)}) collective-permute-start(bf16[3,256,256]{2,1,0:T(8,128)(2,1)S(1)} %get-tuple-element.64), channel_id=1, source_target_pairs={{0,15},{1,2},{2,1},{3,4},{4,3},{5,6},{6,5},{7,8},{8,7},{9,10},{10,... | collective-permute-start | bytes 1179656 | tf_op jit(solution)/shard_map/ppermute | solution.py:374
  7.9 12.0 %collective-permute-start.1 = (bf16[3,256,256]{2,1,0:T(8,128)(2,1)S(1)}, bf16[3,256,256]{2,1,0:T(8,128)(2,1)S(1)}, u32[]{:S(2)}, u32[]{:S(2)}) collective-permute-start(bf16[3,256,256]{2,1,0:T(8,128)(2,1)S(1)} %get-tuple-element.65), channel_id=1, source_target_pairs={{0,1},{1,0},{2,3},{3,2},{4,5},{5,4},{6,7},{7,6},{8,9},{9,8},{10,11... | collective-permute-start | bytes 1179656 | tf_op jit(solution)/shard_map/ppermute | solution.py:375
  11.7 13.3 %collective-permute-start.2 = (bf16[256,256]{1,0:T(8,128)(2,1)S(1)}, bf16[256,256]{1,0:T(8,128)(2,1)S(1)}, u32[]{:S(2)}, u32[]{:S(2)}) collective-permute-start(bf16[256,256]{1,0:T(8,128)(2,1)S(1)} %get-tuple-element.69), channel_id=1, source_target_pairs={{0,15},{1,2},{2,1},{3,4},{4,3},{5,6},{6,5},{7,8},{8,7},{9,10},{10,... | collective-permute-start | bytes 393224 | tf_op jit(solution)/shard_map/ppermute | solution.py:374
  13.1 11.9 %collective-permute-start.3 = (bf16[256,256]{1,0:T(8,128)(2,1)S(1)}, bf16[256,256]{1,0:T(8,128)(2,1)S(1)}, u32[]{:S(2)}, u32[]{:S(2)}) collective-permute-start(bf16[256,256]{1,0:T(8,128)(2,1)S(1)} %get-tuple-element.70), channel_id=1, source_target_pairs={{0,1},{1,0},{2,3},{3,2},{4,5},{5,4},{6,7},{7,6},{8,9},{9,8},{10,11... | collective-permute-start | bytes 393224 | tf_op jit(solution)/shard_map/ppermute | solution.py:375
  21.8 8.6 %collective-permute-start.4 = (bf16[256,256]{1,0:T(8,128)(2,1)S(1)}, bf16[256,256]{1,0:T(8,128)(2,1)S(1)}, u32[]{:S(2)}, u32[]{:S(2)}) collective-permute-start(bf16[256,256]{1,0:T(8,128)(2,1)S(1)} %get-tuple-element.74), channel_id=1, source_target_pairs={{0,15},{1,2},{2,1},{3,4},{4,3},{5,6},{6,5},{7,8},{8,7},{9,10},{10,... | collective-permute-start | bytes 393224 | tf_op jit(solution)/shard_map/ppermute | solution.py:374
  25.0 5.5 %collective-permute-start.5 = (bf16[256,256]{1,0:T(8,128)(2,1)S(1)}, bf16[256,256]{1,0:T(8,128)(2,1)S(1)}, u32[]{:S(2)}, u32[]{:S(2)}) collective-permute-start(bf16[256,256]{1,0:T(8,128)(2,1)S(1)} %get-tuple-element.75), channel_id=1, source_target_pairs={{0,1},{1,0},{2,3},{3,2},{4,5},{5,4},{6,7},{7,6},{8,9},{9,8},{10,11... | collective-permute-start | bytes 393224 | tf_op jit(solution)/shard_map/ppermute | solution.py:375
  27.0 8.9 %collective-permute-start.6 = (bf16[256,256]{1,0:T(8,128)(2,1)S(1)}, bf16[256,256]{1,0:T(8,128)(2,1)S(1)}, u32[]{:S(2)}, u32[]{:S(2)}) collective-permute-start(bf16[256,256]{1,0:T(8,128)(2,1)S(1)} %get-tuple-element.79), channel_id=1, source_target_pairs={{0,15},{1,2},{2,1},{3,4},{4,3},{5,6},{6,5},{7,8},{8,7},{9,10},{10,... | collective-permute-start | bytes 393224 | tf_op jit(solution)/shard_map/ppermute | solution.py:374
  29.2 6.7 %collective-permute-start.7 = (bf16[256,256]{1,0:T(8,128)(2,1)S(1)}, bf16[256,256]{1,0:T(8,128)(2,1)S(1)}, u32[]{:S(2)}, u32[]{:S(2)}) collective-permute-start(bf16[256,256]{1,0:T(8,128)(2,1)S(1)} %get-tuple-element.80), channel_id=1, source_target_pairs={{0,1},{1,0},{2,3},{3,2},{4,5},{5,4},{6,7},{7,6},{8,9},{9,8},{10,11... | collective-permute-start | bytes 393224 | tf_op jit(solution)/shard_map/ppermute | solution.py:375
  48.0 7.2 %collective-permute-start.9 = (bf16[2,272,256]{2,1,0:T(8,128)(2,1)S(1)}, bf16[2,272,256]{2,1,0:T(8,128)(2,1)S(1)}, u32[]{:S(2)}, u32[]{:S(2)}) collective-permute-start(bf16[2,272,256]{2,1,0:T(8,128)(2,1)S(1)} %get-tuple-element.86.factor), channel_id=1, source_target_pairs={{0,16},{16,32},{32,48},{48,64},{64,80},{80,96},{96,112},{112,128},... | collective-permute-start | bytes 835592 | tf_op jit(solution)/shard_map/ppermute | solution.py:470
  48.0 11.3 %collective-permute-start.10 = (bf16[256,256]{1,0:T(8,128)(2,1)S(1)}, bf16[256,256]{1,0:T(8,128)(2,1)S(1)}, u32[]{:S(2)}, u32[]{:S(2)}) collective-permute-start(bf16[256,256]{1,0:T(8,128)(2,1)S(1)} %get-tuple-element.89), channel_id=1, source_target_pairs={{0,15},{1,2},{2,1},{3,4},{4,3},{5,6},{6,5},{7,8},{8,7},{9,10},{10,... | collective-permute-start | bytes 393224 | tf_op jit(solution)/shard_map/ppermute | solution.py:374
  49.9 9.4 %collective-permute-start.11 = (bf16[256,256]{1,0:T(8,128)(2,1)S(1)}, bf16[256,256]{1,0:T(8,128)(2,1)S(1)}, u32[]{:S(2)}, u32[]{:S(2)}) collective-permute-start(bf16[256,256]{1,0:T(8,128)(2,1)S(1)} %get-tuple-element.90), channel_id=1, source_target_pairs={{0,1},{1,0},{2,3},{3,2},{4,5},{5,4},{6,7},{7,6},{8,9},{9,8},{10,11... | collective-permute-start | bytes 393224 | tf_op jit(solution)/shard_map/ppermute | solution.py:375
  57.4 8.4 %collective-permute-start.12 = (bf16[256,256]{1,0:T(8,128)(2,1)S(1)}, bf16[256,256]{1,0:T(8,128)(2,1)S(1)}, u32[]{:S(2)}, u32[]{:S(2)}) collective-permute-start(bf16[256,256]{1,0:T(8,128)(2,1)S(1)} %get-tuple-element.94), channel_id=1, source_target_pairs={{0,15},{1,2},{2,1},{3,4},{4,3},{5,6},{6,5},{7,8},{8,7},{9,10},{10,... | collective-permute-start | bytes 393224 | tf_op jit(solution)/shard_map/ppermute | solution.py:374
  59.3 6.5 %collective-permute-start.13 = (bf16[256,256]{1,0:T(8,128)(2,1)S(1)}, bf16[256,256]{1,0:T(8,128)(2,1)S(1)}, u32[]{:S(2)}, u32[]{:S(2)}) collective-permute-start(bf16[256,256]{1,0:T(8,128)(2,1)S(1)} %get-tuple-element.95), channel_id=1, source_target_pairs={{0,1},{1,0},{2,3},{3,2},{4,5},{5,4},{6,7},{7,6},{8,9},{9,8},{10,11... | collective-permute-start | bytes 393224 | tf_op jit(solution)/shard_map/ppermute | solution.py:375
  61.2 8.6 %collective-permute-start.14 = (bf16[256,256]{1,0:T(8,128)(2,1)S(1)}, bf16[256,256]{1,0:T(8,128)(2,1)S(1)}, u32[]{:S(2)}, u32[]{:S(2)}) collective-permute-start(bf16[256,256]{1,0:T(8,128)(2,1)S(1)} %get-tuple-element.99), channel_id=1, source_target_pairs={{0,15},{1,2},{2,1},{3,4},{4,3},{5,6},{6,5},{7,8},{8,7},{9,10},{10,... | collective-permute-start | bytes 393224 | tf_op jit(solution)/shard_map/ppermute | solution.py:374
  64.9 5.0 %collective-permute-start.15 = (bf16[256,256]{1,0:T(8,128)(2,1)S(1)}, bf16[256,256]{1,0:T(8,128)(2,1)S(1)}, u32[]{:S(2)}, u32[]{:S(2)}) collective-permute-start(bf16[256,256]{1,0:T(8,128)(2,1)S(1)} %get-tuple-element.100), channel_id=1, source_target_pairs={{0,1},{1,0},{2,3},{3,2},{4,5},{5,4},{6,7},{7,6},{8,9},{9,8},{10,11... | collective-permute-start | bytes 393224 | tf_op jit(solution)/shard_map/ppermute | solution.py:375
  67.7 8.4 %collective-permute-start.16 = (bf16[256,256]{1,0:T(8,128)(2,1)S(1)}, bf16[256,256]{1,0:T(8,128)(2,1)S(1)}, u32[]{:S(2)}, u32[]{:S(2)}) collective-permute-start(bf16[256,256]{1,0:T(8,128)(2,1)S(1)} %get-tuple-element.104), channel_id=1, source_target_pairs={{0,15},{1,2},{2,1},{3,4},{4,3},{5,6},{6,5},{7,8},{8,7},{9,10},{10,... | collective-permute-start | bytes 393224 | tf_op jit(solution)/shard_map/ppermute | solution.py:374
  69.8 6.3 %collective-permute-start.17 = (bf16[256,256]{1,0:T(8,128)(2,1)S(1)}, bf16[256,256]{1,0:T(8,128)(2,1)S(1)}, u32[]{:S(2)}, u32[]{:S(2)}) collective-permute-start(bf16[256,256]{1,0:T(8,128)(2,1)S(1)} %get-tuple-element.105), channel_id=1, source_target_pairs={{0,1},{1,0},{2,3},{3,2},{4,5},{5,4},{6,7},{7,6},{8,9},{9,8},{10,11... | collective-permute-start | bytes 393224 | tf_op jit(solution)/shard_map/ppermute | solution.py:375

commit v8 on v7

--- a/solution.py
+++ b/solution.py
@@ -284,7 +284,7 @@
     cap = env.shape[0]
     block = factor[:cap]
     product = nn(block.T, nn(env, block).astype(BF16))
-    return (product / factor[cap : cap + 1].astype(F32)).astype(BF16)
+    return (product * (1.0 / factor[cap : cap + 1].astype(F32))).astype(BF16)
 
 
 def grow_kernel(left, factor, out, token, held_out, sent):

time: 89.8 us -> 89.8 us (level)
  no operation moved by 1% of the time
where the time goes in v8:
time: 89.8 us; the launch traced here: 89.3 us
  Pallas kernels  25.6 us (29%)
  starting transfers between devices  22.6 us (25%)
  blocking collectives  21.3 us (24%)
  waiting for transfers between devices  18.8 us (21%)
  between operations  0.94 us (1%)
    pallas_call x14, Pallas kernels, call(): pl.pallas_call(kernel, out_shape=tuple(outs.values()), in_specs=specs or...  25.6 us
    ppermute x8, starting transfers between devices, exchange(): lax.ppermute(got['across'], 'sec', others)  21.7 us
    all_to_all x2, blocking collectives, relaxed(): return (basis, lax.all_to_all(got['line'], 'sec', 0, 0))  21.3 us
    ppermute x8, waiting for transfers between devices, exchange(): lax.ppermute(got['across'], 'sec', others)  13.1 us
    ppermute x1, waiting for transfers between devices, body(): earlier_factor = lax.ppermute(factor, 'seg', onward)  3.38 us
    ppermute x8, waiting for transfers between devices, exchange(): lax.ppermute(got['inside'], 'sec', pairs)  2.35 us
  transfers between devices with their start and end apart: 18, of which 8 were waited for; matrix products, arithmetic and copies ran while one was open for 0% of the time, Pallas kernels for 26%

profile of v8, /device:TPU:128, one launch (start us, length us, event | category | flops | bytes accessed | tf_op | source)
XLA Modules:
  0.0 89.3 jit_solution(18174669539202644250)
XLA Ops:
  0.7 1.8 %start.1 = (f32[2,256,256]{2,1,0:T(8,128)S(1)}, bf16[3,256,256]{2,1,0:T(8,128)(2,1)S(1)}, bf16[3,256,256]{2,1,0:T(8,128)(2,1)S(1)}, s32[8,128]{1,0:T(8,128)S(1)}) custom-call(s32[2]{0:T(128)S(1)} %pad_add_fusion.place, s32[1,32]{1,0:T(1,128)} %dims_at.1, f32[1,2,256,256]{3,2,1,0:T(8,128)} %psi_at.1, bf16[1,2,2,256,256]{4,3,2,1,0:T(8,128)(2,1)} %refs_4_.1, ...), custom_call_target="tpu_custom_call" | custom-call | bytes 1573000 | tf_op jit(solution)/shard_map/start/pallas_call | solution.py:336
  2.6 5.3 %collective-permute-start = (bf16[3,256,256]{2,1,0:T(8,128)(2,1)S(1)}, bf16[3,256,256]{2,1,0:T(8,128)(2,1)S(1)}, u32[]{:S(2)}, u32[]{:S(2)}) collective-permute-start(bf16[3,256,256]{2,1,0:T(8,128)(2,1)S(1)} %get-tuple-element.64), channel_id=1, source_target_pairs={{0,15},{1,2},{2,1},{3,4},{4,3},{5,6},{6,5},{7,8},{8,7},{9,10},{10,... | collective-permute-start | bytes 1179656 | tf_op jit(solution)/shard_map/ppermute | solution.py:374
  7.9 3.8 %local.1 = (bf16[1,6,2,256,256]{4,3,2,1,0:T(8,128)(2,1)S(1)}, bf16[1,6,2,256,256]{4,3,2,1,0:T(8,128)(2,1)S(1)}, bf16[1,2,2,256,256]{4,3,2,1,0:T(8,128)(2,1)S(1)}...) custom-call(s32[8,128]{1,0:T(8,128)S(1)} %get-tuple-element.58.refs_, ...), custom_call_target="tpu_custom_call" | custom-call | flops 939524096 | bytes 4722688 | tf_op jit(solution)/shard_map/local/pallas_call | solution.py:336
  13.9 3.8 %collective-permute-done.refs_6_.refs_10_.refs_12_.refs_13_ = bf16[3,256,256]{2,1,0:T(8,128)(2,1)S(1)} collective-permute-done((bf16[3,256,256]{2,1,0:T(8,128)(2,1)S(1)}, bf16[3,256,256]{2,1,0:T(8,128)(2,1)S(1)}, u32[]{:S(2)}, u32[]{:S(2)}) %collective-permute-start) | collective-permute-done | bytes 393248 | tf_op jit(solution)/shard_map/ppermute | solution.py:374
  17.7 2.2 %collective-permute-done.1.refs_7_.refs_9_.refs_11_.refs_12_ = bf16[3,256,256]{2,1,0:T(8,128)(2,1)S(1)} collective-permute-done((bf16[3,256,256]{2,1,0:T(8,128)(2,1)S(1)}, bf16[3,256,256]{2,1,0:T(8,128)(2,1)S(1)}, u32[]{:S(2)}, u32[]{:S(2)}) %collective-permute-start.1) | collective-permute-done | bytes 393248 | tf_op jit(solution)/shard_map/ppermute | solution.py:375
  19.8 1.9 %step0.2 = (f32[2,256,256]{2,1,0:T(8,128)S(1)}, f32[2,256,256]{2,1,0:T(8,128)S(1)}, f32[2,256,256]{2,1,0:T(8,128)S(1)}, bf16[256,256]{1,0:T(8,128)(2,1)S(1)}, bf16[256,256]{1,0:T(8,128)(2,1)S(1)}) custom-call(f32[2,256,256]{2,1,0:T(8,128)S(1)} %get-tuple-element.60.refs_0_, s32[8,128]{1,0:T(8,128)S(1)} %get-tuple-element.58.refs_0_.refs_1_.refs_5_, ...), custom_call_target="tpu_custom_call" | custom-call | flops 1207959552 | bytes 6819840 | tf_op jit(solution)/shard_map/step0/pallas_call | solution.py:336
  21.8 3.3 %collective-permute-start.4 = (bf16[256,256]{1,0:T(8,128)(2,1)S(1)}, bf16[256,256]{1,0:T(8,128)(2,1)S(1)}, u32[]{:S(2)}, u32[]{:S(2)}) collective-permute-start(bf16[256,256]{1,0:T(8,128)(2,1)S(1)} %get-tuple-element.74), channel_id=1, source_target_pairs={{0,15},{1,2},{2,1},{3,4},{4,3},{5,6},{6,5},{7,8},{8,7},{9,10},{10,... | collective-permute-start | bytes 393224 | tf_op jit(solution)/shard_map/ppermute | solution.py:374
  25.0 1.9 %step1.2 = (f32[2,256,256]{2,1,0:T(8,128)S(1)}, f32[2,256,256]{2,1,0:T(8,128)S(1)}, f32[2,256,256]{2,1,0:T(8,128)S(1)}, bf16[256,256]{1,0:T(8,128)(2,1)S(1)}, bf16[256,256]{1,0:T(8,128)(2,1)S(1)}) custom-call(f32[2,256,256]{2,1,0:T(8,128)S(1)} %get-tuple-element.67.refs_0_, s32[8,128]{1,0:T(8,128)S(1)} %get-tuple-element.58.refs_0_.refs_1_.refs_5_, ...), custom_call_target="tpu_custom_call" | custom-call | flops 1207959552 | bytes 7344128 | tf_op jit(solution)/shard_map/step1/pallas_call | solution.py:336
  27.0 2.3 %collective-permute-start.6 = (bf16[256,256]{1,0:T(8,128)(2,1)S(1)}, bf16[256,256]{1,0:T(8,128)(2,1)S(1)}, u32[]{:S(2)}, u32[]{:S(2)}) collective-permute-start(bf16[256,256]{1,0:T(8,128)(2,1)S(1)} %get-tuple-element.79), channel_id=1, source_target_pairs={{0,15},{1,2},{2,1},{3,4},{4,3},{5,6},{6,5},{7,8},{8,7},{9,10},{10,... | collective-permute-start | bytes 393224 | tf_op jit(solution)/shard_map/ppermute | solution.py:374
  30.5 2.2 %step2.2 = (f32[2,256,256]{2,1,0:T(8,128)S(1)}, f32[2,256,256]{2,1,0:T(8,128)S(1)}, f32[2,256,256]{2,1,0:T(8,128)S(1)}, f32[4,8,128]{2,1,0:T(8,128)S(1)}) custom-call(f32[2,256,256]{2,1,0:T(8,128)S(1)} %get-tuple-element.72.refs_0_, s32[8,128]{1,0:T(8,128)S(1)} %get-tuple-element.58.refs_0_.refs_1_.refs_5_, ...), custom_call_target="tpu_custom_call" | custom-call | flops 1207959552 | bytes 7868416 | tf_op jit(solution)/shard_map/step2/pallas_call | solution.py:336
  32.7 3.2 %collective-permute-done.6.refs_8_ = bf16[256,256]{1,0:T(8,128)(2,1)S(1)} collective-permute-done((bf16[256,256]{1,0:T(8,128)(2,1)S(1)}, bf16[256,256]{1,0:T(8,128)(2,1)S(1)}, u32[]{:S(2)}, u32[]{:S(2)}) %collective-permute-start.6) | collective-permute-done | bytes 131104 | tf_op jit(solution)/shard_map/ppermute | solution.py:374
  36.8 10.5 %all_to_all.10.refs_1_ = f32[16,1,128]{2,1,0:T(1,128)S(1)} all-to-all(f32[16,1,128]{2,1,0:T(1,128)S(1)} %get-tuple-element.83), channel_id=1, replica_groups=mesh['seg'=16,'sec'=16] {'sec'}, dimensions={0} | all-to-all | bytes 16384 | tf_op jit(solution)/shard_map/all_to_all | solution.py:431
  48.0 1.9 %collective-permute-start.10 = (bf16[256,256]{1,0:T(8,128)(2,1)S(1)}, bf16[256,256]{1,0:T(8,128)(2,1)S(1)}, u32[]{:S(2)}, u32[]{:S(2)}) collective-permute-start(bf16[256,256]{1,0:T(8,128)(2,1)S(1)} %get-tuple-element.89), channel_id=1, source_target_pairs={{0,15},{1,2},{2,1},{3,4},{4,3},{5,6},{6,5},{7,8},{8,7},{9,10},{10,... | collective-permute-start | bytes 393224 | tf_op jit(solution)/shard_map/ppermute | solution.py:374
  49.9 1.9 %grow.1 = (bf16[1,6,2,256,256]{4,3,2,1,0:T(8,128)(2,1)}, f32[8,128]{1,0:T(8,128)S(1)}) custom-call(bf16[1,6,2,256,256]{4,3,2,1,0:T(8,128)(2,1)S(1)} %get-tuple-element.66.refs_8_.refs_10_.refs_11_.left.refs_1_, bf16[2,272,256]{2,1,0:T(8,128)(2,1)S(1)} %get-tuple-element.86.factor), custom_call_target="tpu_custom_call" | custom-call | flops 805306368 | bytes 1851392 | tf_op jit(solution)/shard_map/grow/pallas_call | solution.py:336
  51.8 3.4 %collective-permute-done.9.refs_3_ = bf16[2,272,256]{2,1,0:T(8,128)(2,1)S(1)} collective-permute-done((bf16[2,272,256]{2,1,0:T(8,128)(2,1)S(1)}, bf16[2,272,256]{2,1,0:T(8,128)(2,1)S(1)}, u32[]{:S(2)}, u32[]{:S(2)}) %collective-permute-start.9) | collective-permute-done | bytes 278560 | tf_op jit(solution)/shard_map/ppermute | solution.py:470
  55.2 2.2 %second.1 = (bf16[6,2,256,256]{3,2,1,0:T(8,128)(2,1)S(1)}, f32[2,256,256]{2,1,0:T(8,128)S(1)}, bf16[256,256]{1,0:T(8,128)(2,1)S(1)}, bf16[256,256]{1,0:T(8,128)(2,1)S(1)}) custom-call(f32[2,256,256]{2,1,0:T(8,128)S(1)} %get-tuple-element.85.refs_0_.refs_5_.refs_4_.refs_2_, ...), custom_call_target="tpu_custom_call" | custom-call | flops 1744830464 | bytes 6578176 | tf_op jit(solution)/shard_map/second/pallas_call | solution.py:336
  57.4 1.9 %collective-permute-start.12 = (bf16[256,256]{1,0:T(8,128)(2,1)S(1)}, bf16[256,256]{1,0:T(8,128)(2,1)S(1)}, u32[]{:S(2)}, u32[]{:S(2)}) collective-permute-start(bf16[256,256]{1,0:T(8,128)(2,1)S(1)} %get-tuple-element.94), channel_id=1, source_target_pairs={{0,15},{1,2},{2,1},{3,4},{4,3},{5,6},{6,5},{7,8},{8,7},{9,10},{10,... | collective-permute-start | bytes 393224 | tf_op jit(solution)/shard_map/ppermute | solution.py:374
  59.3 1.9 %step0.3 = (f32[2,256,256]{2,1,0:T(8,128)S(1)}, f32[2,256,256]{2,1,0:T(8,128)S(1)}, f32[2,256,256]{2,1,0:T(8,128)S(1)}, bf16[256,256]{1,0:T(8,128)(2,1)S(1)}, bf16[256,256]{1,0:T(8,128)(2,1)S(1)}) custom-call(f32[2,256,256]{2,1,0:T(8,128)S(1)} %get-tuple-element.88.refs_0_, s32[8,128]{1,0:T(8,128)S(1)} %get-tuple-element.58.refs_0_.refs_1_.refs_5_, ...), custom_call_target="tpu_custom_call" | custom-call | flops 1207959552 | bytes 6295552 | tf_op jit(solution)/shard_map/step0/pallas_call | solution.py:336
  61.2 3.7 %collective-permute-start.14 = (bf16[256,256]{1,0:T(8,128)(2,1)S(1)}, bf16[256,256]{1,0:T(8,128)(2,1)S(1)}, u32[]{:S(2)}, u32[]{:S(2)}) collective-permute-start(bf16[256,256]{1,0:T(8,128)(2,1)S(1)} %get-tuple-element.99), channel_id=1, source_target_pairs={{0,15},{1,2},{2,1},{3,4},{4,3},{5,6},{6,5},{7,8},{8,7},{9,10},{10,... | collective-permute-start | bytes 393224 | tf_op jit(solution)/shard_map/ppermute | solution.py:374
  65.8 1.9 %step1.3 = (f32[2,256,256]{2,1,0:T(8,128)S(1)}, f32[2,256,256]{2,1,0:T(8,128)S(1)}, f32[2,256,256]{2,1,0:T(8,128)S(1)}, bf16[256,256]{1,0:T(8,128)(2,1)S(1)}, bf16[256,256]{1,0:T(8,128)(2,1)S(1)}) custom-call(f32[2,256,256]{2,1,0:T(8,128)S(1)} %get-tuple-element.92.refs_0_, s32[8,128]{1,0:T(8,128)S(1)} %get-tuple-element.58.refs_0_.refs_1_.refs_5_, ...), custom_call_target="tpu_custom_call" | custom-call | flops 1207959552 | bytes 7344128 | tf_op jit(solution)/shard_map/step1/pallas_call | solution.py:336
  67.7 2.1 %collective-permute-start.16 = (bf16[256,256]{1,0:T(8,128)(2,1)S(1)}, bf16[256,256]{1,0:T(8,128)(2,1)S(1)}, u32[]{:S(2)}, u32[]{:S(2)}) collective-permute-start(bf16[256,256]{1,0:T(8,128)(2,1)S(1)} %get-tuple-element.104), channel_id=1, source_target_pairs={{0,15},{1,2},{2,1},{3,4},{4,3},{5,6},{6,5},{7,8},{8,7},{9,10},{10,... | collective-permute-start | bytes 393224 | tf_op jit(solution)/shard_map/ppermute | solution.py:374
  69.8 2.2 %step2.3 = (f32[2,256,256]{2,1,0:T(8,128)S(1)}, f32[2,256,256]{2,1,0:T(8,128)S(1)}, f32[2,256,256]{2,1,0:T(8,128)S(1)}, f32[4,8,128]{2,1,0:T(8,128)S(1)}) custom-call(f32[2,256,256]{2,1,0:T(8,128)S(1)} %get-tuple-element.97.refs_0_, s32[8,128]{1,0:T(8,128)S(1)} %get-tuple-element.58.refs_0_.refs_1_.refs_5_, ...), custom_call_target="tpu_custom_call" | custom-call | flops 1207959552 | bytes 7868416 | tf_op jit(solution)/shard_map/step2/pallas_call | solution.py:336
  72.0 4.1 %collective-permute-done.16.refs_8_ = bf16[256,256]{1,0:T(8,128)(2,1)S(1)} collective-permute-done((bf16[256,256]{1,0:T(8,128)(2,1)S(1)}, bf16[256,256]{1,0:T(8,128)(2,1)S(1)}, u32[]{:S(2)}, u32[]{:S(2)}) %collective-permute-start.16) | collective-permute-done | bytes 131104 | tf_op jit(solution)/shard_map/ppermute | solution.py:374
  77.0 10.8 %all_to_all.11.refs_1_ = f32[16,1,128]{2,1,0:T(1,128)S(1)} all-to-all(f32[16,1,128]{2,1,0:T(1,128)S(1)} %get-tuple-element.108), channel_id=1, replica_groups=mesh['seg'=16,'sec'=16] {'sec'}, dimensions={0} | all-to-all | bytes 16384 | tf_op jit(solution)/shard_map/all_to_all | solution.py:431
  (29 shorter events, 8.4 us)
Async XLA Ops:
  0.6 54.5 %collective-permute-start.8 = (bf16[1,6,2,256,256]{4,3,2,1,0:T(8,128)(2,1)}, bf16[1,6,2,256,256]{4,3,2,1,0:T(8,128)(2,1)S(1)}, u32[]{:S(2)}, u32[]{:S(2)}) collective-permute-start(bf16[1,6,2,256,256]{4,3,2,1,0:T(8,128)(2,1)} %refs_2_.1), channel_id=1, source_target_pairs={{0,16},{16,32},{32,48},{48,64},{64,80},{80,96},{96,112},{112,128},... | collective-permute-start | bytes 4718600 | tf_op jit(solution)/shard_map/ppermute | solution.py:409
  2.6 15.1 %collective-permute-start = (bf16[3,256,256]{2,1,0:T(8,128)(2,1)S(1)}, bf16[3,256,256]{2,1,0:T(8,128)(2,1)S(1)}, u32[]{:S(2)}, u32[]{:S(2)}) collective-permute-start(bf16[3,256,256]{2,1,0:T(8,128)(2,1)S(1)} %get-tuple-element.64), channel_id=1, source_target_pairs={{0,15},{1,2},{2,1},{3,4},{4,3},{5,6},{6,5},{7,8},{8,7},{9,10},{10,... | collective-permute-start | bytes 1179656 | tf_op jit(solution)/shard_map/ppermute | solution.py:374
  7.9 12.0 %collective-permute-start.1 = (bf16[3,256,256]{2,1,0:T(8,128)(2,1)S(1)}, bf16[3,256,256]{2,1,0:T(8,128)(2,1)S(1)}, u32[]{:S(2)}, u32[]{:S(2)}) collective-permute-start(bf16[3,256,256]{2,1,0:T(8,128)(2,1)S(1)} %get-tuple-element.65), channel_id=1, source_target_pairs={{0,1},{1,0},{2,3},{3,2},{4,5},{5,4},{6,7},{7,6},{8,9},{9,8},{10,11... | collective-permute-start | bytes 1179656 | tf_op jit(solution)/shard_map/ppermute | solution.py:375
  11.7 13.3 %collective-permute-start.2 = (bf16[256,256]{1,0:T(8,128)(2,1)S(1)}, bf16[256,256]{1,0:T(8,128)(2,1)S(1)}, u32[]{:S(2)}, u32[]{:S(2)}) collective-permute-start(bf16[256,256]{1,0:T(8,128)(2,1)S(1)} %get-tuple-element.69), channel_id=1, source_target_pairs={{0,15},{1,2},{2,1},{3,4},{4,3},{5,6},{6,5},{7,8},{8,7},{9,10},{10,... | collective-permute-start | bytes 393224 | tf_op jit(solution)/shard_map/ppermute | solution.py:374
  13.1 11.9 %collective-permute-start.3 = (bf16[256,256]{1,0:T(8,128)(2,1)S(1)}, bf16[256,256]{1,0:T(8,128)(2,1)S(1)}, u32[]{:S(2)}, u32[]{:S(2)}) collective-permute-start(bf16[256,256]{1,0:T(8,128)(2,1)S(1)} %get-tuple-element.70), channel_id=1, source_target_pairs={{0,1},{1,0},{2,3},{3,2},{4,5},{5,4},{6,7},{7,6},{8,9},{9,8},{10,11... | collective-permute-start | bytes 393224 | tf_op jit(solution)/shard_map/ppermute | solution.py:375
  21.8 8.6 %collective-permute-start.4 = (bf16[256,256]{1,0:T(8,128)(2,1)S(1)}, bf16[256,256]{1,0:T(8,128)(2,1)S(1)}, u32[]{:S(2)}, u32[]{:S(2)}) collective-permute-start(bf16[256,256]{1,0:T(8,128)(2,1)S(1)} %get-tuple-element.74), channel_id=1, source_target_pairs={{0,15},{1,2},{2,1},{3,4},{4,3},{5,6},{6,5},{7,8},{8,7},{9,10},{10,... | collective-permute-start | bytes 393224 | tf_op jit(solution)/shard_map/ppermute | solution.py:374
  25.0 5.5 %collective-permute-start.5 = (bf16[256,256]{1,0:T(8,128)(2,1)S(1)}, bf16[256,256]{1,0:T(8,128)(2,1)S(1)}, u32[]{:S(2)}, u32[]{:S(2)}) collective-permute-start(bf16[256,256]{1,0:T(8,128)(2,1)S(1)} %get-tuple-element.75), channel_id=1, source_target_pairs={{0,1},{1,0},{2,3},{3,2},{4,5},{5,4},{6,7},{7,6},{8,9},{9,8},{10,11... | collective-permute-start | bytes 393224 | tf_op jit(solution)/shard_map/ppermute | solution.py:375
  27.0 8.9 %collective-permute-start.6 = (bf16[256,256]{1,0:T(8,128)(2,1)S(1)}, bf16[256,256]{1,0:T(8,128)(2,1)S(1)}, u32[]{:S(2)}, u32[]{:S(2)}) collective-permute-start(bf16[256,256]{1,0:T(8,128)(2,1)S(1)} %get-tuple-element.79), channel_id=1, source_target_pairs={{0,15},{1,2},{2,1},{3,4},{4,3},{5,6},{6,5},{7,8},{8,7},{9,10},{10,... | collective-permute-start | bytes 393224 | tf_op jit(solution)/shard_map/ppermute | solution.py:374
  29.2 6.7 %collective-permute-start.7 = (bf16[256,256]{1,0:T(8,128)(2,1)S(1)}, bf16[256,256]{1,0:T(8,128)(2,1)S(1)}, u32[]{:S(2)}, u32[]{:S(2)}) collective-permute-start(bf16[256,256]{1,0:T(8,128)(2,1)S(1)} %get-tuple-element.80), channel_id=1, source_target_pairs={{0,1},{1,0},{2,3},{3,2},{4,5},{5,4},{6,7},{7,6},{8,9},{9,8},{10,11... | collective-permute-start | bytes 393224 | tf_op jit(solution)/shard_map/ppermute | solution.py:375
  48.0 7.2 %collective-permute-start.9 = (bf16[2,272,256]{2,1,0:T(8,128)(2,1)S(1)}, bf16[2,272,256]{2,1,0:T(8,128)(2,1)S(1)}, u32[]{:S(2)}, u32[]{:S(2)}) collective-permute-start(bf16[2,272,256]{2,1,0:T(8,128)(2,1)S(1)} %get-tuple-element.86.factor), channel_id=1, source_target_pairs={{0,16},{16,32},{32,48},{48,64},{64,80},{80,96},{96,112},{112,128},... | collective-permute-start | bytes 835592 | tf_op jit(solution)/shard_map/ppermute | solution.py:470
  48.0 11.3 %collective-permute-start.10 = (bf16[256,256]{1,0:T(8,128)(2,1)S(1)}, bf16[256,256]{1,0:T(8,128)(2,1)S(1)}, u32[]{:S(2)}, u32[]{:S(2)}) collective-permute-start(bf16[256,256]{1,0:T(8,128)(2,1)S(1)} %get-tuple-element.89), channel_id=1, source_target_pairs={{0,15},{1,2},{2,1},{3,4},{4,3},{5,6},{6,5},{7,8},{8,7},{9,10},{10,... | collective-permute-start | bytes 393224 | tf_op jit(solution)/shard_map/ppermute | solution.py:374
  49.9 9.4 %collective-permute-start.11 = (bf16[256,256]{1,0:T(8,128)(2,1)S(1)}, bf16[256,256]{1,0:T(8,128)(2,1)S(1)}, u32[]{:S(2)}, u32[]{:S(2)}) collective-permute-start(bf16[256,256]{1,0:T(8,128)(2,1)S(1)} %get-tuple-element.90), channel_id=1, source_target_pairs={{0,1},{1,0},{2,3},{3,2},{4,5},{5,4},{6,7},{7,6},{8,9},{9,8},{10,11... | collective-permute-start | bytes 393224 | tf_op jit(solution)/shard_map/ppermute | solution.py:375
  57.4 8.4 %collective-permute-start.12 = (bf16[256,256]{1,0:T(8,128)(2,1)S(1)}, bf16[256,256]{1,0:T(8,128)(2,1)S(1)}, u32[]{:S(2)}, u32[]{:S(2)}) collective-permute-start(bf16[256,256]{1,0:T(8,128)(2,1)S(1)} %get-tuple-element.94), channel_id=1, source_target_pairs={{0,15},{1,2},{2,1},{3,4},{4,3},{5,6},{6,5},{7,8},{8,7},{9,10},{10,... | collective-permute-start | bytes 393224 | tf_op jit(solution)/shard_map/ppermute | solution.py:374
  59.3 6.5 %collective-permute-start.13 = (bf16[256,256]{1,0:T(8,128)(2,1)S(1)}, bf16[256,256]{1,0:T(8,128)(2,1)S(1)}, u32[]{:S(2)}, u32[]{:S(2)}) collective-permute-start(bf16[256,256]{1,0:T(8,128)(2,1)S(1)} %get-tuple-element.95), channel_id=1, source_target_pairs={{0,1},{1,0},{2,3},{3,2},{4,5},{5,4},{6,7},{7,6},{8,9},{9,8},{10,11... | collective-permute-start | bytes 393224 | tf_op jit(solution)/shard_map/ppermute | solution.py:375
  61.2 8.6 %collective-permute-start.14 = (bf16[256,256]{1,0:T(8,128)(2,1)S(1)}, bf16[256,256]{1,0:T(8,128)(2,1)S(1)}, u32[]{:S(2)}, u32[]{:S(2)}) collective-permute-start(bf16[256,256]{1,0:T(8,128)(2,1)S(1)} %get-tuple-element.99), channel_id=1, source_target_pairs={{0,15},{1,2},{2,1},{3,4},{4,3},{5,6},{6,5},{7,8},{8,7},{9,10},{10,... | collective-permute-start | bytes 393224 | tf_op jit(solution)/shard_map/ppermute | solution.py:374
  64.9 5.0 %collective-permute-start.15 = (bf16[256,256]{1,0:T(8,128)(2,1)S(1)}, bf16[256,256]{1,0:T(8,128)(2,1)S(1)}, u32[]{:S(2)}, u32[]{:S(2)}) collective-permute-start(bf16[256,256]{1,0:T(8,128)(2,1)S(1)} %get-tuple-element.100), channel_id=1, source_target_pairs={{0,1},{1,0},{2,3},{3,2},{4,5},{5,4},{6,7},{7,6},{8,9},{9,8},{10,11... | collective-permute-start | bytes 393224 | tf_op jit(solution)/shard_map/ppermute | solution.py:375
  67.7 8.4 %collective-permute-start.16 = (bf16[256,256]{1,0:T(8,128)(2,1)S(1)}, bf16[256,256]{1,0:T(8,128)(2,1)S(1)}, u32[]{:S(2)}, u32[]{:S(2)}) collective-permute-start(bf16[256,256]{1,0:T(8,128)(2,1)S(1)} %get-tuple-element.104), channel_id=1, source_target_pairs={{0,15},{1,2},{2,1},{3,4},{4,3},{5,6},{6,5},{7,8},{8,7},{9,10},{10,... | collective-permute-start | bytes 393224 | tf_op jit(solution)/shard_map/ppermute | solution.py:374
  69.8 6.3 %collective-permute-start.17 = (bf16[256,256]{1,0:T(8,128)(2,1)S(1)}, bf16[256,256]{1,0:T(8,128)(2,1)S(1)}, u32[]{:S(2)}, u32[]{:S(2)}) collective-permute-start(bf16[256,256]{1,0:T(8,128)(2,1)S(1)} %get-tuple-element.105), channel_id=1, source_target_pairs={{0,1},{1,0},{2,3},{3,2},{4,5},{5,4},{6,7},{7,6},{8,9},{9,8},{10,11... | collective-permute-start | bytes 393224 | tf_op jit(solution)/shard_map/ppermute | solution.py:375
